TPU v7x, 32 devices: a whole 2x2x4 slice. The times are simulated.
32 devices in a mesh: gx: 4 (over y, x), gy: 8 (over z, core).
Axes of the slice: x: 2, y: 2, z: 4, core: 2. Of those that a mesh axis runs over, the one named last changes fastest.
Arguments:
- material: int32 [8, 128, 512], P('gx', 'gy'), may hold values from 0 to 3
- phase: int32 [8, 128, 512], P('gx', 'gy'), may hold values from 0 to 7
- clock: float32 [1], replicated, may hold values from -3.140625 to 3.140625
- displacement: float32 [3, 8, 128, 512], P(None, 'gx', 'gy'), may hold values from -6 to 6
- velocity: float32 [3, 8, 128, 512], P(None, 'gx', 'gy'), may hold values from -6 to 6
- cotangent: float32 [3, 8, 128, 512], P(None, 'gx', 'gy'), may hold values from -4 to 4
- material_table: float32 [2, 4], replicated, may hold values from 0.5 to 4
- w_in: bfloat16 [256, 10], replicated, may hold values from -2 to 2
- b_in: float32 [256], replicated, may hold values from -3 to 3
- w_mid: bfloat16 [2, 256, 256], replicated, may hold values from -0.375 to 0.375
- b_mid: float32 [2, 256], replicated, may hold values from -3 to 3
- w_out: bfloat16 [9, 256], replicated, may hold values from -0.375 to 0.375
- b_out: float32 [9], replicated, may hold values from -3 to 3
Outputs:
- velocity_new: float32 [3, 8, 128, 512], P(None, 'gx', 'gy')
- displacement_grad: float32 [3, 8, 128, 512], P(None, 'gx', 'gy')
- grad_w_in: float32 [256, 10], replicated
- grad_b_in: float32 [256], replicated
- grad_w_mid: float32 [2, 256, 256], replicated
- grad_b_mid: float32 [2, 256], replicated
- grad_w_out: float32 [9, 256], replicated
- grad_b_out: float32 [9], replicated
All inputs are finite; a program needn't handle non-finite values.
Results may differ from a plain program's by a relative error of at most 0.02.
Values sent between devices are 32-bit elements; how exact they have to be, the bound alone decides.
No kernel may reach another device: no remote copies, remote signals or barrier semaphores. Data moves between devices by JAX's collectives and lax.ppermute only.
A program may use at most 64 MiB of HBM per device.

v0:
```python
import jax
import jax.numpy as jnp
from jax import lax
from jax.sharding import PartitionSpec as P

FEAT = 10
OUT = 9
PHASES = 8
NPARAM = 136713


time_step = 0.25
viscosity = 0.2
norm_eps = 1e-06
two_pi = 6.283185307179586


def with_halo(block, sides, width):
    for axis, dim in sides:
        count = lax.axis_size(axis)
        forward = [(i, i + 1) for i in range(count - 1)]
        backward = [(target, source) for source, target in forward]
        low = lax.ppermute(
            lax.slice_in_dim(block, block.shape[dim] - width, None, axis=dim), axis, forward
        )
        high = lax.ppermute(lax.slice_in_dim(block, 0, width, axis=dim), axis, backward)
        block = jnp.concatenate([low, block, high], axis=dim)
    return block


def zdiff(field):
    padded = jnp.pad(field, ((0, 0), (0, 0), (0, 0), (1, 1)))
    return (padded[..., 2:] - padded[..., :-2]) * 0.5


def xdiff_both(padded):
    return (padded[:, 2:, 1:-1] - padded[:, :-2, 1:-1]) * 0.5


def ydiff_both(padded):
    return (padded[:, 1:-1, 2:] - padded[:, 1:-1, :-2]) * 0.5


def forward_block(feats, w_in, b_in, w_mid, b_mid, w_out, b_out):
    first = jnp.tanh(
        jnp.dot(w_in, feats, preferred_element_type=jnp.float32) + b_in[:, None]
    ).astype(jnp.bfloat16)
    second = jnp.tanh(
        jnp.dot(w_mid[0], first, preferred_element_type=jnp.float32) + b_mid[0][:, None]
    ).astype(jnp.bfloat16)
    third = jnp.tanh(
        jnp.dot(w_mid[1], second, preferred_element_type=jnp.float32) + b_mid[1][:, None]
    ).astype(jnp.bfloat16)
    result = jnp.dot(w_out, third, preferred_element_type=jnp.float32) + b_out[:, None]
    return (first, second, third, result)


def backward_block(feats, delta, w_in, b_in, w_mid, b_mid, w_out, b_out):
    first, second, third, result = forward_block(feats, w_in, b_in, w_mid, b_mid, w_out, b_out)
    delta_out = delta.astype(jnp.bfloat16)
    grad_wout = jnp.dot(delta_out, third.T, preferred_element_type=jnp.float32)
    grad_bout = jnp.sum(delta_out.astype(jnp.float32), axis=1)
    back_third = jnp.dot(w_out.T, delta_out, preferred_element_type=jnp.float32)
    delta_third = (back_third * (1.0 - jnp.square(third.astype(jnp.float32)))).astype(jnp.bfloat16)
    grad_wthree = jnp.dot(delta_third, second.T, preferred_element_type=jnp.float32)
    grad_bthree = jnp.sum(delta_third.astype(jnp.float32), axis=1)
    back_second = jnp.dot(w_mid[1].T, delta_third, preferred_element_type=jnp.float32)
    delta_second = (back_second * (1.0 - jnp.square(second.astype(jnp.float32)))).astype(
        jnp.bfloat16
    )
    grad_wtwo = jnp.dot(delta_second, first.T, preferred_element_type=jnp.float32)
    grad_btwo = jnp.sum(delta_second.astype(jnp.float32), axis=1)
    back_first = jnp.dot(w_mid[0].T, delta_second, preferred_element_type=jnp.float32)
    delta_first = (back_first * (1.0 - jnp.square(first.astype(jnp.float32)))).astype(jnp.bfloat16)
    grad_win = jnp.dot(delta_first, feats.T, preferred_element_type=jnp.float32)
    grad_bin = jnp.sum(delta_first.astype(jnp.float32), axis=1)
    back_feats = jnp.dot(w_in.T, delta_first, preferred_element_type=jnp.float32)
    grads = (
        grad_win,
        grad_bin,
        jnp.stack([grad_wtwo, grad_wthree]),
        jnp.stack([grad_btwo, grad_bthree]),
        grad_wout,
        grad_bout,
    )
    return (grads, back_feats, result)


def body(
    material,
    phase,
    clock,
    displacement,
    velocity,
    cotangent,
    material_table,
    w_in,
    b_in,
    w_mid,
    b_mid,
    w_out,
    b_out,
):
    size_x, size_y, size_z = material.shape
    kinds = jnp.arange(material_table.shape[1], dtype=jnp.int32)
    onehot = (material[None] == kinds[:, None, None, None]).astype(jnp.float32)
    stiffness = jnp.tensordot(material_table[0], onehot, axes=1)
    density = jnp.tensordot(material_table[1], onehot, axes=1)
    occupied = (material > 0).astype(jnp.float32)
    actuation = jnp.sin(two_pi * phase.astype(jnp.float32) / PHASES + clock[0])
    carried = time_step * occupied * cotangent / density
    rims = with_halo(jnp.concatenate([displacement, velocity], 0), (("gx", 1), ("gy", 2)), 1)
    disp_rim = rims[0:3]
    velo_rim = rims[3:6]
    strain = jnp.stack(
        [xdiff_both(disp_rim), ydiff_both(disp_rim), zdiff(displacement)], axis=1
    ).reshape(9, size_x, size_y, size_z)
    feats = jnp.concatenate([strain, actuation[None]], 0).reshape(FEAT, -1).astype(jnp.bfloat16)
    voxels = size_x * size_y * size_z
    block_rows = min(2048, voxels)
    count = voxels // block_rows
    feat_blocks = feats.reshape(FEAT, count, block_rows).transpose(1, 0, 2)
    weights = (w_in, b_in, w_mid, b_mid, w_out, b_out)
    carried_rim = with_halo(carried, (("gx", 1), ("gy", 2)), 1)
    stress_grad = -jnp.stack(
        [xdiff_both(carried_rim), ydiff_both(carried_rim), zdiff(carried)], axis=1
    ).reshape(9, size_x, size_y, size_z)
    delta_all = (
        (occupied * stiffness * stress_grad).reshape(OUT, count, block_rows).transpose(1, 0, 2)
    )
    zeros = (
        jnp.zeros(w_in.shape, jnp.float32),
        jnp.zeros(b_in.shape, jnp.float32),
        jnp.zeros(w_mid.shape, jnp.float32),
        jnp.zeros(b_mid.shape, jnp.float32),
        jnp.zeros(w_out.shape, jnp.float32),
        jnp.zeros(b_out.shape, jnp.float32),
    )

    def backward_step(carry, pieces):
        grads, back_feats, result = backward_block(pieces[0], pieces[1], *weights)
        return (
            jax.tree.map(lambda left, right: left + right, carry, grads),
            (back_feats[:9], result),
        )

    partials, (back_blocks, outputs) = lax.scan(backward_step, zeros, (feat_blocks, delta_all))
    network = outputs.transpose(1, 0, 2).reshape(OUT, size_x, size_y, size_z)
    stress = (occupied * stiffness * network).reshape(3, 3, size_x, size_y, size_z)
    stress_x = with_halo(stress[:, 0], (("gx", 1),), 1)
    stress_y = with_halo(stress[:, 1], (("gy", 2),), 1)
    force = (
        (stress_x[:, 2:] - stress_x[:, :-2]) * 0.5
        + (stress_y[:, :, 2:] - stress_y[:, :, :-2]) * 0.5
        + zdiff(stress[:, 2])
    )
    inner = velo_rim[:, 1:-1, 1:-1]
    lap_z = jnp.pad(velocity, ((0, 0), (0, 0), (0, 0), (1, 1)))
    laplacian = -6.0 * velocity
    laplacian = laplacian + velo_rim[:, 2:, 1:-1] + velo_rim[:, :-2, 1:-1]
    laplacian = laplacian + velo_rim[:, 1:-1, 2:] + velo_rim[:, 1:-1, :-2]
    laplacian = laplacian + lap_z[..., 2:] + lap_z[..., :-2]
    velocity_new = inner + time_step * occupied * (force + viscosity * laplacian) / density
    strain_grad = back_blocks.transpose(1, 0, 2).reshape(3, 3, size_x, size_y, size_z)
    back_x = with_halo(strain_grad[:, 0], (("gx", 1),), 1)
    back_y = with_halo(strain_grad[:, 1], (("gy", 2),), 1)
    displacement_grad = -(
        (back_x[:, 2:] - back_x[:, :-2]) * 0.5
        + (back_y[:, :, 2:] - back_y[:, :, :-2]) * 0.5
        + zdiff(strain_grad[:, 2])
    )
    summed = lax.psum(
        (partials[0], partials[1], partials[2], partials[3], partials[4], partials[5]), ("gx", "gy")
    )
    total = sum((jnp.sum(jnp.square(item)) for item in summed))
    scale = lax.rsqrt(total / NPARAM + norm_eps)
    results = tuple((item * scale for item in summed))
    return (
        velocity_new,
        displacement_grad,
        results[0],
        results[1],
        results[2],
        results[3],
        results[4],
        results[5],
    )


def solution(mesh):
    in_specs = (
        P("gx", "gy", None),
        P("gx", "gy", None),
        P(),
        P(None, "gx", "gy", None),
        P(None, "gx", "gy", None),
        P(None, "gx", "gy", None),
        P(),
        P(),
        P(),
        P(),
        P(),
        P(),
        P(),
    )
    out_specs = (P(None, "gx", "gy", None), P(None, "gx", "gy", None), P(), P(), P(), P(), P(), P())
    return jax.shard_map(body, mesh=mesh, in_specs=in_specs, out_specs=out_specs, check_vma=False)
```

profile of v0, /device:TPU:0, one launch (start us, length us, event | category | flops | bytes accessed | tf_op | source)
XLA Modules:
  0.0 267.0 jit_solution(9475212293226691999)
XLA Ops:
  10.2 4.8 %collective-permute-start.1 = (f32[3,1,16,512]{3,2,1,0:T(8,128)S(1)}, f32[3,1,16,512]{3,2,1,0:T(8,128)S(1)}, u32[]{:S(2)}, u32[]{:S(2)}) collective-permute-start(f32[3,1,16,512]{3,2,1,0:T(8,128)S(1)} %get-tuple-element.257), channel_id=1, source_target_pairs={{0,8},{8,16},{16,24},{1,9},{9,17},{17,25},{2,10},{10,18},{18,26},{... | collective-permute-start | bytes 294920 | tf_op jit(solution)/shard_map/ppermute | solution.py:23
  15.1 1.4 collective-permute-start
  18.2 4.5 %collective-permute-start.5 = (f32[6,1,16,512]{3,2,1,0:T(8,128)}, f32[6,1,16,512]{3,2,1,0:T(8,128)S(1)}, u32[]{:S(2)}, u32[]{:S(2)}) collective-permute-start(f32[6,1,16,512]{3,2,1,0:T(8,128)} %get-tuple-element.240), channel_id=1, source_target_pairs={{0,8},{8,16},{16,24},{1,9},{9,17},{17,25},{2,10},{10,18},{18,26},{... | collective-permute-start | bytes 589832 | tf_op jit(solution)/shard_map/ppermute | solution.py:23
  22.7 1.3 collective-permute-start.4
  24.8 1.3 collective-permute-start.2
  26.1 3.0 %collective-permute-start.3 = (f32[3,4,1,512]{3,2,1,0:T(1,128)S(1)}, f32[3,4,1,512]{3,2,1,0:T(1,128)S(1)}, u32[]{:S(2)}, u32[]{:S(2)}) collective-permute-start(f32[3,4,1,512]{3,2,1,0:T(1,128)S(1)} %get-tuple-element.245), channel_id=1, source_target_pairs={{0,1},{1,2},{2,3},{3,4},{4,5},{5,6},{6,7},{8,9},{9,10},{10,11},{11... | collective-permute-start | bytes 73736 | tf_op jit(solution)/shard_map/ppermute | solution.py:23
  31.3 2.3 collective-permute-done.4
  33.7 1.4 collective-permute-start.6
  35.1 3.0 %collective-permute-start.7 = (f32[6,4,1,512]{3,2,1,0:T(1,128)S(1)}, f32[6,4,1,512]{3,2,1,0:T(1,128)S(1)}, u32[]{:S(2)}, u32[]{:S(2)}) collective-permute-start(f32[6,4,1,512]{3,2,1,0:T(1,128)S(1)} %get-tuple-element.233), channel_id=1, source_target_pairs={{0,1},{1,2},{2,3},{3,4},{4,5},{5,6},{6,7},{8,9},{9,10},{10,11},{11... | collective-permute-start | bytes 147464 | tf_op jit(solution)/shard_map/ppermute | solution.py:23
  40.5 76.0 %while.25 = (s32[]{:T(128)}, f32[256,10]{0,1:T(8,128)S(1)}, f32[256]{0:T(256)}, f32[2,256,256]{2,1,0:T(8,128)S(1)}, f32[2,256]{1,0:T(2,128)}, /*index=5*/f32[9,2...) while((s32[]{:T(128)}, f32[256,10]{0,1:T(8,128)S(1)}, ...), condition=%wide.region_5.6_spmd.clone, body=%wide.region_0.5_spmd.clone.sunk | while | flops 1684996864 | bytes 26539676 | solution.py:147
  118.5 1.3 collective-permute-start.10
  119.9 44.8 %all-reduce.5 = (f32[256,10]{0,1:T(8,128)S(1)}, f32[256]{0:T(256)S(1)}, f32[2,256]{1,0:T(2,128)S(1)}, f32[9,256]{1,0:T(8,128)S(1)}, f32[9]{0:T(128)S(1)}) all-reduce(f32[256,10]{0,1:T(8,128)S(1)} %copy-done.11, f32[256]{0:T(256)S(1)} %copy-done.29, f32[2,256]{1,0:T(2,128)S(1)} %copy-done.25, ...), channel_id=1, replica_groups=mesh['gx'=4,'gy'=8] {'gx','gy'}, use_global_device_ids=true, to_apply=%region_6.7 | all-reduce | flops 5641 | bytes 45128 | tf_op jit(solution)/shard_map/psum | solution.py:172
  167.1 1.6 copy.28
  169.0 1.4 collective-permute-start.14
  170.4 3.0 %collective-permute-start.15 = (f32[3,2,1,512]{3,2,1,0:T(1,128)S(1)}, f32[3,2,1,512]{3,2,1,0:T(1,128)S(1)}, u32[]{:S(2)}, u32[]{:S(2)}) collective-permute-start(f32[3,2,1,512]{3,2,1,0:T(1,128)S(1)} %get-tuple-element.249), channel_id=1, source_target_pairs={{0,1},{1,2},{2,3},{3,4},{4,5},{5,6},{6,7},{8,9},{9,10},{10,11},{11... | collective-permute-start | bytes 36872 | tf_op jit(solution)/shard_map/ppermute | solution.py:23
  173.5 1.3 collective-permute-start.12
  174.8 4.8 %collective-permute-start.13 = (f32[3,1,16,512]{3,2,1,0:T(8,128)S(1)}, f32[3,1,16,512]{3,2,1,0:T(8,128)S(1)}, u32[]{:S(2)}, u32[]{:S(2)}) collective-permute-start(f32[3,1,16,512]{3,2,1,0:T(8,128)S(1)} %get-tuple-element.247), channel_id=1, source_target_pairs={{0,8},{8,16},{16,24},{1,9},{9,17},{17,25},{2,10},{10,18},{18,26},{... | collective-permute-start | bytes 294920 | tf_op jit(solution)/shard_map/ppermute | solution.py:23
  181.4 2.7 %collective-permute-start.11 = (f32[3,2,1,512]{3,2,1,0:T(1,128)S(1)}, f32[3,2,1,512]{3,2,1,0:T(1,128)S(1)}, u32[]{:S(2)}, u32[]{:S(2)}) collective-permute-start(f32[3,2,1,512]{3,2,1,0:T(1,128)S(1)} %get-tuple-element.253), channel_id=1, source_target_pairs={{0,1},{1,2},{2,3},{3,4},{4,5},{5,6},{6,7},{8,9},{9,10},{10,11},{11... | collective-permute-start | bytes 36872 | tf_op jit(solution)/shard_map/ppermute | solution.py:23
  184.2 1.3 collective-permute-start.8
  185.5 5.2 %collective-permute-start.9 = (f32[3,1,16,512]{3,2,1,0:T(8,128)S(1)}, f32[3,1,16,512]{3,2,1,0:T(8,128)S(1)}, u32[]{:S(2)}, u32[]{:S(2)}) collective-permute-start(f32[3,1,16,512]{3,2,1,0:T(8,128)S(1)} %get-tuple-element.251), channel_id=1, source_target_pairs={{0,8},{8,16},{16,24},{1,9},{9,17},{17,25},{2,10},{10,18},{18,26},{... | collective-permute-start | bytes 294920 | tf_op jit(solution)/shard_map/ppermute | solution.py:23
  192.1 1.8 collective-permute-done.9
  194.8 56.2 %all-reduce.8.cloned.1.call-done = f32[2,256,256]{2,1,0:T(8,128)} async-done(((f32[2,256,256]{2,1,0:T(8,128)}), f32[2,256,256]{2,1,0:T(8,128)}) %all-reduce.8.cloned.1.call-update) | async-done | bytes 524304 | tf_op jit(solution)/shard_map/psum | solution.py:172
  251.0 1.8 multiply_reduce_fusion
  258.3 1.9 broadcast_multiply_fusion.1
  (383 shorter events, 94.7 us)
Async XLA Ops:
  7.2 243.8 %all-reduce.8.cloned.1.call-start = ((), (), s32[]{:S(2)}) async-start(), calls=%async_computation | async-start | bytes 1048576 | tf_op jit(solution)/shard_map/psum | solution.py:172
  10.1 19.9 %copy-start.3 = (f32[2,16,512]{2,1,0:T(8,128)}, f32[2,16,512]{2,1,0:T(8,128)S(1)}, u32[]{:S(2)}) copy-start(f32[2,16,512]{2,1,0:T(8,128)S(1)} %get-tuple-element.220) | copy-start | bytes 196612
  10.2 14.4 %collective-permute-start.1 = (f32[3,1,16,512]{3,2,1,0:T(8,128)S(1)}, f32[3,1,16,512]{3,2,1,0:T(8,128)S(1)}, u32[]{:S(2)}, u32[]{:S(2)}) collective-permute-start(f32[3,1,16,512]{3,2,1,0:T(8,128)S(1)} %get-tuple-element.257), channel_id=1, source_target_pairs={{0,8},{8,16},{16,24},{1,9},{9,17},{17,25},{2,10},{10,18},{18,26},{... | collective-permute-start | bytes 294920 | tf_op jit(solution)/shard_map/ppermute | solution.py:23
  15.1 14.0 %copy-start.26 = (s32[2,16,512]{2,1,0:T(8,128)S(1)}, s32[2,16,512]{2,1,0:T(8,128)}, u32[]{:S(2)}) copy-start(s32[2,16,512]{2,1,0:T(8,128)} %param.16) | copy-start | bytes 196612
  15.1 9.6 %collective-permute-start = (f32[3,1,16,512]{3,2,1,0:T(8,128)S(1)}, f32[3,1,16,512]{3,2,1,0:T(8,128)S(1)}, u32[]{:S(2)}, u32[]{:S(2)}) collective-permute-start(f32[3,1,16,512]{3,2,1,0:T(8,128)S(1)} %get-tuple-element.258), channel_id=1, source_target_pairs={{8,0},{16,8},{24,16},{9,1},{17,9},{25,17},{10,2},{18,10},{26,18},{... | collective-permute-start | bytes 294920 | tf_op jit(solution)/shard_map/ppermute | solution.py:26
  18.2 13.1 %collective-permute-start.5 = (f32[6,1,16,512]{3,2,1,0:T(8,128)}, f32[6,1,16,512]{3,2,1,0:T(8,128)S(1)}, u32[]{:S(2)}, u32[]{:S(2)}) collective-permute-start(f32[6,1,16,512]{3,2,1,0:T(8,128)} %get-tuple-element.240), channel_id=1, source_target_pairs={{0,8},{8,16},{16,24},{1,9},{9,17},{17,25},{2,10},{10,18},{18,26},{... | collective-permute-start | bytes 589832 | tf_op jit(solution)/shard_map/ppermute | solution.py:23
  22.7 10.8 %collective-permute-start.4 = (f32[6,1,16,512]{3,2,1,0:T(8,128)}, f32[6,1,16,512]{3,2,1,0:T(8,128)S(1)}, u32[]{:S(2)}, u32[]{:S(2)}) collective-permute-start(f32[6,1,16,512]{3,2,1,0:T(8,128)} %get-tuple-element.241), channel_id=1, source_target_pairs={{8,0},{16,8},{24,16},{9,1},{17,9},{25,17},{10,2},{18,10},{26,18},{... | collective-permute-start | bytes 589832 | tf_op jit(solution)/shard_map/ppermute | solution.py:26
  24.8 6.0 %collective-permute-start.2 = (f32[3,4,1,512]{3,2,1,0:T(1,128)S(1)}, f32[3,4,1,512]{3,2,1,0:T(1,128)S(1)}, u32[]{:S(2)}, u32[]{:S(2)}) collective-permute-start(f32[3,4,1,512]{3,2,1,0:T(1,128)S(1)} %get-tuple-element.244), channel_id=1, source_target_pairs={{1,0},{2,1},{3,2},{4,3},{5,4},{6,5},{7,6},{9,8},{10,9},{11,10},{12... | collective-permute-start | bytes 73736 | tf_op jit(solution)/shard_map/ppermute | solution.py:26
  26.1 4.7 %collective-permute-start.3 = (f32[3,4,1,512]{3,2,1,0:T(1,128)S(1)}, f32[3,4,1,512]{3,2,1,0:T(1,128)S(1)}, u32[]{:S(2)}, u32[]{:S(2)}) collective-permute-start(f32[3,4,1,512]{3,2,1,0:T(1,128)S(1)} %get-tuple-element.245), channel_id=1, source_target_pairs={{0,1},{1,2},{2,3},{3,4},{4,5},{5,6},{6,7},{8,9},{9,10},{10,11},{11... | collective-permute-start | bytes 73736 | tf_op jit(solution)/shard_map/ppermute | solution.py:23
  33.7 5.4 %collective-permute-start.6 = (f32[6,4,1,512]{3,2,1,0:T(1,128)S(1)}, f32[6,4,1,512]{3,2,1,0:T(1,128)S(1)}, u32[]{:S(2)}, u32[]{:S(2)}) collective-permute-start(f32[6,4,1,512]{3,2,1,0:T(1,128)S(1)} %get-tuple-element.232), channel_id=1, source_target_pairs={{1,0},{2,1},{3,2},{4,3},{5,4},{6,5},{7,6},{9,8},{10,9},{11,10},{12... | collective-permute-start | bytes 147464 | tf_op jit(solution)/shard_map/ppermute | solution.py:26
  35.1 3.9 %collective-permute-start.7 = (f32[6,4,1,512]{3,2,1,0:T(1,128)S(1)}, f32[6,4,1,512]{3,2,1,0:T(1,128)S(1)}, u32[]{:S(2)}, u32[]{:S(2)}) collective-permute-start(f32[6,4,1,512]{3,2,1,0:T(1,128)S(1)} %get-tuple-element.233), channel_id=1, source_target_pairs={{0,1},{1,2},{2,3},{3,4},{4,5},{5,6},{6,7},{8,9},{9,10},{10,11},{11... | collective-permute-start | bytes 147464 | tf_op jit(solution)/shard_map/ppermute | solution.py:23
  118.5 73.0 %collective-permute-start.10 = (f32[3,2,1,512]{3,2,1,0:T(1,128)S(1)}, f32[3,2,1,512]{3,2,1,0:T(1,128)S(1)}, u32[]{:S(2)}, u32[]{:S(2)}) collective-permute-start(f32[3,2,1,512]{3,2,1,0:T(1,128)S(1)} %get-tuple-element.252), channel_id=1, source_target_pairs={{1,0},{2,1},{3,2},{4,3},{5,4},{6,5},{7,6},{9,8},{10,9},{11,10},{12... | collective-permute-start | bytes 36872 | tf_op jit(solution)/shard_map/ppermute | solution.py:26
  168.8 25.0 %copy-start.2 = (f32[3,2,16,512]{3,2,1,0:T(8,128)S(1)}, f32[3,2,16,512]{3,2,1,0:T(8,128)}, u32[]{:S(2)}) copy-start(f32[3,2,16,512]{3,2,1,0:T(8,128)} %param.19) | copy-start | bytes 589828
  168.8 25.0 %copy-start.6 = (f32[2,16,512]{2,1,0:T(8,128)S(1)}, f32[2,16,512]{2,1,0:T(8,128)}, u32[]{:S(2)}) copy-start(f32[2,16,512]{2,1,0:T(8,128)} %copy-done.5) | copy-start | bytes 196612
  168.8 25.0 %copy-start.8 = (f32[1,2,16,512]{3,2,1,0:T(8,128)S(1)}, f32[1,2,16,512]{3,2,1,0:T(8,128)}, u32[]{:S(2)}) copy-start(f32[1,2,16,512]{3,2,1,0:T(8,128)} %copy-done.7) | copy-start | bytes 196612
  168.9 25.0 %copy-start.17 = (f32[6,4,1,512]{3,2,1,0:T(1,128)S(1)}, f32[6,4,1,512]{3,2,1,0:T(1,128)}, u32[]{:S(2)}) copy-start(f32[6,4,1,512]{3,2,1,0:T(1,128)} %copy-done.16) | copy-start | bytes 147460
  168.9 25.0 %copy-start.19 = (f32[6,4,1,512]{3,2,1,0:T(1,128)S(1)}, f32[6,4,1,512]{3,2,1,0:T(1,128)}, u32[]{:S(2)}) copy-start(f32[6,4,1,512]{3,2,1,0:T(1,128)} %copy-done.18) | copy-start | bytes 147460
  169.0 12.5 %collective-permute-start.14 = (f32[3,2,1,512]{3,2,1,0:T(1,128)S(1)}, f32[3,2,1,512]{3,2,1,0:T(1,128)S(1)}, u32[]{:S(2)}, u32[]{:S(2)}) collective-permute-start(f32[3,2,1,512]{3,2,1,0:T(1,128)S(1)} %get-tuple-element.248), channel_id=1, source_target_pairs={{1,0},{2,1},{3,2},{4,3},{5,4},{6,5},{7,6},{9,8},{10,9},{11,10},{12... | collective-permute-start | bytes 36872 | tf_op jit(solution)/shard_map/ppermute | solution.py:26
  170.4 13.8 %collective-permute-start.15 = (f32[3,2,1,512]{3,2,1,0:T(1,128)S(1)}, f32[3,2,1,512]{3,2,1,0:T(1,128)S(1)}, u32[]{:S(2)}, u32[]{:S(2)}) collective-permute-start(f32[3,2,1,512]{3,2,1,0:T(1,128)S(1)} %get-tuple-element.249), channel_id=1, source_target_pairs={{0,1},{1,2},{2,3},{3,4},{4,5},{5,6},{6,7},{8,9},{9,10},{10,11},{11... | collective-permute-start | bytes 36872 | tf_op jit(solution)/shard_map/ppermute | solution.py:23
  173.5 12.1 %collective-permute-start.12 = (f32[3,1,16,512]{3,2,1,0:T(8,128)S(1)}, f32[3,1,16,512]{3,2,1,0:T(8,128)S(1)}, u32[]{:S(2)}, u32[]{:S(2)}) collective-permute-start(f32[3,1,16,512]{3,2,1,0:T(8,128)S(1)} %get-tuple-element.246), channel_id=1, source_target_pairs={{8,0},{16,8},{24,16},{9,1},{17,9},{25,17},{10,2},{18,10},{26,18},{... | collective-permute-start | bytes 294920 | tf_op jit(solution)/shard_map/ppermute | solution.py:26
  174.8 15.9 %collective-permute-start.13 = (f32[3,1,16,512]{3,2,1,0:T(8,128)S(1)}, f32[3,1,16,512]{3,2,1,0:T(8,128)S(1)}, u32[]{:S(2)}, u32[]{:S(2)}) collective-permute-start(f32[3,1,16,512]{3,2,1,0:T(8,128)S(1)} %get-tuple-element.247), channel_id=1, source_target_pairs={{0,8},{8,16},{16,24},{1,9},{9,17},{17,25},{2,10},{10,18},{18,26},{... | collective-permute-start | bytes 294920 | tf_op jit(solution)/shard_map/ppermute | solution.py:23
  181.4 10.1 %collective-permute-start.11 = (f32[3,2,1,512]{3,2,1,0:T(1,128)S(1)}, f32[3,2,1,512]{3,2,1,0:T(1,128)S(1)}, u32[]{:S(2)}, u32[]{:S(2)}) collective-permute-start(f32[3,2,1,512]{3,2,1,0:T(1,128)S(1)} %get-tuple-element.253), channel_id=1, source_target_pairs={{0,1},{1,2},{2,3},{3,4},{4,5},{5,6},{6,7},{8,9},{9,10},{10,11},{11... | collective-permute-start | bytes 36872 | tf_op jit(solution)/shard_map/ppermute | solution.py:23
  184.2 7.9 %collective-permute-start.8 = (f32[3,1,16,512]{3,2,1,0:T(8,128)S(1)}, f32[3,1,16,512]{3,2,1,0:T(8,128)S(1)}, u32[]{:S(2)}, u32[]{:S(2)}) collective-permute-start(f32[3,1,16,512]{3,2,1,0:T(8,128)S(1)} %get-tuple-element.250), channel_id=1, source_target_pairs={{8,0},{16,8},{24,16},{9,1},{17,9},{25,17},{10,2},{18,10},{26,18},{... | collective-permute-start | bytes 294920 | tf_op jit(solution)/shard_map/ppermute | solution.py:26
  185.5 8.3 %collective-permute-start.9 = (f32[3,1,16,512]{3,2,1,0:T(8,128)S(1)}, f32[3,1,16,512]{3,2,1,0:T(8,128)S(1)}, u32[]{:S(2)}, u32[]{:S(2)}) collective-permute-start(f32[3,1,16,512]{3,2,1,0:T(8,128)S(1)} %get-tuple-element.251), channel_id=1, source_target_pairs={{0,8},{8,16},{16,24},{1,9},{9,17},{17,25},{2,10},{10,18},{18,26},{... | collective-permute-start | bytes 294920 | tf_op jit(solution)/shard_map/ppermute | solution.py:23
  (68 other events, 106.8 us)
Sparse Core Ops, SparseCore 0:
  118.6 132.3 all-reduce.7
where the time goes:
time: 269 us; the launch traced here: 267 us
  waiting for transfers between devices  60.7 us (23%)
  matrix products  50.9 us (19%)
  blocking collectives  44.8 us (17%)
  starting transfers between devices  41.9 us (16%)
  other arithmetic  26.1 us (10%)
  local copies, waits for them, and re-layouts  22.3 us (8%)
  between operations  19.4 us (7%)
    psum x1, waiting for transfers between devices, body(): lax.psum((partials[0], partials[1], partials[2], partials[3], partials[4]...  56.2 us
    psum x1, blocking collectives, body(): lax.psum((partials[0], partials[1], partials[2], partials[3], partials[4]...  44.8 us
    ppermute x8, starting transfers between devices, with_halo(): lax.ppermute(lax.slice_in_dim(block, block.shape[dim] - width, None, axis...  31.2 us
    ppermute x8, starting transfers between devices, with_halo(): lax.ppermute(lax.slice_in_dim(block, 0, width, axis=dim), axis, backward)  10.7 us
    add x32, other arithmetic, backward_step(): left + right  10.1 us
    dot_general x8, matrix products, forward_block(): jnp.dot(w_in, feats, preferred_element_type=jnp.float32) + b_in[:, None]  9.4 us
    slice x8, local copies, waits for them, and re-layouts, forward_block(): b_mid[1][:, None]  6.08 us
    dynamic_update_slice x8, local copies, waits for them, and re-layouts, body(): lax.scan(backward_step, zeros, (feat_blocks, delta_all))  5.41 us
  transfers between devices with their start and end apart: 17, of which 4 were waited for; matrix products, arithmetic and copies ran while one was open for 4% of the time, Pallas kernels for 0%

commit v1 on v0

v1 whole, which is shorter than its diff:
```python
import functools
import jax
import jax.numpy as jnp
from jax import lax
from jax.experimental import pallas as pl
from jax.experimental.pallas import tpu as pltpu
from jax.sharding import PartitionSpec as P

FEAT = 10
OUT = 9
HID = 256
PHASES = 8
NPARAM = 136713
SMALL = 8
GROUPS = 5

time_step = 0.25
viscosity = 0.2
norm_eps = 1e-06
two_pi = 6.283185307179586

bf16 = jnp.bfloat16
f32 = jnp.float32
VMEM = pl.BlockSpec(memory_space=pltpu.VMEM)
SMEM = pl.BlockSpec(memory_space=pltpu.SMEM)


def pick(table, row, material):
    value = jnp.full(material.shape, table[row, 0], f32)
    for kind in range(1, table.shape[1]):
        value = jnp.where(material == kind, table[row, kind], value)
    return value


def step_factor(table, material):
    occupied = jnp.where(material > 0, 1.0, 0.0).astype(f32)
    return occupied, pick(table, 1, material)


def x_ends(field, low, high, rows):
    return (
        jnp.concatenate([low, field[:-rows]], 0),
        jnp.concatenate([field[rows:], high], 0),
    )


def y_ends(field, low, high, rows):
    planes = field.shape[0] // rows
    where = lax.broadcasted_iota(jnp.int32, field.shape, 0)

    def spread(edge):
        return jnp.concatenate(
            [jnp.broadcast_to(edge[p : p + 1], (rows, field.shape[1])) for p in range(planes)], 0
        )

    before, after = pltpu.roll(field, 1, 0), pltpu.roll(field, field.shape[0] - 1, 0)
    low = 0.0 if low is None else spread(low)
    high = 0.0 if high is None else spread(high)
    return (
        jnp.where(where % rows == 0, low, before),
        jnp.where(where % rows == rows - 1, high, after),
    )


def z_ends(field):
    lanes = field.shape[1]
    where = lax.broadcasted_iota(jnp.int32, field.shape, 1)
    return (
        jnp.where(where == 0, 0.0, pltpu.roll(field, 1, 1)),
        jnp.where(where == lanes - 1, 0.0, pltpu.roll(field, lanes - 1, 1)),
    )


def half_diff(ends):
    return (ends[1] - ends[0]) * 0.5


def faces_kernel(rows, table, material, displacement, velocity, cotangent, xf, xb, yf, yb, vf, vb):
    size = material.shape[0]
    planes = size // rows
    occupied, density = step_factor(table, material[...])
    for i in range(3):
        carried = time_step * occupied * cotangent[i] / density
        for slot, field in ((i, displacement[i]), (3 + i, carried), (6 + i, velocity[i])):
            if slot < 6:
                xf[slot] = field[size - rows :]
                xb[slot] = field[:rows]
            else:
                vf[i] = field[size - rows :]
                vb[i] = field[:rows]
            for p in range(planes):
                yf[slot, p : p + 1] = field[(p + 1) * rows - 1 : (p + 1) * rows]
                yb[slot, p : p + 1] = field[p * rows : p * rows + 1]


def network_kernel(
    rows,
    block,
    table,
    clock,
    b_out,
    material,
    phase,
    displacement,
    cotangent,
    xl,
    xh,
    yl,
    yh,
    w_in,
    b_in,
    w_mid,
    b_mid,
    w_out,
    sxf,
    sxb,
    syf,
    syb,
    force,
    dgrad,
    grads,
    grid_in,
    grid_delta,
    feats,
    delta,
    net,
    back,
    win,
    winT,
    wmidT,
    wout,
    woutT,
    bias,
    acc_mid,
    acc_in,
    acc_out,
    acc_b,
    acc_bo,
    tall,
    wide,
):
    size, lanes = material.shape
    planes = size // rows
    tiles = lanes // 128
    voxels = size * lanes
    mat = material[...]
    occupied, density = step_factor(table, mat)
    strength = occupied * pick(table, 0, mat)

    tall[...] = jnp.zeros_like(tall)
    tall[:, :FEAT] = w_in[...].astype(f32)
    win[...] = tall[:, :16].astype(bf16)
    winT[...] = tall[...].T[:16].astype(bf16)
    wide[...] = jnp.zeros_like(wide)
    wide[:OUT] = w_out[...].astype(f32)
    wout[...] = wide[:16].astype(bf16)
    woutT[...] = wide[...].T[:, :16].astype(bf16)
    for k in range(2):
        wmidT[k] = w_mid[k].astype(f32).T.astype(bf16)
    for k, row in enumerate((b_in[...], b_mid[0:1], b_mid[1:2])):
        bias[k] = jnp.broadcast_to(row, (128, HID)).T
    for ref in (acc_mid, acc_in, acc_out, acc_b, acc_bo):
        ref[...] = jnp.zeros_like(ref)

    def put(ref, slot, field):
        for t in range(tiles):
            ref[t, slot * size : (slot + 1) * size] = field[:, t * 128 : (t + 1) * 128]

    factor = time_step * occupied
    for i in range(3):
        field = displacement[i]
        put(grid_in, 3 * i, half_diff(x_ends(field, xl[i], xh[i], rows)))
        put(grid_in, 3 * i + 1, half_diff(y_ends(field, yl[i], yh[i], rows)))
        put(grid_in, 3 * i + 2, half_diff(z_ends(field)))
        field = factor * cotangent[i] / density
        put(grid_delta, 3 * i, strength * -half_diff(x_ends(field, xl[3 + i], xh[3 + i], rows)))
        put(grid_delta, 3 * i + 1, strength * -half_diff(y_ends(field, yl[3 + i], yh[3 + i], rows)))
        put(grid_delta, 3 * i + 2, strength * -half_diff(z_ends(field)))
    put(grid_in, 9, jnp.sin(two_pi * phase[...].astype(f32) / PHASES + clock[0]))
    put(grid_in, 10, jnp.ones((size, lanes), f32))
    for slot in range(11, 16):
        put(grid_in, slot, jnp.zeros((size, lanes), f32))
    for slot in range(9, 16):
        put(grid_delta, slot, jnp.zeros((size, lanes), f32))
    for r in range(size):
        for t in range(tiles):
            at = slice((r * tiles + t) * 128, (r * tiles + t + 1) * 128)
            feats[:, at] = grid_in[t, pl.ds(r, 16, stride=size), :].astype(bf16)
            delta[:, at] = grid_delta[t, pl.ds(r, 16, stride=size), :].astype(bf16)

    rowid = lax.broadcasted_iota(jnp.int32, (16, 1), 0)
    bias_out = jnp.zeros((16, 1), f32)
    for k in range(OUT):
        bias_out = jnp.where(rowid == k, b_out[k], bias_out)

    def mul(a, b):
        return jnp.dot(a, b, preferred_element_type=f32)

    def mul_t(a, b):
        return lax.dot_general(a, b, (((1,), (1,)), ((), ())), preferred_element_type=f32)

    def lane_sum(value):
        total = value[:, :128].astype(f32)
        for k in range(1, block // 128):
            total = total + value[:, k * 128 : (k + 1) * 128].astype(f32)
        return total

    def slope(value):
        wider = value.astype(f32)
        return 1.0 - wider * wider

    def step(index, carry):
        at = pl.ds(pl.multiple_of(index * block, block), block)
        f, d = feats[:, at], delta[:, at]
        h1 = jnp.tanh(mul(win[...], f) + bias[0][:, :1]).astype(bf16)
        h2 = jnp.tanh(mul(w_mid[0], h1) + bias[1][:, :1]).astype(bf16)
        h3 = jnp.tanh(mul(w_mid[1], h2) + bias[2][:, :1]).astype(bf16)
        net[:, at] = mul(wout[...], h3) + bias_out
        acc_out[...] += mul_t(d, h3)
        acc_bo[...] += lane_sum(d)
        d3 = (mul(woutT[...], d) * slope(h3)).astype(bf16)
        acc_mid[HID:] += mul_t(d3, h2)
        acc_b[1] += lane_sum(d3)
        d2 = (mul(wmidT[1], d3) * slope(h2)).astype(bf16)
        acc_mid[:HID] += mul_t(d2, h1)
        acc_b[0] += lane_sum(d2)
        d1 = (mul(wmidT[0], d2) * slope(h1)).astype(bf16)
        acc_in[...] += mul_t(f, d1)
        back[:, at] = mul(winT[...], d1)
        return carry

    lax.fori_loop(0, voxels // block, step, 0)

    for r in range(size):
        for t in range(tiles):
            at = slice((r * tiles + t) * 128, (r * tiles + t + 1) * 128)
            grid_in[t, pl.ds(r, 16, stride=size), :] = net[:, at]
            grid_delta[t, pl.ds(r, 16, stride=size), :] = back[:, at]

    def get(ref, slot):
        return jnp.concatenate(
            [ref[t, slot * size : (slot + 1) * size] for t in range(tiles)], axis=1
        )

    nothing = jnp.zeros((rows, lanes), f32)
    for base, ref, scale, out in ((0, grid_in, strength, force), (3, grid_delta, None, dgrad)):
        for i in range(3):
            along = [get(ref, 3 * i + j) for j in range(3)]
            if scale is not None:
                along = [scale * item for item in along]
            slot = base + i
            sxf[slot] = along[0][size - rows :]
            sxb[slot] = along[0][:rows]
            for p in range(planes):
                syf[slot, p : p + 1] = along[1][(p + 1) * rows - 1 : (p + 1) * rows]
                syb[slot, p : p + 1] = along[1][p * rows : p * rows + 1]
            out[i] = (
                half_diff(x_ends(along[0], nothing, nothing, rows))
                + half_diff(y_ends(along[1], None, None, rows))
                + half_diff(z_ends(along[2]))
            )

    chunks = grads.shape[0]
    part = 2 * HID // chunks
    for c in range(chunks):
        grads[c, :part] = acc_mid[c * part : (c + 1) * part]
        grads[c, part:] = jnp.zeros((SMALL, HID), f32)
    grads[0, part:] = acc_in[:8]
    grads[1, part:] = jnp.where(rowid[:8] < 3, acc_in[8:], 0.0)
    grads[2, part:] = acc_out[:8]
    grads[3, part:] = acc_out[8:]
    for k in range(2):
        grads[4, part + k : part + k + 1] = jnp.sum(acc_b[k].T, axis=0, keepdims=True)
    wide[...] = jnp.zeros_like(wide)
    wide[:16, :128] = acc_bo[...]
    grads[4, part + 2 : part + 3, :128] = jnp.sum(wide[:, :128].T, axis=0, keepdims=True)


def fields_kernel(
    rows,
    table,
    material,
    velocity,
    force,
    dgrad,
    vl,
    vh,
    yl,
    yh,
    sxl,
    sxh,
    syl,
    syh,
    velocity_new,
    displacement_grad,
):
    size, lanes = material.shape
    planes = size // rows
    occupied, density = step_factor(table, material[...])

    def halo_part(slot):
        middle = [jnp.zeros((rows, lanes), f32)] * (planes - 2)
        first, last = -0.5 * sxl[slot], 0.5 * sxh[slot]
        part = jnp.concatenate([first, *middle, last] if planes > 1 else [first + last], 0)
        where = lax.broadcasted_iota(jnp.int32, (size, lanes), 0)

        def spread(edge):
            return jnp.concatenate(
                [jnp.broadcast_to(edge[p : p + 1], (rows, lanes)) for p in range(planes)], 0
            )

        part = part - jnp.where(where % rows == 0, spread(syl[slot]) * 0.5, 0.0)
        return part + jnp.where(where % rows == rows - 1, spread(syh[slot]) * 0.5, 0.0)

    for i in range(3):
        value = velocity[i]
        around = -6.0 * value
        for low, high in (
            x_ends(value, vl[i], vh[i], rows),
            y_ends(value, yl[6 + i], yh[6 + i], rows),
            z_ends(value),
        ):
            around = around + high + low
        pull = force[i] + halo_part(i) + viscosity * around
        velocity_new[i] = value + time_step * occupied * pull / density
        displacement_grad[i] = -(dgrad[i] + halo_part(3 + i))


def finish_kernel(place, mine, other, g_in, gb_in, g_mid, gb_mid, g_out, gb_out, small, wide):
    count, height, _ = mine.shape
    part = height - SMALL
    total = jnp.sum(jnp.square(mine[...])) + jnp.sum(jnp.square(other[...]))
    scale = lax.rsqrt(jnp.full((1, 1), total, f32) / NPARAM + norm_eps)
    half, index = place[0], place[1]
    for m in range(count):
        for ref, side in ((mine, half), (other, 1 - half)):
            chunk = side * count + (index ^ m)
            g_mid[pl.ds(pl.multiple_of(chunk * part, part), part), :] = ref[m, :part] * scale
            small[pl.ds(pl.multiple_of(chunk * SMALL, SMALL), SMALL), :] = ref[m, part:] * scale
    wide[...] = jnp.zeros_like(wide)
    wide[:16] = small[:16]
    g_in[...] = wide[...].T[:, :FEAT]
    gb_in[...] = small[10:11]
    g_out[...] = small[16 : 16 + OUT]
    gb_mid[...] = small[32:34]
    gb_out[...] = small[34:35, :OUT]


def shapes(*items):
    return [jax.ShapeDtypeStruct(item, f32) for item in items]


def along(axis, step):
    count = lax.axis_size(axis)
    return [(i, i + step) for i in range(count) if 0 <= i + step < count]


def swap(value, axis, mask):
    return lax.ppermute(value, axis, [(i, i ^ mask) for i in range(lax.axis_size(axis))])


def body(
    material,
    phase,
    clock,
    displacement,
    velocity,
    cotangent,
    material_table,
    w_in,
    b_in,
    w_mid,
    b_mid,
    w_out,
    b_out,
):
    planes, rows, lanes = material.shape
    size = planes * rows
    voxels = size * lanes
    nx, ny = lax.axis_size("gx"), lax.axis_size("gy")
    chunks = 2 * nx
    part = 2 * HID // chunks
    assert chunks >= GROUPS and ny % 2 == 0 and part % 8 == 0
    material = material.reshape(size, lanes)
    phase = phase.reshape(size, lanes)
    displacement = displacement.reshape(3, size, lanes)
    velocity = velocity.reshape(3, size, lanes)
    cotangent = cotangent.reshape(3, size, lanes)

    faces = pl.pallas_call(
        functools.partial(faces_kernel, rows),
        out_shape=shapes(
            *[(6, rows, lanes)] * 2, *[(9, planes, lanes)] * 2, *[(3, rows, lanes)] * 2
        ),
        in_specs=[SMEM] + [VMEM] * 4,
        out_specs=[VMEM] * 6,
        name="faces",
    )(material_table, material, displacement, velocity, cotangent)
    xl = lax.ppermute(faces[0], "gx", along("gx", 1))
    xh = lax.ppermute(faces[1], "gx", along("gx", -1))
    yl = lax.ppermute(faces[2], "gy", along("gy", 1))
    yh = lax.ppermute(faces[3], "gy", along("gy", -1))
    vl = lax.ppermute(faces[4], "gx", along("gx", 1))
    vh = lax.ppermute(faces[5], "gx", along("gx", -1))

    block = 4096
    while voxels % block:
        block //= 2
    outs = pl.pallas_call(
        functools.partial(network_kernel, rows, block),
        out_shape=shapes(
            *[(6, rows, lanes)] * 2,
            *[(6, planes, lanes)] * 2,
            *[(3, size, lanes)] * 2,
            (chunks, part + SMALL, HID),
        ),
        in_specs=[SMEM] * 3 + [VMEM] * 13,
        out_specs=[VMEM] * 7,
        scratch_shapes=[
            pltpu.VMEM((lanes // 128, 16 * size, 128), f32),
            pltpu.VMEM((lanes // 128, 16 * size, 128), f32),
            pltpu.VMEM((16, voxels), bf16),
            pltpu.VMEM((16, voxels), bf16),
            pltpu.VMEM((16, voxels), f32),
            pltpu.VMEM((16, voxels), f32),
            pltpu.VMEM((HID, 16), bf16),
            pltpu.VMEM((16, HID), bf16),
            pltpu.VMEM((2, HID, HID), bf16),
            pltpu.VMEM((16, HID), bf16),
            pltpu.VMEM((HID, 16), bf16),
            pltpu.VMEM((3, HID, 128), f32),
            pltpu.VMEM((2 * HID, HID), f32),
            pltpu.VMEM((16, HID), f32),
            pltpu.VMEM((16, HID), f32),
            pltpu.VMEM((2, HID, 128), f32),
            pltpu.VMEM((16, 128), f32),
            pltpu.VMEM((HID, 128), f32),
            pltpu.VMEM((128, HID), f32),
        ],
        compiler_params=pltpu.CompilerParams(vmem_limit_bytes=50 << 20),
        cost_estimate=pl.CostEstimate(
            flops=6 * voxels * (HID * FEAT + 2 * HID * HID + OUT * HID),
            bytes_accessed=64 * voxels,
            transcendentals=3 * HID * voxels,
        ),
        name="network",
    )(
        material_table,
        clock,
        b_out,
        material,
        phase,
        displacement,
        cotangent,
        xl,
        xh,
        yl,
        yh,
        w_in,
        b_in.reshape(1, HID),
        w_mid,
        b_mid,
        w_out,
    )
    sxl = lax.ppermute(outs[0], "gx", along("gx", 1))
    sxh = lax.ppermute(outs[1], "gx", along("gx", -1))
    syl = lax.ppermute(outs[2], "gy", along("gy", 1))
    syh = lax.ppermute(outs[3], "gy", along("gy", -1))

    half = lax.axis_index("gy") % 2
    index = lax.axis_index("gx")
    pile = outs[6].reshape(2, nx, part + SMALL, HID)
    kept = lax.dynamic_index_in_dim(pile, half, 0, keepdims=False)
    sent = lax.dynamic_index_in_dim(pile, 1 - half, 0, keepdims=False)
    kept = kept + swap(sent, "gy", 1)
    share = lax.dynamic_index_in_dim(kept, index, 0, keepdims=False)
    for m in range(1, nx):
        piece = lax.dynamic_index_in_dim(kept, index ^ m, 0, keepdims=False)
        share = share + swap(piece, "gx", m)
    mask = 2
    while mask < ny:
        share = share + swap(share, "gy", mask)
        mask *= 2
    mine = jnp.stack([share] + [swap(share, "gx", m) for m in range(1, nx)])
    other = swap(mine, "gy", 1)

    fields = pl.pallas_call(
        functools.partial(fields_kernel, rows),
        out_shape=shapes(*[(3, size, lanes)] * 2),
        in_specs=[SMEM] + [VMEM] * 12,
        out_specs=[VMEM] * 2,
        name="fields",
    )(
        material_table,
        material,
        velocity,
        outs[4],
        outs[5],
        vl,
        vh,
        yl,
        yh,
        sxl,
        sxh,
        syl,
        syh,
    )
    place = jnp.stack([half, index]).astype(jnp.int32)
    done = pl.pallas_call(
        finish_kernel,
        out_shape=shapes((HID, FEAT), (1, HID), (2 * HID, HID), (2, HID), (OUT, HID), (1, OUT)),
        in_specs=[SMEM] + [VMEM] * 2,
        out_specs=[VMEM] * 6,
        scratch_shapes=[
            pltpu.VMEM((chunks * SMALL, HID), f32),
            pltpu.VMEM((128, HID), f32),
        ],
        name="finish",
    )(place, mine, other)
    shape = (3, planes, rows, lanes)
    return (
        fields[0].reshape(shape),
        fields[1].reshape(shape),
        done[0],
        done[1].reshape(HID),
        done[2].reshape(2, HID, HID),
        done[3],
        done[4],
        done[5].reshape(OUT),
    )


def solution(mesh):
    in_specs = (
        P("gx", "gy", None),
        P("gx", "gy", None),
        P(),
        P(None, "gx", "gy", None),
        P(None, "gx", "gy", None),
        P(None, "gx", "gy", None),
        P(),
        P(),
        P(),
        P(),
        P(),
        P(),
        P(),
    )
    out_specs = (P(None, "gx", "gy", None), P(None, "gx", "gy", None), P(), P(), P(), P(), P(), P())
    return jax.shard_map(body, mesh=mesh, in_specs=in_specs, out_specs=out_specs, check_vma=False)
```

time: 269 us -> 111 us (0.41)
  matrix products: 50.9 us -> 0 us
  blocking collectives: 44.8 us -> 0 us
  Pallas kernels: 0 us -> 40 us
  waiting for transfers between devices: 60.7 us -> 25.7 us
  other arithmetic: 26.1 us -> 0.7 us
  between operations: 19.4 us -> 1.67 us
  local copies, waits for them, and re-layouts: 22.3 us -> 6.12 us
  starting transfers between devices: 41.9 us -> 34.8 us
    psum x1 -> x0, waiting for transfers between devices: 56.2 us -> none  [body(): lax.psum((partials[0], partials[1], partials[2], partials[3], partials[4]...]
    dot_general x98 -> x0, matrix products: 50.9 us -> none  [the longest x8 9.4 us: forward_block(): jnp.dot(w_in, feats, preferred_element_type=jnp.float32) + b_in[:, None]]
    psum x1 -> x0, blocking collectives: 44.8 us -> none  [body(): lax.psum((partials[0], partials[1], partials[2], partials[3], partials[4]...]
    pallas_call x0 -> x4, Pallas kernels: none -> 40 us  [the longest x1 33.4 us: body(): pl.pallas_call(functools.partial(network_kernel, rows, block), out_shape=...]
    ppermute x16 -> x20, waiting for transfers between devices: 4.57 us -> 25.7 us  [the longest x10 13.9 us: swap(): lax.ppermute(value, axis, [(i, i ^ mask) for i in range(lax.axis_size(axi...]
    add x33 -> x4, other arithmetic: 11.1 us -> 0.08 us  [the longest x1 0.04 us: body(): kept = kept + swap(sent, 'gy', 1)]
    ppermute x16 -> x20, starting transfers between devices: 41.9 us -> 34.8 us  [the longest x10 12.7 us: swap(): lax.ppermute(value, axis, [(i, i ^ mask) for i in range(lax.axis_size(axi...]
    slice x14 -> x0, local copies, waits for them, and re-layouts: 6.93 us -> none  [the longest x8 6.08 us: forward_block(): b_mid[1][:, None]]
  transfers between devices with their start and end apart: 17 -> 20, of which waited for: 4 -> 13; matrix products, arithmetic and copies ran while one was open for 4% -> 1% of each run, Pallas kernels for 0% -> 2%
where the time goes in v1:
time: 111 us; the launch traced here: 109 us
  Pallas kernels  40 us (36%)
  starting transfers between devices  34.8 us (31%)
  waiting for transfers between devices  25.7 us (23%)
  local copies, waits for them, and re-layouts  6.12 us (6%)
  between operations  1.67 us (2%)
    pallas_call x1, Pallas kernels, body(): pl.pallas_call(functools.partial(network_kernel, rows, block), out_shape=...  33.4 us
    ppermute x10, waiting for transfers between devices, swap(): lax.ppermute(value, axis, [(i, i ^ mask) for i in range(lax.axis_size(axi...  13.9 us
    ppermute x10, starting transfers between devices, swap(): lax.ppermute(value, axis, [(i, i ^ mask) for i in range(lax.axis_size(axi...  12.7 us
    unnamed x52, local copies, waits for them, and re-layouts  6.06 us
    ppermute x1, starting transfers between devices, body(): xl = lax.ppermute(faces[0], 'gx', along('gx', 1))  4.99 us
    ppermute x1, starting transfers between devices, body(): sxl = lax.ppermute(outs[0], 'gx', along('gx', 1))  4.56 us
    ppermute x1, starting transfers between devices, body(): vl = lax.ppermute(faces[4], 'gx', along('gx', 1))  3.33 us
    ppermute x1, waiting for transfers between devices, body(): sxh = lax.ppermute(outs[1], 'gx', along('gx', -1))  3.17 us
  transfers between devices with their start and end apart: 20, of which 13 were waited for; matrix products, arithmetic and copies ran while one was open for 1% of the time, Pallas kernels for 2%

profile of v1, /device:TPU:0, one launch (start us, length us, event | category | flops | bytes accessed | tf_op | source)
XLA Modules:
  0.0 108.9 jit_solution(6579631851813937257)
XLA Ops:
  0.7 2.1 %faces.1 = (f32[6,16,512]{2,1,0:T(8,128)}, f32[6,16,512]{2,1,0:T(8,128)}, f32[9,2,512]{2,1,0:T(2,128)}, f32[9,2,512]{2,1,0:T(2,128)}, f32[3,16,512]{2,1,0:T(8,128)}, /*index=5*/f32[3,16,512]{2,1,0:T(8,128)}) custom-call(f32[2,4]{1,0:T(2,128)} %table.5, s32[32,512]{1,0:T(8,128)} %bitcast.36, f32[3,32,512]{2,1,0:T(8,128)} %bitcast.39, f32[3,32,512]{2,1,0:T(8,128)} %bitcast.45, ...), custom_call_target="tpu_custom_call" | custom-call | tf_op jit(solution)/shard_map/faces/pallas_call | solution.py:390
  2.8 5.0 %collective-permute-start = (f32[6,16,512]{2,1,0:T(8,128)}, f32[6,16,512]{2,1,0:T(8,128)S(1)}, u32[]{:S(2)}, u32[]{:S(2)}) collective-permute-start(f32[6,16,512]{2,1,0:T(8,128)} %get-tuple-element.29), channel_id=1, source_target_pairs={{0,8},{8,16},{16,24},{1,9},{9,17},{17,25},{2,10},{10,18},{18,26},{... | collective-permute-start | bytes 589832 | tf_op jit(solution)/shard_map/ppermute | solution.py:399
  9.1 1.5 %collective-permute-start.2 = (f32[9,2,512]{2,1,0:T(2,128)}, f32[9,2,512]{2,1,0:T(2,128)S(1)}, u32[]{:S(2)}, u32[]{:S(2)}) collective-permute-start(f32[9,2,512]{2,1,0:T(2,128)} %get-tuple-element.31), channel_id=1, source_target_pairs={{0,1},{1,2},{2,3},{3,4},{4,5},{5,6},{6,7},{8,9},{9,10},{10,11},{11... | collective-permute-start | bytes 110600 | tf_op jit(solution)/shard_map/ppermute | solution.py:401
  12.7 2.8 %collective-permute-done.3.yh = f32[9,2,512]{2,1,0:T(2,128)S(1)} collective-permute-done((f32[9,2,512]{2,1,0:T(2,128)}, f32[9,2,512]{2,1,0:T(2,128)S(1)}, u32[]{:S(2)}, u32[]{:S(2)}) %collective-permute-start.3) | collective-permute-done | bytes 36896 | tf_op jit(solution)/shard_map/ppermute | solution.py:402
  15.5 2.8 %collective-permute-done.1.xh = f32[6,16,512]{2,1,0:T(8,128)S(1)} collective-permute-done((f32[6,16,512]{2,1,0:T(8,128)}, f32[6,16,512]{2,1,0:T(8,128)S(1)}, u32[]{:S(2)}, u32[]{:S(2)}) %collective-permute-start.1) | collective-permute-done | bytes 196640 | tf_op jit(solution)/shard_map/ppermute | solution.py:400
  19.8 33.4 %network.1 = (f32[6,16,512]{2,1,0:T(8,128)S(1)}, f32[6,16,512]{2,1,0:T(8,128)S(1)}, f32[6,2,512]{2,1,0:T(2,128)S(1)}, f32[6,2,512]{2,1,0:T(2,128)S(1)}, f32[3,32...) custom-call(f32[2,4]{1,0:T(2,128)S(1)} %copy-done.7, f32[1]{0:T(128)S(6)} %copy.23.clock, ...), custom_call_target="tpu_custom_call" | custom-call | flops 13363052544 | bytes 1048576 | tf_op jit(solution)/shard_map/network/pallas_call | solution.py:409
  54.1 1.4 %collective-permute-done.10 = f32[4,72,256]{2,1,0:T(8,128)S(1)} collective-permute-done((f32[4,72,256]{2,1,0:T(8,128)S(1)}, f32[4,72,256]{2,1,0:T(8,128)S(1)}, u32[]{:S(2)}, u32[]{:S(2)}) %collective-permute-start.10) | collective-permute-done | bytes 294944 | tf_op jit(solution)/shard_map/ppermute | solution.py:359
  55.6 3.2 %collective-permute-start.13 = (f32[72,256]{1,0:T(8,128)S(1)}, f32[72,256]{1,0:T(8,128)S(1)}, u32[]{:S(2)}, u32[]{:S(2)}) collective-permute-start(f32[72,256]{1,0:T(8,128)S(1)} %get-tuple-element.59), channel_id=1, source_target_pairs={{0,24},{8,16},{16,8},{24,0},{1,25},{9,17},{17,9},{25,1},{2,26},{10... | collective-permute-start | bytes 221192 | tf_op jit(solution)/shard_map/ppermute | solution.py:359
  60.3 1.4 %collective-permute-done.13 = f32[72,256]{1,0:T(8,128)S(1)} collective-permute-done((f32[72,256]{1,0:T(8,128)S(1)}, f32[72,256]{1,0:T(8,128)S(1)}, u32[]{:S(2)}, u32[]{:S(2)}) %collective-permute-start.13) | collective-permute-done | bytes 73760 | tf_op jit(solution)/shard_map/ppermute | solution.py:359
  61.6 1.6 %collective-permute-done.12 = f32[72,256]{1,0:T(8,128)S(1)} collective-permute-done((f32[72,256]{1,0:T(8,128)S(1)}, f32[72,256]{1,0:T(8,128)S(1)}, u32[]{:S(2)}, u32[]{:S(2)}) %collective-permute-start.12) | collective-permute-done | bytes 73760 | tf_op jit(solution)/shard_map/ppermute | solution.py:359
  64.4 1.6 %collective-permute-start.14 = (f32[72,256]{1,0:T(8,128)S(1)}, f32[72,256]{1,0:T(8,128)S(1)}, u32[]{:S(2)}, u32[]{:S(2)}) collective-permute-start(f32[72,256]{1,0:T(8,128)S(1)} %fusion.1), channel_id=1, source_target_pairs={{0,2},{1,3},{2,0},{3,1},{4,6},{5,7},{6,4},{7,5},{8,10},{9,11},{10,... | collective-permute-start | bytes 221192 | tf_op jit(solution)/shard_map/ppermute | solution.py:359
  66.1 2.8 %collective-permute-done.14 = f32[72,256]{1,0:T(8,128)S(1)} collective-permute-done((f32[72,256]{1,0:T(8,128)S(1)}, f32[72,256]{1,0:T(8,128)S(1)}, u32[]{:S(2)}, u32[]{:S(2)}) %collective-permute-start.14) | collective-permute-done | bytes 73760 | tf_op jit(solution)/shard_map/ppermute | solution.py:359
  68.8 2.6 %collective-permute-start.15 = (f32[72,256]{1,0:T(8,128)S(1)}, f32[72,256]{1,0:T(8,128)S(1)}, u32[]{:S(2)}, u32[]{:S(2)}) collective-permute-start(f32[72,256]{1,0:T(8,128)S(1)} %add.54), channel_id=1, source_target_pairs={{0,4},{1,5},{2,6},{3,7},{4,0},{5,1},{6,2},{7,3},{8,12},{9,13},{10,... | collective-permute-start | bytes 221192 | tf_op jit(solution)/shard_map/ppermute | solution.py:359
  71.5 2.7 %collective-permute-done.15 = f32[72,256]{1,0:T(8,128)S(1)} collective-permute-done((f32[72,256]{1,0:T(8,128)S(1)}, f32[72,256]{1,0:T(8,128)S(1)}, u32[]{:S(2)}, u32[]{:S(2)}) %collective-permute-start.15) | collective-permute-done | bytes 73760 | tf_op jit(solution)/shard_map/ppermute | solution.py:359
  74.2 1.8 %collective-permute-start.18 = (f32[72,256]{1,0:T(8,128)S(1)}, f32[72,256]{1,0:T(8,128)S(1)}, u32[]{:S(2)}, u32[]{:S(2)}) collective-permute-start(f32[72,256]{1,0:T(8,128)S(1)} %add.55), channel_id=1, source_target_pairs={{0,24},{8,16},{16,8},{24,0},{1,25},{9,17},{17,9},{25,1},{2,26},{10... | collective-permute-start | bytes 221192 | tf_op jit(solution)/shard_map/ppermute | solution.py:359
  76.3 1.4 %collective-permute-start.16 = (f32[72,256]{1,0:T(8,128)S(1)}, f32[72,256]{1,0:T(8,128)S(1)}, u32[]{:S(2)}, u32[]{:S(2)}) collective-permute-start(f32[72,256]{1,0:T(8,128)S(1)} %add.55), channel_id=1, source_target_pairs={{0,8},{8,0},{16,24},{24,16},{1,9},{9,1},{17,25},{25,17},{2,10},{10... | collective-permute-start | bytes 221192 | tf_op jit(solution)/shard_map/ppermute | solution.py:359
  77.7 1.8 %collective-permute-done.18 = f32[72,256]{1,0:T(8,128)S(1)} collective-permute-done((f32[72,256]{1,0:T(8,128)S(1)}, f32[72,256]{1,0:T(8,128)S(1)}, u32[]{:S(2)}, u32[]{:S(2)}) %collective-permute-start.18) | collective-permute-done | bytes 73760 | tf_op jit(solution)/shard_map/ppermute | solution.py:359
  81.6 3.3 %collective-permute-start.4 = (f32[3,16,512]{2,1,0:T(8,128)S(1)}, f32[3,16,512]{2,1,0:T(8,128)S(1)}, u32[]{:S(2)}, u32[]{:S(2)}) collective-permute-start(f32[3,16,512]{2,1,0:T(8,128)S(1)} %copy-done.24), channel_id=1, source_target_pairs={{0,8},{8,16},{16,24},{1,9},{9,17},{17,25},{2,10},{10,18},{18,26},{... | collective-permute-start | bytes 294920 | tf_op jit(solution)/shard_map/ppermute | solution.py:403
  86.2 4.6 %collective-permute-start.6 = (f32[6,16,512]{2,1,0:T(8,128)S(1)}, f32[6,16,512]{2,1,0:T(8,128)S(1)}, u32[]{:S(2)}, u32[]{:S(2)}) collective-permute-start(f32[6,16,512]{2,1,0:T(8,128)S(1)} %get-tuple-element.37), channel_id=1, source_target_pairs={{0,8},{8,16},{16,24},{1,9},{9,17},{17,25},{2,10},{10,18},{18,26},{... | collective-permute-start | bytes 589832 | tf_op jit(solution)/shard_map/ppermute | solution.py:465
  95.3 3.0 %collective-permute-done.9.syh = f32[6,2,512]{2,1,0:T(2,128)S(1)} collective-permute-done((f32[6,2,512]{2,1,0:T(2,128)S(1)}, f32[6,2,512]{2,1,0:T(2,128)S(1)}, u32[]{:S(2)}, u32[]{:S(2)}) %collective-permute-start.9) | collective-permute-done | bytes 24608 | tf_op jit(solution)/shard_map/ppermute | solution.py:468
  98.3 3.2 %collective-permute-done.7.sxh = f32[6,16,512]{2,1,0:T(8,128)S(1)} collective-permute-done((f32[6,16,512]{2,1,0:T(8,128)S(1)}, f32[6,16,512]{2,1,0:T(8,128)S(1)}, u32[]{:S(2)}, u32[]{:S(2)}) %collective-permute-start.7) | collective-permute-done | bytes 196640 | tf_op jit(solution)/shard_map/ppermute | solution.py:466
  102.1 2.3 %fields.1 = (f32[3,32,512]{2,1,0:T(8,128)}, f32[3,32,512]{2,1,0:T(8,128)}) custom-call(f32[2,4]{1,0:T(2,128)} %table.5, s32[32,512]{1,0:T(8,128)} %bitcast.37, f32[3,32,512]{2,1,0:T(8,128)} %bitcast.46, f32[3,32,512]{2,1,0:T(8,128)} %copy-done.1, f32[3,32,512]{2,1,0:T(8,128)} %copy-done.2, f32[3,16,512]{2,1,0:T(8,128)} %copy-done.18, ...), custom_call_target="tpu_custom_call" | custom-call | tf_op jit(solution)/shard_map/fields/pallas_call | solution.py:487
  105.2 2.2 %finish.1 = (f32[256,10]{1,0:T(8,128)}, f32[1,256]{1,0:T(1,128)}, f32[512,256]{1,0:T(8,128)}, f32[2,256]{1,0:T(2,128)}, f32[9,256]{1,0:T(8,128)}, /*index=5*/f32[1,9]{1,0:T(1,128)}) custom-call(s32[2]{0:T(128)} %pad_add_fusion.place, f32[4,72,256]{2,1,0:T(8,128)} %copy-done.14, f32[4,72,256]{2,1,0:T(8,128)} %copy-done.15), custom_call_target="tpu_custom_call" | custom-call | tf_op jit(solution)/shard_map/finish/pallas_call | solution.py:509
  107.4 1.6 %copy.22 = f32[256,10]{0,1:T(8,128)} copy(f32[256,10]{1,0:T(8,128)} %get-tuple-element.52) | data formatting | bytes 20480
  (80 shorter events, 17.4 us)
Async XLA Ops:
  0.6 17.6 %copy-start.3 = (f32[3,2,16,512]{3,2,1,0:T(8,128)S(1)}, f32[3,2,16,512]{3,2,1,0:T(8,128)}, u32[]{:S(2)}) copy-start(f32[3,2,16,512]{3,2,1,0:T(8,128)} %param.16) | copy-start | bytes 589828
  2.8 12.7 %collective-permute-start = (f32[6,16,512]{2,1,0:T(8,128)}, f32[6,16,512]{2,1,0:T(8,128)S(1)}, u32[]{:S(2)}, u32[]{:S(2)}) collective-permute-start(f32[6,16,512]{2,1,0:T(8,128)} %get-tuple-element.29), channel_id=1, source_target_pairs={{0,8},{8,16},{16,24},{1,9},{9,17},{17,25},{2,10},{10,18},{18,26},{... | collective-permute-start | bytes 589832 | tf_op jit(solution)/shard_map/ppermute | solution.py:399
  7.8 10.5 %collective-permute-start.1 = (f32[6,16,512]{2,1,0:T(8,128)}, f32[6,16,512]{2,1,0:T(8,128)S(1)}, u32[]{:S(2)}, u32[]{:S(2)}) collective-permute-start(f32[6,16,512]{2,1,0:T(8,128)} %get-tuple-element.30), channel_id=1, source_target_pairs={{8,0},{16,8},{24,16},{9,1},{17,9},{25,17},{10,2},{18,10},{26,18},{... | collective-permute-start | bytes 589832 | tf_op jit(solution)/shard_map/ppermute | solution.py:400
  9.1 3.6 %collective-permute-start.2 = (f32[9,2,512]{2,1,0:T(2,128)}, f32[9,2,512]{2,1,0:T(2,128)S(1)}, u32[]{:S(2)}, u32[]{:S(2)}) collective-permute-start(f32[9,2,512]{2,1,0:T(2,128)} %get-tuple-element.31), channel_id=1, source_target_pairs={{0,1},{1,2},{2,3},{3,4},{4,5},{5,6},{6,7},{8,9},{9,10},{10,11},{11... | collective-permute-start | bytes 110600 | tf_op jit(solution)/shard_map/ppermute | solution.py:401
  10.5 5.0 %collective-permute-start.3 = (f32[9,2,512]{2,1,0:T(2,128)}, f32[9,2,512]{2,1,0:T(2,128)S(1)}, u32[]{:S(2)}, u32[]{:S(2)}) collective-permute-start(f32[9,2,512]{2,1,0:T(2,128)} %get-tuple-element.32), channel_id=1, source_target_pairs={{1,0},{2,1},{3,2},{4,3},{5,4},{6,5},{7,6},{9,8},{10,9},{11,10},{12... | collective-permute-start | bytes 110600 | tf_op jit(solution)/shard_map/ppermute | solution.py:402
  12.7 40.5 %copy-start.5 = (f32[9,2,512]{2,1,0:T(2,128)}, f32[9,2,512]{2,1,0:T(2,128)S(1)}, u32[]{:S(2)}) copy-start(f32[9,2,512]{2,1,0:T(2,128)S(1)} %collective-permute-done.2.yl) | copy-start | bytes 110596
  15.5 37.7 %copy-start.6 = (f32[9,2,512]{2,1,0:T(2,128)}, f32[9,2,512]{2,1,0:T(2,128)S(1)}, u32[]{:S(2)}) copy-start(f32[9,2,512]{2,1,0:T(2,128)S(1)} %collective-permute-done.3.yh) | copy-start | bytes 110596
  54.0 1.6 %collective-permute-start.10 = (f32[4,72,256]{2,1,0:T(8,128)S(1)}, f32[4,72,256]{2,1,0:T(8,128)S(1)}, u32[]{:S(2)}, u32[]{:S(2)}) collective-permute-start(f32[4,72,256]{2,1,0:T(8,128)S(1)} %dynamic-slice_bitcast_fusion), channel_id=1, source_target_pairs={{0,1},{1,0},{2,3},{3,2},{4,5},{5,4},{6,7},{7,6},{8,9},{9,8},{10,11... | collective-permute-start | bytes 884744 | tf_op jit(solution)/shard_map/ppermute | solution.py:359
  55.6 6.0 %collective-permute-start.13 = (f32[72,256]{1,0:T(8,128)S(1)}, f32[72,256]{1,0:T(8,128)S(1)}, u32[]{:S(2)}, u32[]{:S(2)}) collective-permute-start(f32[72,256]{1,0:T(8,128)S(1)} %get-tuple-element.59), channel_id=1, source_target_pairs={{0,24},{8,16},{16,8},{24,0},{1,25},{9,17},{17,9},{25,1},{2,26},{10... | collective-permute-start | bytes 221192 | tf_op jit(solution)/shard_map/ppermute | solution.py:359
  58.8 4.4 %collective-permute-start.12 = (f32[72,256]{1,0:T(8,128)S(1)}, f32[72,256]{1,0:T(8,128)S(1)}, u32[]{:S(2)}, u32[]{:S(2)}) collective-permute-start(f32[72,256]{1,0:T(8,128)S(1)} %get-tuple-element.60), channel_id=1, source_target_pairs={{0,16},{8,24},{16,0},{24,8},{1,17},{9,25},{17,1},{25,9},{2,18},{10... | collective-permute-start | bytes 221192 | tf_op jit(solution)/shard_map/ppermute | solution.py:359
  59.4 5.0 %collective-permute-start.11 = (f32[72,256]{1,0:T(8,128)S(1)}, f32[72,256]{1,0:T(8,128)S(1)}, u32[]{:S(2)}, u32[]{:S(2)}) collective-permute-start(f32[72,256]{1,0:T(8,128)S(1)} %get-tuple-element.58), channel_id=1, source_target_pairs={{0,8},{8,0},{16,24},{24,16},{1,9},{9,1},{17,25},{25,17},{2,10},{10... | collective-permute-start | bytes 221192 | tf_op jit(solution)/shard_map/ppermute | solution.py:359
  64.4 4.4 %collective-permute-start.14 = (f32[72,256]{1,0:T(8,128)S(1)}, f32[72,256]{1,0:T(8,128)S(1)}, u32[]{:S(2)}, u32[]{:S(2)}) collective-permute-start(f32[72,256]{1,0:T(8,128)S(1)} %fusion.1), channel_id=1, source_target_pairs={{0,2},{1,3},{2,0},{3,1},{4,6},{5,7},{6,4},{7,5},{8,10},{9,11},{10,... | collective-permute-start | bytes 221192 | tf_op jit(solution)/shard_map/ppermute | solution.py:359
  68.8 5.3 %collective-permute-start.15 = (f32[72,256]{1,0:T(8,128)S(1)}, f32[72,256]{1,0:T(8,128)S(1)}, u32[]{:S(2)}, u32[]{:S(2)}) collective-permute-start(f32[72,256]{1,0:T(8,128)S(1)} %add.54), channel_id=1, source_target_pairs={{0,4},{1,5},{2,6},{3,7},{4,0},{5,1},{6,2},{7,3},{8,12},{9,13},{10,... | collective-permute-start | bytes 221192 | tf_op jit(solution)/shard_map/ppermute | solution.py:359
  74.2 5.3 %collective-permute-start.18 = (f32[72,256]{1,0:T(8,128)S(1)}, f32[72,256]{1,0:T(8,128)S(1)}, u32[]{:S(2)}, u32[]{:S(2)}) collective-permute-start(f32[72,256]{1,0:T(8,128)S(1)} %add.55), channel_id=1, source_target_pairs={{0,24},{8,16},{16,8},{24,0},{1,25},{9,17},{17,9},{25,1},{2,26},{10... | collective-permute-start | bytes 221192 | tf_op jit(solution)/shard_map/ppermute | solution.py:359
  75.9 4.4 %collective-permute-start.17 = (f32[72,256]{1,0:T(8,128)S(1)}, f32[72,256]{1,0:T(8,128)S(1)}, u32[]{:S(2)}, u32[]{:S(2)}) collective-permute-start(f32[72,256]{1,0:T(8,128)S(1)} %add.55), channel_id=1, source_target_pairs={{0,16},{8,24},{16,0},{24,8},{1,17},{9,25},{17,1},{25,9},{2,18},{10... | collective-permute-start | bytes 221192 | tf_op jit(solution)/shard_map/ppermute | solution.py:359
  76.3 4.4 %collective-permute-start.16 = (f32[72,256]{1,0:T(8,128)S(1)}, f32[72,256]{1,0:T(8,128)S(1)}, u32[]{:S(2)}, u32[]{:S(2)}) collective-permute-start(f32[72,256]{1,0:T(8,128)S(1)} %add.55), channel_id=1, source_target_pairs={{0,8},{8,0},{16,24},{24,16},{1,9},{9,1},{17,25},{25,17},{2,10},{10... | collective-permute-start | bytes 221192 | tf_op jit(solution)/shard_map/ppermute | solution.py:359
  80.7 23.8 %copy-start.14 = (f32[4,72,256]{2,1,0:T(8,128)}, f32[4,72,256]{2,1,0:T(8,128)S(1)}, u32[]{:S(2)}) copy-start(f32[4,72,256]{2,1,0:T(8,128)S(1)} %pad_maximum_fusion.mine) | copy-start | bytes 884740
  80.7 23.8 %collective-permute-start.19 = (f32[4,72,256]{2,1,0:T(8,128)S(1)}, f32[4,72,256]{2,1,0:T(8,128)S(1)}, u32[]{:S(2)}, u32[]{:S(2)}) collective-permute-start(f32[4,72,256]{2,1,0:T(8,128)S(1)} %pad_maximum_fusion.mine), channel_id=1, source_target_pairs={{0,1},{1,0},{2,3},{3,2},{4,5},{5,4},{6,7},{7,6},{8,9},{9,8},{10,11... | collective-permute-start | bytes 884744 | tf_op jit(solution)/shard_map/ppermute | solution.py:359
  81.6 10.5 %collective-permute-start.4 = (f32[3,16,512]{2,1,0:T(8,128)S(1)}, f32[3,16,512]{2,1,0:T(8,128)S(1)}, u32[]{:S(2)}, u32[]{:S(2)}) collective-permute-start(f32[3,16,512]{2,1,0:T(8,128)S(1)} %copy-done.24), channel_id=1, source_target_pairs={{0,8},{8,16},{16,24},{1,9},{9,17},{17,25},{2,10},{10,18},{18,26},{... | collective-permute-start | bytes 294920 | tf_op jit(solution)/shard_map/ppermute | solution.py:403
  84.9 8.5 %collective-permute-start.5 = (f32[3,16,512]{2,1,0:T(8,128)S(1)}, f32[3,16,512]{2,1,0:T(8,128)S(1)}, u32[]{:S(2)}, u32[]{:S(2)}) collective-permute-start(f32[3,16,512]{2,1,0:T(8,128)S(1)} %copy-done.23), channel_id=1, source_target_pairs={{8,0},{16,8},{24,16},{9,1},{17,9},{25,17},{10,2},{18,10},{26,18},{... | collective-permute-start | bytes 294920 | tf_op jit(solution)/shard_map/ppermute | solution.py:404
  86.2 12.1 %collective-permute-start.6 = (f32[6,16,512]{2,1,0:T(8,128)S(1)}, f32[6,16,512]{2,1,0:T(8,128)S(1)}, u32[]{:S(2)}, u32[]{:S(2)}) collective-permute-start(f32[6,16,512]{2,1,0:T(8,128)S(1)} %get-tuple-element.37), channel_id=1, source_target_pairs={{0,8},{8,16},{16,24},{1,9},{9,17},{17,25},{2,10},{10,18},{18,26},{... | collective-permute-start | bytes 589832 | tf_op jit(solution)/shard_map/ppermute | solution.py:465
  90.8 10.7 %collective-permute-start.7 = (f32[6,16,512]{2,1,0:T(8,128)S(1)}, f32[6,16,512]{2,1,0:T(8,128)S(1)}, u32[]{:S(2)}, u32[]{:S(2)}) collective-permute-start(f32[6,16,512]{2,1,0:T(8,128)S(1)} %get-tuple-element.38), channel_id=1, source_target_pairs={{8,0},{16,8},{24,16},{9,1},{17,9},{25,17},{10,2},{18,10},{26,18},{... | collective-permute-start | bytes 589832 | tf_op jit(solution)/shard_map/ppermute | solution.py:466
  92.1 3.2 %collective-permute-start.8 = (f32[6,2,512]{2,1,0:T(2,128)S(1)}, f32[6,2,512]{2,1,0:T(2,128)S(1)}, u32[]{:S(2)}, u32[]{:S(2)}) collective-permute-start(f32[6,2,512]{2,1,0:T(2,128)S(1)} %get-tuple-element.39), channel_id=1, source_target_pairs={{0,1},{1,2},{2,3},{3,4},{4,5},{5,6},{6,7},{8,9},{9,10},{10,11},{11... | collective-permute-start | bytes 73736 | tf_op jit(solution)/shard_map/ppermute | solution.py:467
  93.4 4.9 %collective-permute-start.9 = (f32[6,2,512]{2,1,0:T(2,128)S(1)}, f32[6,2,512]{2,1,0:T(2,128)S(1)}, u32[]{:S(2)}, u32[]{:S(2)}) collective-permute-start(f32[6,2,512]{2,1,0:T(2,128)S(1)} %get-tuple-element.40), channel_id=1, source_target_pairs={{1,0},{2,1},{3,2},{4,3},{5,4},{6,5},{7,6},{9,8},{10,9},{11,10},{12... | collective-permute-start | bytes 73736 | tf_op jit(solution)/shard_map/ppermute | solution.py:468
  (21 other events, 119.8 us)

commit v2 on v1

--- a/solution.py
+++ b/solution.py
@@ -23,6 +23,17 @@
 f32 = jnp.float32
 VMEM = pl.BlockSpec(memory_space=pltpu.VMEM)
 SMEM = pl.BlockSpec(memory_space=pltpu.SMEM)
+HBM = pl.BlockSpec(memory_space=pltpu.HBM)
+
+
+def fetch(sources, targets, sems):
+    copies = [
+        pltpu.make_async_copy(source, target, sems.at[k])
+        for k, (source, target) in enumerate(zip(sources, targets))
+    ]
+    for copy in copies:
+        copy.start()
+    return copies
 
 
 def pick(table, row, material):
@@ -75,7 +86,11 @@
     return (ends[1] - ends[0]) * 0.5
 
 
-def faces_kernel(rows, table, material, displacement, velocity, cotangent, xf, xb, yf, yb, vf, vb):
+def faces_kernel(rows, *refs):
+    sources, (xf, xb, yf, yb), targets, sems = refs[:5], refs[5:9], refs[9:14], refs[14]
+    for copy in fetch(sources, targets, sems):
+        copy.wait()
+    table, material, displacement, velocity, cotangent = targets
     size = material.shape[0]
     planes = size // rows
     occupied, density = step_factor(table, material[...])
@@ -85,60 +100,26 @@
             if slot < 6:
                 xf[slot] = field[size - rows :]
                 xb[slot] = field[:rows]
-            else:
-                vf[i] = field[size - rows :]
-                vb[i] = field[:rows]
             for p in range(planes):
                 yf[slot, p : p + 1] = field[(p + 1) * rows - 1 : (p + 1) * rows]
                 yb[slot, p : p + 1] = field[p * rows : p * rows + 1]
 
 
-def network_kernel(
-    rows,
-    block,
-    table,
-    clock,
-    b_out,
-    material,
-    phase,
-    displacement,
-    cotangent,
-    xl,
-    xh,
-    yl,
-    yh,
-    w_in,
-    b_in,
-    w_mid,
-    b_mid,
-    w_out,
-    sxf,
-    sxb,
-    syf,
-    syb,
-    force,
-    dgrad,
-    grads,
-    grid_in,
-    grid_delta,
-    feats,
-    delta,
-    net,
-    back,
-    win,
-    winT,
-    wmidT,
-    wout,
-    woutT,
-    bias,
-    acc_mid,
-    acc_in,
-    acc_out,
-    acc_b,
-    acc_bo,
-    tall,
-    wide,
-):
+def network_kernel(rows, block, *refs):
+    sources, refs = refs[:13], refs[13:]
+    (xl, xh, yl, yh), refs = refs[:4], refs[4:]
+    (sxf, sxb, syf, syb, force, dgrad, grads), refs = refs[:7], refs[7:]
+    targets, sems, refs = refs[:13], refs[13], refs[14:]
+    grid_in, grid_delta, feats, delta, net, back, refs = *refs[:6], refs[6:]
+    win, winT, wmidT, wout, woutT, bias, refs = *refs[:6], refs[6:]
+    acc_mid, acc_in, acc_out, acc_b, acc_bo, wide = refs
+    copies = fetch(sources, targets, sems)
+    for ref in (acc_mid, acc_in, acc_out, acc_b, acc_bo):
+        ref[...] = jnp.zeros_like(ref)
+    for copy in copies:
+        copy.wait()
+    table, clock, b_out, material, phase, displacement, cotangent, velocity = targets[:8]
+    w_inT, b_in, w_mid, b_mid, w_out = targets[8:]
     size, lanes = material.shape
     planes = size // rows
     tiles = lanes // 128
@@ -147,10 +128,10 @@
     occupied, density = step_factor(table, mat)
     strength = occupied * pick(table, 0, mat)
 
-    tall[...] = jnp.zeros_like(tall)
-    tall[:, :FEAT] = w_in[...].astype(f32)
-    win[...] = tall[:, :16].astype(bf16)
-    winT[...] = tall[...].T[:16].astype(bf16)
+    wide[...] = jnp.zeros_like(wide)
+    wide[:FEAT] = w_inT[...].astype(f32)
+    winT[...] = wide[:16].astype(bf16)
+    win[...] = wide[...].T[:, :16].astype(bf16)
     wide[...] = jnp.zeros_like(wide)
     wide[:OUT] = w_out[...].astype(f32)
     wout[...] = wide[:16].astype(bf16)
@@ -159,8 +140,6 @@
         wmidT[k] = w_mid[k].astype(f32).T.astype(bf16)
     for k, row in enumerate((b_in[...], b_mid[0:1], b_mid[1:2])):
         bias[k] = jnp.broadcast_to(row, (128, HID)).T
-    for ref in (acc_mid, acc_in, acc_out, acc_b, acc_bo):
-        ref[...] = jnp.zeros_like(ref)
 
     def put(ref, slot, field):
         for t in range(tiles):
@@ -242,6 +221,9 @@
             [ref[t, slot * size : (slot + 1) * size] for t in range(tiles)], axis=1
         )
 
+    for i in range(3):
+        sxf[6 + i] = velocity[i, size - rows :]
+        sxb[6 + i] = velocity[i, :rows]
     nothing = jnp.zeros((rows, lanes), f32)
     for base, ref, scale, out in ((0, grid_in, strength, force), (3, grid_delta, None, dgrad)):
         for i in range(3):
@@ -283,8 +265,6 @@
     velocity,
     force,
     dgrad,
-    vl,
-    vh,
     yl,
     yh,
     sxl,
@@ -316,7 +296,7 @@
         value = velocity[i]
         around = -6.0 * value
         for low, high in (
-            x_ends(value, vl[i], vh[i], rows),
+            x_ends(value, sxl[6 + i], sxh[6 + i], rows),
             y_ends(value, yl[6 + i], yh[6 + i], rows),
             z_ends(value),
         ):
@@ -326,7 +306,7 @@
         displacement_grad[i] = -(dgrad[i] + halo_part(3 + i))
 
 
-def finish_kernel(place, mine, other, g_in, gb_in, g_mid, gb_mid, g_out, gb_out, small, wide):
+def finish_kernel(place, mine, other, g_in, gb_in, g_mid, gb_mid, g_out, gb_out, small):
     count, height, _ = mine.shape
     part = height - SMALL
     total = jnp.sum(jnp.square(mine[...])) + jnp.sum(jnp.square(other[...]))
@@ -337,9 +317,7 @@
             chunk = side * count + (index ^ m)
             g_mid[pl.ds(pl.multiple_of(chunk * part, part), part), :] = ref[m, :part] * scale
             small[pl.ds(pl.multiple_of(chunk * SMALL, SMALL), SMALL), :] = ref[m, part:] * scale
-    wide[...] = jnp.zeros_like(wide)
-    wide[:16] = small[:16]
-    g_in[...] = wide[...].T[:, :FEAT]
+    g_in[...] = small[:FEAT]
     gb_in[...] = small[10:11]
     g_out[...] = small[16 : 16 + OUT]
     gb_mid[...] = small[32:34]
@@ -348,6 +326,12 @@
 
 def shapes(*items):
     return [jax.ShapeDtypeStruct(item, f32) for item in items]
+
+
+def stay(value):
+    if value.size < 2:
+        return value
+    return pltpu.with_memory_space_constraint(value, pltpu.HBM)
 
 
 def along(axis, step):
@@ -390,18 +374,23 @@
     faces = pl.pallas_call(
         functools.partial(faces_kernel, rows),
         out_shape=shapes(
-            *[(6, rows, lanes)] * 2, *[(9, planes, lanes)] * 2, *[(3, rows, lanes)] * 2
+            *[(6, rows, lanes)] * 2, *[(9, planes, lanes)] * 2
         ),
-        in_specs=[SMEM] + [VMEM] * 4,
-        out_specs=[VMEM] * 6,
+        in_specs=[HBM] * 5,
+        out_specs=[VMEM] * 4,
+        scratch_shapes=[
+            pltpu.SMEM(material_table.shape, f32),
+            pltpu.VMEM((size, lanes), jnp.int32),
+            *[pltpu.VMEM((3, size, lanes), f32)] * 3,
+            pltpu.SemaphoreType.DMA((5,)),
+        ],
+        compiler_params=pltpu.CompilerParams(vmem_limit_bytes=6 << 20),
         name="faces",
-    )(material_table, material, displacement, velocity, cotangent)
+    )(*map(stay, (material_table, material, displacement, velocity, cotangent)))
     xl = lax.ppermute(faces[0], "gx", along("gx", 1))
     xh = lax.ppermute(faces[1], "gx", along("gx", -1))
     yl = lax.ppermute(faces[2], "gy", along("gy", 1))
     yh = lax.ppermute(faces[3], "gy", along("gy", -1))
-    vl = lax.ppermute(faces[4], "gx", along("gx", 1))
-    vh = lax.ppermute(faces[5], "gx", along("gx", -1))
 
     block = 4096
     while voxels % block:
@@ -409,14 +398,23 @@
     outs = pl.pallas_call(
         functools.partial(network_kernel, rows, block),
         out_shape=shapes(
-            *[(6, rows, lanes)] * 2,
+            *[(9, rows, lanes)] * 2,
             *[(6, planes, lanes)] * 2,
             *[(3, size, lanes)] * 2,
             (chunks, part + SMALL, HID),
         ),
-        in_specs=[SMEM] * 3 + [VMEM] * 13,
+        in_specs=[HBM] * 13 + [VMEM] * 4,
         out_specs=[VMEM] * 7,
         scratch_shapes=[
+            *[pltpu.SMEM(item.shape, f32) for item in (material_table, clock, b_out)],
+            *[pltpu.VMEM((size, lanes), jnp.int32)] * 2,
+            *[pltpu.VMEM((3, size, lanes), f32)] * 3,
+            pltpu.VMEM((FEAT, HID), bf16),
+            pltpu.VMEM((1, HID), f32),
+            pltpu.VMEM((2, HID, HID), bf16),
+            pltpu.VMEM((2, HID), f32),
+            pltpu.VMEM((OUT, HID), bf16),
+            pltpu.SemaphoreType.DMA((13,)),
             pltpu.VMEM((lanes // 128, 16 * size, 128), f32),
             pltpu.VMEM((lanes // 128, 16 * size, 128), f32),
             pltpu.VMEM((16, voxels), bf16),
@@ -434,10 +432,9 @@
             pltpu.VMEM((16, HID), f32),
             pltpu.VMEM((2, HID, 128), f32),
             pltpu.VMEM((16, 128), f32),
-            pltpu.VMEM((HID, 128), f32),
             pltpu.VMEM((128, HID), f32),
         ],
-        compiler_params=pltpu.CompilerParams(vmem_limit_bytes=50 << 20),
+        compiler_params=pltpu.CompilerParams(vmem_limit_bytes=36 << 20),
         cost_estimate=pl.CostEstimate(
             flops=6 * voxels * (HID * FEAT + 2 * HID * HID + OUT * HID),
             bytes_accessed=64 * voxels,
@@ -445,22 +442,28 @@
         ),
         name="network",
     )(
-        material_table,
-        clock,
-        b_out,
-        material,
-        phase,
-        displacement,
-        cotangent,
+        *map(
+            stay,
+            (
+                material_table,
+                clock,
+                b_out,
+                material,
+                phase,
+                displacement,
+                cotangent,
+                velocity,
+                w_in.T,
+                b_in.reshape(1, HID),
+                w_mid,
+                b_mid,
+                w_out,
+            ),
+        ),
         xl,
         xh,
         yl,
         yh,
-        w_in,
-        b_in.reshape(1, HID),
-        w_mid,
-        b_mid,
-        w_out,
     )
     sxl = lax.ppermute(outs[0], "gx", along("gx", 1))
     sxh = lax.ppermute(outs[1], "gx", along("gx", -1))
@@ -481,14 +484,16 @@
     while mask < ny:
         share = share + swap(share, "gy", mask)
         mask *= 2
+    share, sxl, sxh, syl, syh = lax.optimization_barrier((share, sxl, sxh, syl, syh))
     mine = jnp.stack([share] + [swap(share, "gx", m) for m in range(1, nx)])
     other = swap(mine, "gy", 1)
 
     fields = pl.pallas_call(
         functools.partial(fields_kernel, rows),
         out_shape=shapes(*[(3, size, lanes)] * 2),
-        in_specs=[SMEM] + [VMEM] * 12,
+        in_specs=[SMEM] + [VMEM] * 10,
         out_specs=[VMEM] * 2,
+        compiler_params=pltpu.CompilerParams(vmem_limit_bytes=6 << 20),
         name="fields",
     )(
         material_table,
@@ -496,8 +501,6 @@
         velocity,
         outs[4],
         outs[5],
-        vl,
-        vh,
         yl,
         yh,
         sxl,
@@ -508,20 +511,18 @@
     place = jnp.stack([half, index]).astype(jnp.int32)
     done = pl.pallas_call(
         finish_kernel,
-        out_shape=shapes((HID, FEAT), (1, HID), (2 * HID, HID), (2, HID), (OUT, HID), (1, OUT)),
+        out_shape=shapes((FEAT, HID), (1, HID), (2 * HID, HID), (2, HID), (OUT, HID), (1, OUT)),
         in_specs=[SMEM] + [VMEM] * 2,
         out_specs=[VMEM] * 6,
-        scratch_shapes=[
-            pltpu.VMEM((chunks * SMALL, HID), f32),
-            pltpu.VMEM((128, HID), f32),
-        ],
+        scratch_shapes=[pltpu.VMEM((chunks * SMALL, HID), f32)],
+        compiler_params=pltpu.CompilerParams(vmem_limit_bytes=6 << 20),
         name="finish",
     )(place, mine, other)
     shape = (3, planes, rows, lanes)
     return (
         fields[0].reshape(shape),
         fields[1].reshape(shape),
-        done[0],
+        done[0].T,
         done[1].reshape(HID),
         done[2].reshape(2, HID, HID),
         done[3],

time: 111 us -> 89.1 us (0.80); the launches traced: 109 us -> 88.7 us
  waiting for transfers between devices: 25.7 us -> 18.4 us
  local copies, waits for them, and re-layouts: 6.12 us -> 0.77 us
  starting transfers between devices: 34.8 us -> 29.8 us
  Pallas kernels: 40 us -> 38.1 us
    unnamed x52 -> x6, local copies, waits for them, and re-layouts: 6.06 us -> 0.71 us
    ppermute x10, waiting for transfers between devices: 13.9 us -> 8.96 us  [swap(): lax.ppermute(value, axis, [(i, i ^ mask) for i in range(lax.axis_size(axi...]
    ppermute x2 -> x0, starting transfers between devices: 4.62 us -> none  [the longest x1 3.33 us: body(): vl = lax.ppermute(faces[4], 'gx', along('gx', 1))]
    ppermute x1, waiting for transfers between devices: 3.17 us -> 1.14 us  [body(): sxh = lax.ppermute(outs[1], 'gx', along('gx', -1))]
    ppermute x1, starting transfers between devices: 4.56 us -> 3 us  [body(): sxl = lax.ppermute(outs[0], 'gx', along('gx', 1))]
    ppermute x10, starting transfers between devices: 12.7 us -> 14 us  [swap(): lax.ppermute(value, axis, [(i, i ^ mask) for i in range(lax.axis_size(axi...]
  transfers between devices with their start and end apart: 20 -> 18, of which waited for: 13 -> 10; matrix products, arithmetic and copies ran while one was open for 1% -> 0% of each run, Pallas kernels for 2% -> 2%
where the time goes in v2:
time: 89.1 us; the launch traced here: 88.7 us
  Pallas kernels  38.1 us (43%)
  starting transfers between devices  29.8 us (33%)
  waiting for transfers between devices  18.4 us (21%)
  between operations  1.44 us (2%)
    pallas_call x1, Pallas kernels, body(): pl.pallas_call(functools.partial(network_kernel, rows, block), out_shape=...  33.7 us
    ppermute x10, starting transfers between devices, swap(): lax.ppermute(value, axis, [(i, i ^ mask) for i in range(lax.axis_size(axi...  14 us
    ppermute x10, waiting for transfers between devices, swap(): lax.ppermute(value, axis, [(i, i ^ mask) for i in range(lax.axis_size(axi...  8.96 us
    ppermute x1, starting transfers between devices, body(): xl = lax.ppermute(faces[0], 'gx', along('gx', 1))  4.85 us
    ppermute x1, starting transfers between devices, body(): sxl = lax.ppermute(outs[0], 'gx', along('gx', 1))  3 us
    ppermute x1, waiting for transfers between devices, body(): syh = lax.ppermute(outs[3], 'gy', along('gy', -1))  2.78 us
    ppermute x1, waiting for transfers between devices, body(): yh = lax.ppermute(faces[3], 'gy', along('gy', -1))  2.77 us
    ppermute x1, waiting for transfers between devices, body(): xh = lax.ppermute(faces[1], 'gx', along('gx', -1))  2.77 us
  transfers between devices with their start and end apart: 18, of which 10 were waited for; matrix products, arithmetic and copies ran while one was open for 0% of the time, Pallas kernels for 2%

profile of v2, /device:TPU:0, one launch (start us, length us, event | category | flops | bytes accessed | tf_op | source)
XLA Modules:
  0.0 88.7 jit_solution(16374141596901746325)
XLA Ops:
  0.6 1.3 %faces.1 = (f32[6,16,512]{2,1,0:T(8,128)S(1)}, f32[6,16,512]{2,1,0:T(8,128)S(1)}, f32[9,2,512]{2,1,0:T(2,128)S(1)}, f32[9,2,512]{2,1,0:T(2,128)S(1)}) custom-call(f32[2,4]{1,0:T(2,128)} %table.1, s32[32,512]{1,0:T(8,128)} %bitcast.41, f32[3,32,512]{2,1,0:T(8,128)} %bitcast.45, f32[3,32,512]{2,1,0:T(8,128)} %bitcast.36, f32[3,32,512]{2,1,0:T(8,128)} %bitcast.47), custom_call_target="tpu_custom_call" | custom-call | tf_op jit(solution)/shard_map/faces/pallas_call | solution.py:374
  1.9 4.9 %collective-permute-start = (f32[6,16,512]{2,1,0:T(8,128)S(1)}, f32[6,16,512]{2,1,0:T(8,128)S(1)}, u32[]{:S(2)}, u32[]{:S(2)}) collective-permute-start(f32[6,16,512]{2,1,0:T(8,128)S(1)} %get-tuple-element.32), channel_id=1, source_target_pairs={{0,8},{8,16},{16,24},{1,9},{9,17},{17,25},{2,10},{10,18},{18,26},{... | collective-permute-start | bytes 589832 | tf_op jit(solution)/shard_map/ppermute | solution.py:390
  6.8 1.3 %collective-permute-start.1 = (f32[6,16,512]{2,1,0:T(8,128)S(1)}, f32[6,16,512]{2,1,0:T(8,128)S(1)}, u32[]{:S(2)}, u32[]{:S(2)}) collective-permute-start(f32[6,16,512]{2,1,0:T(8,128)S(1)} %get-tuple-element.33), channel_id=1, source_target_pairs={{8,0},{16,8},{24,16},{9,1},{17,9},{25,17},{10,2},{18,10},{26,18},{... | collective-permute-start | bytes 589832 | tf_op jit(solution)/shard_map/ppermute | solution.py:391
  8.1 1.5 %collective-permute-start.2 = (f32[9,2,512]{2,1,0:T(2,128)S(1)}, f32[9,2,512]{2,1,0:T(2,128)S(1)}, u32[]{:S(2)}, u32[]{:S(2)}) collective-permute-start(f32[9,2,512]{2,1,0:T(2,128)S(1)} %get-tuple-element.34), channel_id=1, source_target_pairs={{0,1},{1,2},{2,3},{3,4},{4,5},{5,6},{6,7},{8,9},{9,10},{10,11},{11... | collective-permute-start | bytes 110600 | tf_op jit(solution)/shard_map/ppermute | solution.py:392
  9.6 1.3 %collective-permute-start.3 = (f32[9,2,512]{2,1,0:T(2,128)S(1)}, f32[9,2,512]{2,1,0:T(2,128)S(1)}, u32[]{:S(2)}, u32[]{:S(2)}) collective-permute-start(f32[9,2,512]{2,1,0:T(2,128)S(1)} %get-tuple-element.35), channel_id=1, source_target_pairs={{1,0},{2,1},{3,2},{4,3},{5,4},{6,5},{7,6},{9,8},{10,9},{11,10},{12... | collective-permute-start | bytes 110600 | tf_op jit(solution)/shard_map/ppermute | solution.py:393
  11.5 2.8 %collective-permute-done.3.refs_16_.yh = f32[9,2,512]{2,1,0:T(2,128)S(1)} collective-permute-done((f32[9,2,512]{2,1,0:T(2,128)S(1)}, f32[9,2,512]{2,1,0:T(2,128)S(1)}, u32[]{:S(2)}, u32[]{:S(2)}) %collective-permute-start.3) | collective-permute-done | bytes 36896 | tf_op jit(solution)/shard_map/ppermute | solution.py:393
  14.3 2.8 %collective-permute-done.1.refs_14_ = f32[6,16,512]{2,1,0:T(8,128)S(1)} collective-permute-done((f32[6,16,512]{2,1,0:T(8,128)S(1)}, f32[6,16,512]{2,1,0:T(8,128)S(1)}, u32[]{:S(2)}, u32[]{:S(2)}) %collective-permute-start.1) | collective-permute-done | bytes 196640 | tf_op jit(solution)/shard_map/ppermute | solution.py:391
  17.1 33.7 %network.1 = (f32[9,16,512]{2,1,0:T(8,128)S(1)}, f32[9,16,512]{2,1,0:T(8,128)S(1)}, f32[6,2,512]{2,1,0:T(2,128)S(1)}, f32[6,2,512]{2,1,0:T(2,128)S(1)}, f32[3,32...) custom-call(f32[2,4]{1,0:T(2,128)} %table.1, f32[1]{0:T(128)S(6)} %copy.21.refs_1_, ...), custom_call_target="tpu_custom_call" | custom-call | flops 13363052544 | bytes 1048576 | tf_op jit(solution)/shard_map/network/pallas_call | solution.py:398
  51.0 1.5 %collective-permute-done.4 = f32[4,72,256]{2,1,0:T(8,128)S(1)} collective-permute-done((f32[4,72,256]{2,1,0:T(8,128)S(1)}, f32[4,72,256]{2,1,0:T(8,128)S(1)}, u32[]{:S(2)}, u32[]{:S(2)}) %collective-permute-start.4) | collective-permute-done | bytes 294944 | tf_op jit(solution)/shard_map/ppermute | solution.py:343
  52.5 2.3 %collective-permute-start.5 = (f32[72,256]{1,0:T(8,128)S(1)}, f32[72,256]{1,0:T(8,128)S(1)}, u32[]{:S(2)}, u32[]{:S(2)}) collective-permute-start(f32[72,256]{1,0:T(8,128)S(1)} %get-tuple-element.56), channel_id=1, source_target_pairs={{0,8},{8,0},{16,24},{24,16},{1,9},{9,1},{17,25},{25,17},{2,10},{10... | collective-permute-start | bytes 221192 | tf_op jit(solution)/shard_map/ppermute | solution.py:343
  54.8 1.5 %collective-permute-start.6 = (f32[72,256]{1,0:T(8,128)S(1)}, f32[72,256]{1,0:T(8,128)S(1)}, u32[]{:S(2)}, u32[]{:S(2)}) collective-permute-start(f32[72,256]{1,0:T(8,128)S(1)} %get-tuple-element.58), channel_id=1, source_target_pairs={{0,16},{8,24},{16,0},{24,8},{1,17},{9,25},{17,1},{25,9},{2,18},{10... | collective-permute-start | bytes 221192 | tf_op jit(solution)/shard_map/ppermute | solution.py:343
  57.2 3.0 %collective-permute-start.10 = (f32[9,16,512]{2,1,0:T(8,128)S(1)}, f32[9,16,512]{2,1,0:T(8,128)S(1)}, u32[]{:S(2)}, u32[]{:S(2)}) collective-permute-start(f32[9,16,512]{2,1,0:T(8,128)S(1)} %get-tuple-element.39), channel_id=1, source_target_pairs={{0,8},{8,16},{16,24},{1,9},{9,17},{17,25},{2,10},{10,18},{18,26},{... | collective-permute-start | bytes 884744 | tf_op jit(solution)/shard_map/ppermute | solution.py:468
  60.2 1.3 %collective-permute-start.11 = (f32[9,16,512]{2,1,0:T(8,128)S(1)}, f32[9,16,512]{2,1,0:T(8,128)S(1)}, u32[]{:S(2)}, u32[]{:S(2)}) collective-permute-start(f32[9,16,512]{2,1,0:T(8,128)S(1)} %get-tuple-element.40), channel_id=1, source_target_pairs={{8,0},{16,8},{24,16},{9,1},{17,9},{25,17},{10,2},{18,10},{26,18},{... | collective-permute-start | bytes 884744 | tf_op jit(solution)/shard_map/ppermute | solution.py:469
  61.6 1.6 %collective-permute-start.8 = (f32[72,256]{1,0:T(8,128)S(1)}, f32[72,256]{1,0:T(8,128)S(1)}, u32[]{:S(2)}, u32[]{:S(2)}) collective-permute-start(f32[72,256]{1,0:T(8,128)S(1)} %fusion.1), channel_id=1, source_target_pairs={{0,2},{1,3},{2,0},{3,1},{4,6},{5,7},{6,4},{7,5},{8,10},{9,11},{10,... | collective-permute-start | bytes 221192 | tf_op jit(solution)/shard_map/ppermute | solution.py:343
  63.2 2.8 %collective-permute-done.8 = f32[72,256]{1,0:T(8,128)S(1)} collective-permute-done((f32[72,256]{1,0:T(8,128)S(1)}, f32[72,256]{1,0:T(8,128)S(1)}, u32[]{:S(2)}, u32[]{:S(2)}) %collective-permute-start.8) | collective-permute-done | bytes 73760 | tf_op jit(solution)/shard_map/ppermute | solution.py:343
  66.0 2.7 %collective-permute-start.9 = (f32[72,256]{1,0:T(8,128)S(1)}, f32[72,256]{1,0:T(8,128)S(1)}, u32[]{:S(2)}, u32[]{:S(2)}) collective-permute-start(f32[72,256]{1,0:T(8,128)S(1)} %add.54), channel_id=1, source_target_pairs={{0,4},{1,5},{2,6},{3,7},{4,0},{5,1},{6,2},{7,3},{8,12},{9,13},{10,... | collective-permute-start | bytes 221192 | tf_op jit(solution)/shard_map/ppermute | solution.py:343
  70.0 1.3 %collective-permute-start.13 = (f32[6,2,512]{2,1,0:T(2,128)S(1)}, f32[6,2,512]{2,1,0:T(2,128)S(1)}, u32[]{:S(2)}, u32[]{:S(2)}) collective-permute-start(f32[6,2,512]{2,1,0:T(2,128)S(1)} %get-tuple-element.42), channel_id=1, source_target_pairs={{1,0},{2,1},{3,2},{4,3},{5,4},{6,5},{7,6},{9,8},{10,9},{11,10},{12... | collective-permute-start | bytes 73736 | tf_op jit(solution)/shard_map/ppermute | solution.py:471
  71.3 2.8 %collective-permute-done.13.syh = f32[6,2,512]{2,1,0:T(2,128)S(1)} collective-permute-done((f32[6,2,512]{2,1,0:T(2,128)S(1)}, f32[6,2,512]{2,1,0:T(2,128)S(1)}, u32[]{:S(2)}, u32[]{:S(2)}) %collective-permute-start.13) | collective-permute-done | bytes 24608 | tf_op jit(solution)/shard_map/ppermute | solution.py:471
  75.3 1.5 %collective-permute-start.14 = (f32[72,256]{1,0:T(8,128)S(1)}, f32[72,256]{1,0:T(8,128)S(1)}, u32[]{:S(2)}, u32[]{:S(2)}) collective-permute-start(f32[72,256]{1,0:T(8,128)S(1)} %add.55), channel_id=1, source_target_pairs={{0,8},{8,0},{16,24},{24,16},{1,9},{9,1},{17,25},{25,17},{2,10},{10... | collective-permute-start | bytes 221192 | tf_op jit(solution)/shard_map/ppermute | solution.py:343
  78.0 1.4 %collective-permute-start.16 = (f32[72,256]{1,0:T(8,128)S(1)}, f32[72,256]{1,0:T(8,128)S(1)}, u32[]{:S(2)}, u32[]{:S(2)}) collective-permute-start(f32[72,256]{1,0:T(8,128)S(1)} %add.55), channel_id=1, source_target_pairs={{0,24},{8,16},{16,8},{24,0},{1,25},{9,17},{17,9},{25,1},{2,26},{10... | collective-permute-start | bytes 221192 | tf_op jit(solution)/shard_map/ppermute | solution.py:343
  79.6 1.5 %collective-permute-done.15 = f32[72,256]{1,0:T(8,128)S(1)} collective-permute-done((f32[72,256]{1,0:T(8,128)S(1)}, f32[72,256]{1,0:T(8,128)S(1)}, u32[]{:S(2)}, u32[]{:S(2)}) %collective-permute-start.15) | collective-permute-done | bytes 73760 | tf_op jit(solution)/shard_map/ppermute | solution.py:343
  81.1 2.9 %collective-permute-done.16 = f32[72,256]{1,0:T(8,128)S(1)} collective-permute-done((f32[72,256]{1,0:T(8,128)S(1)}, f32[72,256]{1,0:T(8,128)S(1)}, u32[]{:S(2)}, u32[]{:S(2)}) %collective-permute-start.16) | collective-permute-done | bytes 73760 | tf_op jit(solution)/shard_map/ppermute | solution.py:343
  85.6 1.5 %fields.1 = (f32[3,32,512]{2,1,0:T(8,128)}, f32[3,32,512]{2,1,0:T(8,128)}) custom-call(f32[2,4]{1,0:T(2,128)S(1)} %copy-done.2, s32[32,512]{1,0:T(8,128)S(1)} %bitcast.43, f32[3,32,512]{2,1,0:T(8,128)S(1)} %bitcast.38, f32[3,32,512]{2,1,0:T(8,128)S(1)} %get-tuple-element.36.force, f32[3,32,512]{2,1,0:T(8,128)S(1)} %get-tuple-element.37.dgrad, ...), custom_call_target="tpu_custom_call" | custom-call | tf_op jit(solution)/shard_map/fields/pallas_call | solution.py:491
  87.1 1.6 %finish.1 = (f32[10,256]{1,0:T(8,128)}, f32[1,256]{1,0:T(1,128)}, f32[512,256]{1,0:T(8,128)}, f32[2,256]{1,0:T(2,128)}, f32[9,256]{1,0:T(8,128)}, /*index=5*/f32[1,9]{1,0:T(1,128)}) custom-call(s32[2]{0:T(128)S(1)} %pad_add_fusion.place, f32[4,72,256]{2,1,0:T(8,128)S(1)} %pad_maximum_fusion.mine, f32[4,72,256]{2,1,0:T(8,128)S(1)} %collective-permute-done.17.other), custom_call_target="tpu_custom_call" | custom-call | tf_op jit(solution)/shard_map/finish/pallas_call | solution.py:512
  (30 shorter events, 6.8 us)
Async XLA Ops:
  1.9 12.4 %collective-permute-start = (f32[6,16,512]{2,1,0:T(8,128)S(1)}, f32[6,16,512]{2,1,0:T(8,128)S(1)}, u32[]{:S(2)}, u32[]{:S(2)}) collective-permute-start(f32[6,16,512]{2,1,0:T(8,128)S(1)} %get-tuple-element.32), channel_id=1, source_target_pairs={{0,8},{8,16},{16,24},{1,9},{9,17},{17,25},{2,10},{10,18},{18,26},{... | collective-permute-start | bytes 589832 | tf_op jit(solution)/shard_map/ppermute | solution.py:390
  6.8 10.3 %collective-permute-start.1 = (f32[6,16,512]{2,1,0:T(8,128)S(1)}, f32[6,16,512]{2,1,0:T(8,128)S(1)}, u32[]{:S(2)}, u32[]{:S(2)}) collective-permute-start(f32[6,16,512]{2,1,0:T(8,128)S(1)} %get-tuple-element.33), channel_id=1, source_target_pairs={{8,0},{16,8},{24,16},{9,1},{17,9},{25,17},{10,2},{18,10},{26,18},{... | collective-permute-start | bytes 589832 | tf_op jit(solution)/shard_map/ppermute | solution.py:391
  8.1 3.4 %collective-permute-start.2 = (f32[9,2,512]{2,1,0:T(2,128)S(1)}, f32[9,2,512]{2,1,0:T(2,128)S(1)}, u32[]{:S(2)}, u32[]{:S(2)}) collective-permute-start(f32[9,2,512]{2,1,0:T(2,128)S(1)} %get-tuple-element.34), channel_id=1, source_target_pairs={{0,1},{1,2},{2,3},{3,4},{4,5},{5,6},{6,7},{8,9},{9,10},{10,11},{11... | collective-permute-start | bytes 110600 | tf_op jit(solution)/shard_map/ppermute | solution.py:392
  9.6 4.7 %collective-permute-start.3 = (f32[9,2,512]{2,1,0:T(2,128)S(1)}, f32[9,2,512]{2,1,0:T(2,128)S(1)}, u32[]{:S(2)}, u32[]{:S(2)}) collective-permute-start(f32[9,2,512]{2,1,0:T(2,128)S(1)} %get-tuple-element.35), channel_id=1, source_target_pairs={{1,0},{2,1},{3,2},{4,3},{5,4},{6,5},{7,6},{9,8},{10,9},{11,10},{12... | collective-permute-start | bytes 110600 | tf_op jit(solution)/shard_map/ppermute | solution.py:393
  50.8 1.6 %collective-permute-start.4 = (f32[4,72,256]{2,1,0:T(8,128)S(1)}, f32[4,72,256]{2,1,0:T(8,128)S(1)}, u32[]{:S(2)}, u32[]{:S(2)}) collective-permute-start(f32[4,72,256]{2,1,0:T(8,128)S(1)} %dynamic-slice_bitcast_fusion), channel_id=1, source_target_pairs={{0,1},{1,0},{2,3},{3,2},{4,5},{5,4},{6,7},{7,6},{8,9},{9,8},{10,11... | collective-permute-start | bytes 884744 | tf_op jit(solution)/shard_map/ppermute | solution.py:343
  52.5 9.0 %collective-permute-start.5 = (f32[72,256]{1,0:T(8,128)S(1)}, f32[72,256]{1,0:T(8,128)S(1)}, u32[]{:S(2)}, u32[]{:S(2)}) collective-permute-start(f32[72,256]{1,0:T(8,128)S(1)} %get-tuple-element.56), channel_id=1, source_target_pairs={{0,8},{8,0},{16,24},{24,16},{1,9},{9,1},{17,25},{25,17},{2,10},{10... | collective-permute-start | bytes 221192 | tf_op jit(solution)/shard_map/ppermute | solution.py:343
  54.8 6.7 %collective-permute-start.6 = (f32[72,256]{1,0:T(8,128)S(1)}, f32[72,256]{1,0:T(8,128)S(1)}, u32[]{:S(2)}, u32[]{:S(2)}) collective-permute-start(f32[72,256]{1,0:T(8,128)S(1)} %get-tuple-element.58), channel_id=1, source_target_pairs={{0,16},{8,24},{16,0},{24,8},{1,17},{9,25},{17,1},{25,9},{2,18},{10... | collective-permute-start | bytes 221192 | tf_op jit(solution)/shard_map/ppermute | solution.py:343
  56.3 5.3 %collective-permute-start.7 = (f32[72,256]{1,0:T(8,128)S(1)}, f32[72,256]{1,0:T(8,128)S(1)}, u32[]{:S(2)}, u32[]{:S(2)}) collective-permute-start(f32[72,256]{1,0:T(8,128)S(1)} %get-tuple-element.57), channel_id=1, source_target_pairs={{0,24},{8,16},{16,8},{24,0},{1,25},{9,17},{17,9},{25,1},{2,26},{10... | collective-permute-start | bytes 221192 | tf_op jit(solution)/shard_map/ppermute | solution.py:343
  57.2 17.0 %collective-permute-start.10 = (f32[9,16,512]{2,1,0:T(8,128)S(1)}, f32[9,16,512]{2,1,0:T(8,128)S(1)}, u32[]{:S(2)}, u32[]{:S(2)}) collective-permute-start(f32[9,16,512]{2,1,0:T(8,128)S(1)} %get-tuple-element.39), channel_id=1, source_target_pairs={{0,8},{8,16},{16,24},{1,9},{9,17},{17,25},{2,10},{10,18},{18,26},{... | collective-permute-start | bytes 884744 | tf_op jit(solution)/shard_map/ppermute | solution.py:468
  60.2 15.1 %collective-permute-start.11 = (f32[9,16,512]{2,1,0:T(8,128)S(1)}, f32[9,16,512]{2,1,0:T(8,128)S(1)}, u32[]{:S(2)}, u32[]{:S(2)}) collective-permute-start(f32[9,16,512]{2,1,0:T(8,128)S(1)} %get-tuple-element.40), channel_id=1, source_target_pairs={{8,0},{16,8},{24,16},{9,1},{17,9},{25,17},{10,2},{18,10},{26,18},{... | collective-permute-start | bytes 884744 | tf_op jit(solution)/shard_map/ppermute | solution.py:469
  61.6 4.4 %collective-permute-start.8 = (f32[72,256]{1,0:T(8,128)S(1)}, f32[72,256]{1,0:T(8,128)S(1)}, u32[]{:S(2)}, u32[]{:S(2)}) collective-permute-start(f32[72,256]{1,0:T(8,128)S(1)} %fusion.1), channel_id=1, source_target_pairs={{0,2},{1,3},{2,0},{3,1},{4,6},{5,7},{6,4},{7,5},{8,10},{9,11},{10,... | collective-permute-start | bytes 221192 | tf_op jit(solution)/shard_map/ppermute | solution.py:343
  66.0 5.3 %collective-permute-start.9 = (f32[72,256]{1,0:T(8,128)S(1)}, f32[72,256]{1,0:T(8,128)S(1)}, u32[]{:S(2)}, u32[]{:S(2)}) collective-permute-start(f32[72,256]{1,0:T(8,128)S(1)} %add.54), channel_id=1, source_target_pairs={{0,4},{1,5},{2,6},{3,7},{4,0},{5,1},{6,2},{7,3},{8,12},{9,13},{10,... | collective-permute-start | bytes 221192 | tf_op jit(solution)/shard_map/ppermute | solution.py:343
  68.7 2.7 %collective-permute-start.12 = (f32[6,2,512]{2,1,0:T(2,128)S(1)}, f32[6,2,512]{2,1,0:T(2,128)S(1)}, u32[]{:S(2)}, u32[]{:S(2)}) collective-permute-start(f32[6,2,512]{2,1,0:T(2,128)S(1)} %get-tuple-element.41), channel_id=1, source_target_pairs={{0,1},{1,2},{2,3},{3,4},{4,5},{5,6},{6,7},{8,9},{9,10},{10,11},{11... | collective-permute-start | bytes 73736 | tf_op jit(solution)/shard_map/ppermute | solution.py:470
  70.0 4.2 %collective-permute-start.13 = (f32[6,2,512]{2,1,0:T(2,128)S(1)}, f32[6,2,512]{2,1,0:T(2,128)S(1)}, u32[]{:S(2)}, u32[]{:S(2)}) collective-permute-start(f32[6,2,512]{2,1,0:T(2,128)S(1)} %get-tuple-element.42), channel_id=1, source_target_pairs={{1,0},{2,1},{3,2},{4,3},{5,4},{6,5},{7,6},{9,8},{10,9},{11,10},{12... | collective-permute-start | bytes 73736 | tf_op jit(solution)/shard_map/ppermute | solution.py:471
  75.3 4.4 %collective-permute-start.14 = (f32[72,256]{1,0:T(8,128)S(1)}, f32[72,256]{1,0:T(8,128)S(1)}, u32[]{:S(2)}, u32[]{:S(2)}) collective-permute-start(f32[72,256]{1,0:T(8,128)S(1)} %add.55), channel_id=1, source_target_pairs={{0,8},{8,0},{16,24},{24,16},{1,9},{9,1},{17,25},{25,17},{2,10},{10... | collective-permute-start | bytes 221192 | tf_op jit(solution)/shard_map/ppermute | solution.py:343
  76.8 4.4 %collective-permute-start.15 = (f32[72,256]{1,0:T(8,128)S(1)}, f32[72,256]{1,0:T(8,128)S(1)}, u32[]{:S(2)}, u32[]{:S(2)}) collective-permute-start(f32[72,256]{1,0:T(8,128)S(1)} %add.55), channel_id=1, source_target_pairs={{0,16},{8,24},{16,0},{24,8},{1,17},{9,25},{17,1},{25,9},{2,18},{10... | collective-permute-start | bytes 221192 | tf_op jit(solution)/shard_map/ppermute | solution.py:343
  78.0 6.0 %collective-permute-start.16 = (f32[72,256]{1,0:T(8,128)S(1)}, f32[72,256]{1,0:T(8,128)S(1)}, u32[]{:S(2)}, u32[]{:S(2)}) collective-permute-start(f32[72,256]{1,0:T(8,128)S(1)} %add.55), channel_id=1, source_target_pairs={{0,24},{8,16},{16,8},{24,0},{1,25},{9,17},{17,9},{25,1},{2,26},{10... | collective-permute-start | bytes 221192 | tf_op jit(solution)/shard_map/ppermute | solution.py:343
  84.0 0.9 %copy-start = (f32[3,2,16,512]{3,2,1,0:T(8,128)S(1)}, f32[3,2,16,512]{3,2,1,0:T(8,128)}, u32[]{:S(2)}) copy-start(f32[3,2,16,512]{3,2,1,0:T(8,128)} %param.17) | copy-start | bytes 589828
  84.0 0.9 %copy-start.1 = (s32[2,16,512]{2,1,0:T(8,128)S(1)}, s32[2,16,512]{2,1,0:T(8,128)}, u32[]{:S(2)}) copy-start(s32[2,16,512]{2,1,0:T(8,128)} %param.13) | copy-start | bytes 196612
  84.0 3.0 %collective-permute-start.17 = (f32[4,72,256]{2,1,0:T(8,128)S(1)}, f32[4,72,256]{2,1,0:T(8,128)S(1)}, u32[]{:S(2)}, u32[]{:S(2)}) collective-permute-start(f32[4,72,256]{2,1,0:T(8,128)S(1)} %pad_maximum_fusion.mine), channel_id=1, source_target_pairs={{0,1},{1,0},{2,3},{3,2},{4,5},{5,4},{6,7},{7,6},{8,9},{9,8},{10,11... | collective-permute-start | bytes 884744 | tf_op jit(solution)/shard_map/ppermute | solution.py:343
  84.8 0.7 copy-start.2

commit v3 on v2

v3 whole, which is shorter than its diff:
```python
import functools
import jax
import jax.numpy as jnp
from jax import lax
from jax.experimental import pallas as pl
from jax.experimental.pallas import tpu as pltpu
from jax.sharding import PartitionSpec as P

FEAT = 10
OUT = 9
HID = 256
PHASES = 8
NPARAM = 136713
SMALL = 8
GROUPS = 5

time_step = 0.25
viscosity = 0.2
norm_eps = 1e-06
two_pi = 6.283185307179586

bf16 = jnp.bfloat16
f32 = jnp.float32
VMEM = pl.BlockSpec(memory_space=pltpu.VMEM)
SMEM = pl.BlockSpec(memory_space=pltpu.SMEM)
HBM = pl.BlockSpec(memory_space=pltpu.HBM)


def fetch(sources, targets, sems):
    copies = [
        pltpu.make_async_copy(source, target, sems.at[k])
        for k, (source, target) in enumerate(zip(sources, targets))
    ]
    for copy in copies:
        copy.start()
    return copies


def pick(table, row, material):
    value = jnp.full(material.shape, table[row, 0], f32)
    for kind in range(1, table.shape[1]):
        value = jnp.where(material == kind, table[row, kind], value)
    return value


def step_factor(table, material):
    occupied = jnp.where(material > 0, 1.0, 0.0).astype(f32)
    return occupied, pick(table, 1, material)


def x_ends(field, low, high, rows):
    return (
        jnp.concatenate([low, field[:-rows]], 0),
        jnp.concatenate([field[rows:], high], 0),
    )


def y_ends(field, low, high, rows):
    planes = field.shape[0] // rows
    where = lax.broadcasted_iota(jnp.int32, field.shape, 0)

    def spread(edge):
        return jnp.concatenate(
            [jnp.broadcast_to(edge[p : p + 1], (rows, field.shape[1])) for p in range(planes)], 0
        )

    before, after = pltpu.roll(field, 1, 0), pltpu.roll(field, field.shape[0] - 1, 0)
    low = 0.0 if low is None else spread(low)
    high = 0.0 if high is None else spread(high)
    return (
        jnp.where(where % rows == 0, low, before),
        jnp.where(where % rows == rows - 1, high, after),
    )


def z_ends(field):
    lanes = field.shape[1]
    where = lax.broadcasted_iota(jnp.int32, field.shape, 1)
    return (
        jnp.where(where == 0, 0.0, pltpu.roll(field, 1, 1)),
        jnp.where(where == lanes - 1, 0.0, pltpu.roll(field, lanes - 1, 1)),
    )


def half_diff(ends):
    return (ends[1] - ends[0]) * 0.5


def faces_kernel(rows, *refs):
    sources, (xf, xb, yf, yb), targets, sems = refs[:5], refs[5:9], refs[9:14], refs[14]
    for copy in fetch(sources, targets, sems):
        copy.wait()
    table, material, displacement, velocity, cotangent = targets
    occupied, density = step_factor(table, material[...])
    for i in range(3):
        carried = time_step * occupied * cotangent[i] / density
        for slot, field in ((i, displacement[i]), (3 + i, carried), (6 + i, velocity[i])):
            if slot < 6:
                xf[slot] = field[rows:]
            xb[slot] = field[:rows]
            for p in range(2):
                yf[slot, p : p + 1] = field[(p + 1) * rows - 1 : (p + 1) * rows]
                yb[slot, p : p + 1] = field[p * rows : p * rows + 1]


def network_kernel(plane, rows, block, *refs):
    sources, refs = refs[: 12 - plane * 3], refs[12 - plane * 3 :]
    (edge, yl, yh), refs = refs[:3], refs[3:]
    if plane:
        (yf_first, yb_first), given, refs = refs[:2], refs[2:13], refs[13:]
        (sx, yf, yb, rest, grads), refs = refs[:5], refs[5:]
    else:
        (sx, yf, yb, rest), kept, refs = refs[:4], refs[4:15], refs[15:]
    targets, sems, refs = refs[: len(sources)], refs[len(sources)], refs[len(sources) + 1 :]
    grid_in, grid_delta, feats, delta, net, back, wide, *refs = refs
    copies = fetch(sources, targets, sems)
    if plane:
        acc_mid, acc_in, acc_out, acc_b, acc_bo = refs
        win, winT, wmidT, wout, woutT, bias = given[5:]
        for ref, source in zip(refs, given[:5]):
            ref[...] = source[...]
    else:
        acc_mid, acc_in, acc_out, acc_b, acc_bo = kept[:5]
        win, winT, wmidT, wout, woutT, bias = kept[5:]
        for ref in kept[:5]:
            ref[...] = jnp.zeros_like(ref)
    for copy in copies:
        copy.wait()
    table, clock, b_out, material, phase, displacement, cotangent, w_mid = targets[:8]
    lanes = material.shape[1]
    tiles = lanes // 128
    voxels = rows * lanes
    own = slice(plane * rows, (plane + 1) * rows)
    occupied, density = step_factor(table, material[...])
    strength = (occupied * pick(table, 0, material[...]))[own]

    if not plane:
        w_inT, b_in, b_mid, w_out = targets[8:]
        wide[...] = jnp.zeros_like(wide)
        wide[:FEAT] = w_inT[...].astype(f32)
        winT[...] = wide[:16].astype(bf16)
        win[...] = wide[...].T[:, :16].astype(bf16)
        wide[...] = jnp.zeros_like(wide)
        wide[:OUT] = w_out[...].astype(f32)
        wout[...] = wide[:16].astype(bf16)
        woutT[...] = wide[...].T[:, :16].astype(bf16)
        for k in range(2):
            wmidT[k] = w_mid[k].astype(f32).T.astype(bf16)
        for k, row in enumerate((b_in[...], b_mid[0:1], b_mid[1:2])):
            bias[k] = jnp.broadcast_to(row, (128, HID)).T

    def put(ref, slot, field):
        for t in range(tiles):
            ref[t, slot * rows : (slot + 1) * rows] = field[:, t * 128 : (t + 1) * 128]

    def strains(field, slot):
        mine = field[own]
        ends = (field[:rows], edge[slot]) if plane else (edge[slot], field[rows:])
        low, high = yl[slot, plane : plane + 1], yh[slot, plane : plane + 1]
        return half_diff(ends), half_diff(y_ends(mine, low, high, rows)), half_diff(z_ends(mine))

    factor = time_step * occupied
    for i in range(3):
        for j, value in enumerate(strains(displacement[i], i)):
            put(grid_in, 3 * i + j, value)
        for j, value in enumerate(strains(factor * cotangent[i] / density, 3 + i)):
            put(grid_delta, 3 * i + j, strength * -value)
    put(grid_in, 9, jnp.sin(two_pi * phase[own].astype(f32) / PHASES + clock[0]))
    put(grid_in, 10, jnp.ones((rows, lanes), f32))
    for slot in range(11, 16):
        put(grid_in, slot, jnp.zeros((rows, lanes), f32))
    for slot in range(9, 16):
        put(grid_delta, slot, jnp.zeros((rows, lanes), f32))
    for r in range(rows):
        for t in range(tiles):
            at = slice((r * tiles + t) * 128, (r * tiles + t + 1) * 128)
            feats[:, at] = grid_in[t, pl.ds(r, 16, stride=rows), :].astype(bf16)
            delta[:, at] = grid_delta[t, pl.ds(r, 16, stride=rows), :].astype(bf16)

    rowid = lax.broadcasted_iota(jnp.int32, (16, 1), 0)
    bias_out = jnp.zeros((16, 1), f32)
    for k in range(OUT):
        bias_out = jnp.where(rowid == k, b_out[k], bias_out)

    def mul(a, b):
        return jnp.dot(a, b, preferred_element_type=f32)

    def mul_t(a, b):
        return lax.dot_general(a, b, (((1,), (1,)), ((), ())), preferred_element_type=f32)

    def lane_sum(value):
        total = value[:, :128].astype(f32)
        for k in range(1, block // 128):
            total = total + value[:, k * 128 : (k + 1) * 128].astype(f32)
        return total

    def slope(value):
        wider = value.astype(f32)
        return 1.0 - wider * wider

    def step(index, carry):
        at = pl.ds(pl.multiple_of(index * block, block), block)
        f, d = feats[:, at], delta[:, at]
        h1 = jnp.tanh(mul(win[...], f) + bias[0][:, :1]).astype(bf16)
        h2 = jnp.tanh(mul(w_mid[0], h1) + bias[1][:, :1]).astype(bf16)
        h3 = jnp.tanh(mul(w_mid[1], h2) + bias[2][:, :1]).astype(bf16)
        net[:, at] = mul(wout[...], h3) + bias_out
        acc_out[...] += mul_t(d, h3)
        acc_bo[...] += lane_sum(d)
        d3 = (mul(woutT[...], d) * slope(h3)).astype(bf16)
        acc_mid[HID:] += mul_t(d3, h2)
        acc_b[1] += lane_sum(d3)
        d2 = (mul(wmidT[1], d3) * slope(h2)).astype(bf16)
        acc_mid[:HID] += mul_t(d2, h1)
        acc_b[0] += lane_sum(d2)
        d1 = (mul(wmidT[0], d2) * slope(h1)).astype(bf16)
        acc_in[...] += mul_t(f, d1)
        back[:, at] = mul(winT[...], d1)
        return carry

    lax.fori_loop(0, voxels // block, step, 0)

    for r in range(rows):
        for t in range(tiles):
            at = slice((r * tiles + t) * 128, (r * tiles + t + 1) * 128)
            grid_in[t, pl.ds(r, 16, stride=rows), :] = net[:, at]
            grid_delta[t, pl.ds(r, 16, stride=rows), :] = back[:, at]

    def get(ref, slot):
        return jnp.concatenate(
            [ref[t, slot * rows : (slot + 1) * rows] for t in range(tiles)], axis=1
        )

    for base, ref, scale in ((0, grid_in, strength), (3, grid_delta, None)):
        for i in range(3):
            along = [get(ref, 3 * i + j) for j in range(3)]
            if scale is not None:
                along = [scale * item for item in along]
            slot = base + i
            sx[slot] = along[0]
            yf[slot, plane : plane + 1] = along[1][rows - 1 :]
            yb[slot, plane : plane + 1] = along[1][:1]
            if plane:
                yf[slot, 0:1] = yf_first[slot, 0:1]
                yb[slot, 0:1] = yb_first[slot, 0:1]
            rest[slot] = half_diff(y_ends(along[1], None, None, rows)) + half_diff(
                z_ends(along[2])
            )
    if not plane:
        return
    for i in range(3):
        sx[6 + i] = targets[8][i, own]

    chunks = grads.shape[0]
    part = 2 * HID // chunks
    for c in range(chunks):
        grads[c, :part] = acc_mid[c * part : (c + 1) * part]
        grads[c, part:] = jnp.zeros((SMALL, HID), f32)
    grads[0, part:] = acc_in[:8]
    grads[1, part:] = jnp.where(rowid[:8] < 3, acc_in[8:], 0.0)
    grads[2, part:] = acc_out[:8]
    grads[3, part:] = acc_out[8:]
    for k in range(2):
        grads[4, part + k : part + k + 1] = jnp.sum(acc_b[k].T, axis=0, keepdims=True)
    wide[...] = jnp.zeros_like(wide)
    wide[:16, :128] = acc_bo[...]
    grads[4, part + 2 : part + 3, :128] = jnp.sum(wide[:, :128].T, axis=0, keepdims=True)


def fields_kernel(
    rows,
    table,
    material,
    velocity,
    first,
    second,
    rest_first,
    rest_second,
    xh,
    yl,
    yh,
    sxl,
    sxh,
    syl,
    syh,
    velocity_new,
    displacement_grad,
):
    size, lanes = material.shape
    occupied, density = step_factor(table, material[...])
    where = lax.broadcasted_iota(jnp.int32, (size, lanes), 0)

    def spread(edge):
        return jnp.concatenate(
            [jnp.broadcast_to(edge[p : p + 1], (rows, lanes)) for p in range(2)], 0
        )

    def total(slot):
        value = jnp.concatenate(
            [
                rest_first[slot] + half_diff((sxl[slot], second[slot])),
                rest_second[slot] + half_diff((first[slot], sxh[slot])),
            ],
            0,
        )
        value = value - jnp.where(where % rows == 0, spread(syl[slot]) * 0.5, 0.0)
        return value + jnp.where(where % rows == rows - 1, spread(syh[slot]) * 0.5, 0.0)

    for i in range(3):
        value = velocity[i]
        around = -6.0 * value
        for low, high in (
            x_ends(value, sxl[6 + i], xh[6 + i], rows),
            y_ends(value, yl[6 + i], yh[6 + i], rows),
            z_ends(value),
        ):
            around = around + high + low
        pull = total(i) + viscosity * around
        velocity_new[i] = value + time_step * occupied * pull / density
        displacement_grad[i] = -total(3 + i)


def finish_kernel(place, mine, other, g_in, gb_in, g_mid, gb_mid, g_out, gb_out, small):
    count, height, _ = mine.shape
    part = height - SMALL
    total = jnp.sum(jnp.square(mine[...])) + jnp.sum(jnp.square(other[...]))
    scale = lax.rsqrt(jnp.full((1, 1), total, f32) / NPARAM + norm_eps)
    half, index = place[0], place[1]
    for m in range(count):
        for ref, side in ((mine, half), (other, 1 - half)):
            chunk = side * count + (index ^ m)
            g_mid[pl.ds(pl.multiple_of(chunk * part, part), part), :] = ref[m, :part] * scale
            small[pl.ds(pl.multiple_of(chunk * SMALL, SMALL), SMALL), :] = ref[m, part:] * scale
    g_in[...] = small[:FEAT]
    gb_in[...] = small[10:11]
    g_out[...] = small[16 : 16 + OUT]
    gb_mid[...] = small[32:34]
    gb_out[...] = small[34:35, :OUT]


def shapes(*items):
    return [jax.ShapeDtypeStruct(item, f32) for item in items]


def stay(value):
    if value.size < 2:
        return value
    return pltpu.with_memory_space_constraint(value, pltpu.HBM)


def along(axis, step):
    count = lax.axis_size(axis)
    return [(i, i + step) for i in range(count) if 0 <= i + step < count]


def swap(value, axis, mask):
    return lax.ppermute(value, axis, [(i, i ^ mask) for i in range(lax.axis_size(axis))])


def body(
    material,
    phase,
    clock,
    displacement,
    velocity,
    cotangent,
    material_table,
    w_in,
    b_in,
    w_mid,
    b_mid,
    w_out,
    b_out,
):
    planes, rows, lanes = material.shape
    size = planes * rows
    nx, ny = lax.axis_size("gx"), lax.axis_size("gy")
    chunks = 2 * nx
    part = 2 * HID // chunks
    assert planes == 2 and chunks >= GROUPS and ny % 2 == 0 and part % 8 == 0
    material = material.reshape(size, lanes)
    phase = phase.reshape(size, lanes)
    displacement = displacement.reshape(3, size, lanes)
    velocity = velocity.reshape(3, size, lanes)
    cotangent = cotangent.reshape(3, size, lanes)

    faces = pl.pallas_call(
        functools.partial(faces_kernel, rows),
        out_shape=shapes((6, rows, lanes), (9, rows, lanes), *[(9, 2, lanes)] * 2),
        in_specs=[HBM] * 5,
        out_specs=[VMEM] * 4,
        scratch_shapes=[
            pltpu.SMEM(material_table.shape, f32),
            pltpu.VMEM((size, lanes), jnp.int32),
            *[pltpu.VMEM((3, size, lanes), f32)] * 3,
            pltpu.SemaphoreType.DMA((5,)),
        ],
        compiler_params=pltpu.CompilerParams(vmem_limit_bytes=6 << 20),
        name="faces",
    )(*map(stay, (material_table, material, displacement, velocity, cotangent)))
    xl = lax.ppermute(faces[0], "gx", along("gx", 1))
    yl = lax.ppermute(faces[2], "gy", along("gy", 1))
    yh = lax.ppermute(faces[3], "gy", along("gy", -1))
    xh = lax.ppermute(faces[1], "gx", along("gx", -1))

    voxels = rows * lanes
    block = 4096
    while voxels % block:
        block //= 2
    handed = [
        ((2 * HID, HID), f32),
        ((16, HID), f32),
        ((16, HID), f32),
        ((2, HID, 128), f32),
        ((16, 128), f32),
        ((HID, 16), bf16),
        ((16, HID), bf16),
        ((2, HID, HID), bf16),
        ((16, HID), bf16),
        ((HID, 16), bf16),
        ((3, HID, 128), f32),
    ]

    def network(plane, sources, near):
        outs = [jax.ShapeDtypeStruct(*item) for item in handed]
        if plane:
            outs = shapes((chunks, part + SMALL, HID))
        return pl.pallas_call(
            functools.partial(network_kernel, plane, rows, block),
            out_shape=shapes(
                (6 + 3 * plane, rows, lanes), *[(6, 1 + plane, lanes)] * 2, (6, rows, lanes)
            )
            + outs,
            in_specs=[HBM] * len(sources) + [VMEM] * len(near),
            out_specs=[VMEM] * (4 + len(outs)),
            scratch_shapes=[
                *[pltpu.SMEM(item.shape, f32) for item in sources[:3]],
                *[pltpu.VMEM(item.shape, item.dtype) for item in sources[3:]],
                pltpu.SemaphoreType.DMA((len(sources),)),
                *[pltpu.VMEM((lanes // 128, 16 * rows, 128), f32)] * 2,
                *[pltpu.VMEM((16, voxels), bf16)] * 2,
                *[pltpu.VMEM((16, voxels), f32)] * 2,
                pltpu.VMEM((128, HID), f32),
                *[pltpu.VMEM(*item) for item in handed[: 5 * plane]],
            ],
            compiler_params=pltpu.CompilerParams(vmem_limit_bytes=36 << 20),
            cost_estimate=pl.CostEstimate(
                flops=6 * voxels * (HID * FEAT + 2 * HID * HID + OUT * HID),
                bytes_accessed=64 * voxels,
                transcendentals=3 * HID * voxels,
            ),
            name="network",
        )(*map(stay, sources), *near)

    common = [material_table, clock, b_out, material, phase, displacement, cotangent, w_mid]
    first = network(
        0, common + [w_in.T, b_in.reshape(1, HID), b_mid, w_out], [xl, yl, yh]
    )
    sxh = lax.ppermute(first[0], "gx", along("gx", -1))
    second = network(1, common + [velocity], [xh, yl, yh, *first[1:3], *first[4:]])
    sxl = lax.ppermute(second[0], "gx", along("gx", 1))

    half = lax.axis_index("gy") % 2
    index = lax.axis_index("gx")
    pile, sxh = lax.optimization_barrier((second[4], sxh))
    pile = pile.reshape(2, nx, part + SMALL, HID)
    kept = lax.dynamic_index_in_dim(pile, half, 0, keepdims=False)
    sent = lax.dynamic_index_in_dim(pile, 1 - half, 0, keepdims=False)
    kept, face = lax.optimization_barrier((kept + swap(sent, "gy", 1), second[1]))
    syl = lax.ppermute(face, "gy", along("gy", 1))
    share = lax.dynamic_index_in_dim(kept, index, 0, keepdims=False)
    for m in range(1, nx):
        piece = lax.dynamic_index_in_dim(kept, index ^ m, 0, keepdims=False)
        share = share + swap(piece, "gx", m)
    share, face = lax.optimization_barrier((share, second[2]))
    syh = lax.ppermute(face, "gy", along("gy", -1))
    mask = 2
    while mask < ny:
        share = share + swap(share, "gy", mask)
        if mask == 2:
            share, sxl, syl = lax.optimization_barrier((share, sxl, syl))
        mask *= 2
    share, syh = lax.optimization_barrier((share, syh))
    mine = jnp.stack([share] + [swap(share, "gx", m) for m in range(1, nx)])

    fields = pl.pallas_call(
        functools.partial(fields_kernel, rows),
        out_shape=shapes(*[(3, size, lanes)] * 2),
        in_specs=[SMEM] + [VMEM] * 13,
        out_specs=[VMEM] * 2,
        compiler_params=pltpu.CompilerParams(vmem_limit_bytes=6 << 20),
        name="fields",
    )(
        stay(material_table),
        stay(material),
        stay(velocity),
        first[0],
        second[0],
        first[3],
        second[3],
        xh,
        yl,
        yh,
        sxl,
        sxh,
        syl,
        syh,
    )
    mine, *fields = lax.optimization_barrier((mine, *fields))
    other = swap(mine, "gy", 1)
    place = jnp.stack([half, index]).astype(jnp.int32)
    done = pl.pallas_call(
        finish_kernel,
        out_shape=shapes((FEAT, HID), (1, HID), (2 * HID, HID), (2, HID), (OUT, HID), (1, OUT)),
        in_specs=[SMEM] + [VMEM] * 2,
        out_specs=[VMEM] * 6,
        scratch_shapes=[pltpu.VMEM((chunks * SMALL, HID), f32)],
        compiler_params=pltpu.CompilerParams(vmem_limit_bytes=6 << 20),
        name="finish",
    )(place, mine, other)
    shape = (3, planes, rows, lanes)
    return (
        fields[0].reshape(shape),
        fields[1].reshape(shape),
        done[0].T,
        done[1].reshape(HID),
        done[2].reshape(2, HID, HID),
        done[3],
        done[4],
        done[5].reshape(OUT),
    )


def solution(mesh):
    in_specs = (
        P("gx", "gy", None),
        P("gx", "gy", None),
        P(),
        P(None, "gx", "gy", None),
        P(None, "gx", "gy", None),
        P(None, "gx", "gy", None),
        P(),
        P(),
        P(),
        P(),
        P(),
        P(),
        P(),
    )
    out_specs = (P(None, "gx", "gy", None), P(None, "gx", "gy", None), P(), P(), P(), P(), P(), P())
    return jax.shard_map(body, mesh=mesh, in_specs=in_specs, out_specs=out_specs, check_vma=False)
```

time: 89.1 us -> 86.7 us (0.973)
  waiting for transfers between devices: 18.4 us -> 9.99 us
  starting transfers between devices: 29.8 us -> 35.6 us
  Pallas kernels: 38.1 us -> 39 us
    ppermute x10, starting transfers between devices: 14 us -> 19.3 us  [swap(): lax.ppermute(value, axis, [(i, i ^ mask) for i in range(lax.axis_size(axi...]
    ppermute x4, waiting for transfers between devices: 3.93 us -> 0.01 us  [the longest x1 0.01 us: body(): sxh = lax.ppermute(first[0], 'gx', along('gx', -1))]
    ppermute x1, waiting for transfers between devices: 2.77 us -> 0.01 us  [body(): xh = lax.ppermute(faces[1], 'gx', along('gx', -1))]
    ppermute x1, waiting for transfers between devices: 2.77 us -> 1.47 us  [body(): yh = lax.ppermute(faces[3], 'gy', along('gy', -1))]
    pallas_call x2 -> x3, Pallas kernels: 35 us -> 35.5 us  [the longest x2 34.2 us: network(): pl.pallas_call(functools.partial(network_kernel, plane, rows, block), out...]
  transfers between devices with their start and end apart: 18 -> 18, of which waited for: 10 -> 7; matrix products, arithmetic and copies ran while one was open for 0% -> 0% of each run, Pallas kernels for 2% -> 42%
where the time goes in v3:
time: 86.7 us; the launch traced here: 86.3 us
  Pallas kernels  39 us (45%)
  starting transfers between devices  35.6 us (41%)
  waiting for transfers between devices  9.99 us (12%)
  between operations  1.48 us (2%)
    pallas_call x2, Pallas kernels, network(): pl.pallas_call(functools.partial(network_kernel, plane, rows, block), out...  34.2 us
    ppermute x10, starting transfers between devices, swap(): lax.ppermute(value, axis, [(i, i ^ mask) for i in range(lax.axis_size(axi...  19.3 us
    ppermute x10, waiting for transfers between devices, swap(): lax.ppermute(value, axis, [(i, i ^ mask) for i in range(lax.axis_size(axi...  8.5 us
    ppermute x1, starting transfers between devices, body(): xl = lax.ppermute(faces[0], 'gx', along('gx', 1))  4.85 us
    ppermute x1, starting transfers between devices, body(): sxl = lax.ppermute(second[0], 'gx', along('gx', 1))  3.31 us
    pallas_call x1, Pallas kernels, body(): pl.pallas_call(functools.partial(fields_kernel, rows), out_shape=shapes(*...  1.96 us
  transfers between devices with their start and end apart: 18, of which 7 were waited for; matrix products, arithmetic and copies ran while one was open for 0% of the time, Pallas kernels for 42%

profile of v3, /device:TPU:0, one launch (start us, length us, event | category | flops | bytes accessed | tf_op | source)
XLA Modules:
  0.0 86.3 jit_solution(294577635623434156)
XLA Ops:
  0.6 1.3 %faces.1 = (f32[6,16,512]{2,1,0:T(8,128)S(1)}, f32[9,16,512]{2,1,0:T(8,128)S(1)}, f32[9,2,512]{2,1,0:T(2,128)S(1)}, f32[9,2,512]{2,1,0:T(2,128)S(1)}) custom-call(f32[2,4]{1,0:T(2,128)} %table.1, s32[32,512]{1,0:T(8,128)} %bitcast.42, f32[3,32,512]{2,1,0:T(8,128)} %bitcast.46, f32[3,32,512]{2,1,0:T(8,128)} %bitcast.38, f32[3,32,512]{2,1,0:T(8,128)} %bitcast.49), custom_call_target="tpu_custom_call" | custom-call | tf_op jit(solution)/shard_map/faces/pallas_call | solution.py:387
  1.9 4.9 %collective-permute-start.3 = (f32[6,16,512]{2,1,0:T(8,128)S(1)}, f32[6,16,512]{2,1,0:T(8,128)S(1)}, u32[]{:S(2)}, u32[]{:S(2)}) collective-permute-start(f32[6,16,512]{2,1,0:T(8,128)S(1)} %get-tuple-element.57), channel_id=1, source_target_pairs={{0,8},{8,16},{16,24},{1,9},{9,17},{17,25},{2,10},{10,18},{18,26},{... | collective-permute-start | bytes 589832 | tf_op jit(solution)/shard_map/ppermute | solution.py:401
  6.8 1.5 %collective-permute-start.1 = (f32[9,2,512]{2,1,0:T(2,128)S(1)}, f32[9,2,512]{2,1,0:T(2,128)S(1)}, u32[]{:S(2)}, u32[]{:S(2)}) collective-permute-start(f32[9,2,512]{2,1,0:T(2,128)S(1)} %get-tuple-element.55), channel_id=1, source_target_pairs={{0,1},{1,2},{2,3},{3,4},{4,5},{5,6},{6,7},{8,9},{9,10},{10,11},{11... | collective-permute-start | bytes 110600 | tf_op jit(solution)/shard_map/ppermute | solution.py:402
  8.3 1.3 %collective-permute-start.2 = (f32[9,2,512]{2,1,0:T(2,128)S(1)}, f32[9,2,512]{2,1,0:T(2,128)S(1)}, u32[]{:S(2)}, u32[]{:S(2)}) collective-permute-start(f32[9,2,512]{2,1,0:T(2,128)S(1)} %get-tuple-element.56), channel_id=1, source_target_pairs={{1,0},{2,1},{3,2},{4,3},{5,4},{6,5},{7,6},{9,8},{10,9},{11,10},{12... | collective-permute-start | bytes 110600 | tf_op jit(solution)/shard_map/ppermute | solution.py:403
  9.6 1.3 %collective-permute-start = (f32[9,16,512]{2,1,0:T(8,128)S(1)}, f32[9,16,512]{2,1,0:T(8,128)S(1)}, u32[]{:S(2)}, u32[]{:S(2)}) collective-permute-start(f32[9,16,512]{2,1,0:T(8,128)S(1)} %get-tuple-element.54), channel_id=1, source_target_pairs={{8,0},{16,8},{24,16},{9,1},{17,9},{25,17},{10,2},{18,10},{26,18},{... | collective-permute-start | bytes 884744 | tf_op jit(solution)/shard_map/ppermute | solution.py:404
  11.5 1.5 %collective-permute-done.2.refs_14_.refs_11_.yh = f32[9,2,512]{2,1,0:T(2,128)S(1)} collective-permute-done((f32[9,2,512]{2,1,0:T(2,128)S(1)}, f32[9,2,512]{2,1,0:T(2,128)S(1)}, u32[]{:S(2)}, u32[]{:S(2)}) %collective-permute-start.2) | collective-permute-done | bytes 36896 | tf_op jit(solution)/shard_map/ppermute | solution.py:403
  13.0 17.1 %network.2 = (f32[6,16,512]{2,1,0:T(8,128)S(1)}, f32[6,1,512]{2,1,0:T(1,128)S(1)}, f32[6,1,512]{2,1,0:T(1,128)S(1)}, f32[6,16,512]{2,1,0:T(8,128)S(1)}, f32[512,...) custom-call(f32[2,4]{1,0:T(2,128)} %table.1, ...), custom_call_target="tpu_custom_call" | custom-call | flops 6681526272 | bytes 524288 | tf_op jit(solution)/shard_map/network/pallas_call | solution.py:428
  30.1 1.5 %collective-permute-start.4 = (f32[6,16,512]{2,1,0:T(8,128)S(1)}, f32[6,16,512]{2,1,0:T(8,128)S(1)}, u32[]{:S(2)}, u32[]{:S(2)}) collective-permute-start(f32[6,16,512]{2,1,0:T(8,128)S(1)} %get-tuple-element.72.first), channel_id=1, source_target_pairs={{8,0},{16,8},{24,16},{9,1},{17,9},{25,17},{10,2},{18,10},{26,18},{... | collective-permute-start | bytes 589832 | tf_op jit(solution)/shard_map/ppermute | solution.py:459
  31.6 17.1 %network.3 = (f32[9,16,512]{2,1,0:T(8,128)S(1)}, f32[6,2,512]{2,1,0:T(2,128)S(1)}, f32[6,2,512]{2,1,0:T(2,128)S(1)}, f32[6,16,512]{2,1,0:T(8,128)S(1)}, f32[8,72,256]{2,1,0:T(8,128)S(1)}) custom-call(f32[2,4]{1,0:T(2,128)} %table.1, f32[1]{0:T(128)S(6)} %copy.21.refs_1_, f32[9]{0:T(128)} %refs_2_.3, s32[32,512]{1,0:T(8,128)} %bitcast.44, ...), custom_call_target="tpu_custom_call" | custom-call | flops 6681526272 | bytes 524288 | tf_op jit(solution)/shard_map/network/pallas_call | solution.py:428
  48.7 3.0 %collective-permute-start.5 = (f32[4,72,256]{2,1,0:T(8,128)S(1)}, f32[4,72,256]{2,1,0:T(8,128)S(1)}, u32[]{:S(2)}, u32[]{:S(2)}) collective-permute-start(f32[4,72,256]{2,1,0:T(8,128)S(1)} %dynamic-slice_bitcast_fusion), channel_id=1, source_target_pairs={{0,1},{1,0},{2,3},{3,2},{4,5},{5,4},{6,7},{7,6},{8,9},{9,8},{10,11... | collective-permute-start | bytes 884744 | tf_op jit(solution)/shard_map/ppermute | solution.py:357
  51.8 1.2 %collective-permute-done.5 = f32[4,72,256]{2,1,0:T(8,128)S(1)} collective-permute-done((f32[4,72,256]{2,1,0:T(8,128)S(1)}, f32[4,72,256]{2,1,0:T(8,128)S(1)}, u32[]{:S(2)}, u32[]{:S(2)}) %collective-permute-start.5) | collective-permute-done | bytes 294944 | tf_op jit(solution)/shard_map/ppermute | solution.py:357
  53.1 2.4 %collective-permute-start.6 = (f32[72,256]{1,0:T(8,128)S(1)}, f32[72,256]{1,0:T(8,128)S(1)}, u32[]{:S(2)}, u32[]{:S(2)}) collective-permute-start(f32[72,256]{1,0:T(8,128)S(1)} %get-tuple-element.100), channel_id=1, source_target_pairs={{0,8},{8,0},{16,24},{24,16},{1,9},{9,1},{17,25},{25,17},{2,10},{10... | collective-permute-start | bytes 221192 | tf_op jit(solution)/shard_map/ppermute | solution.py:357
  55.5 1.7 %collective-permute-start.7 = (f32[72,256]{1,0:T(8,128)S(1)}, f32[72,256]{1,0:T(8,128)S(1)}, u32[]{:S(2)}, u32[]{:S(2)}) collective-permute-start(f32[72,256]{1,0:T(8,128)S(1)} %get-tuple-element.102), channel_id=1, source_target_pairs={{0,16},{8,24},{16,0},{24,8},{1,17},{9,25},{17,1},{25,9},{2,18},{10... | collective-permute-start | bytes 221192 | tf_op jit(solution)/shard_map/ppermute | solution.py:357
  57.6 3.3 %collective-permute-start.10 = (f32[9,16,512]{2,1,0:T(8,128)S(1)}, f32[9,16,512]{2,1,0:T(8,128)S(1)}, u32[]{:S(2)}, u32[]{:S(2)}) collective-permute-start(f32[9,16,512]{2,1,0:T(8,128)S(1)} %get-tuple-element.78.second), channel_id=1, source_target_pairs={{0,8},{8,16},{16,24},{1,9},{9,17},{17,25},{2,10},{10,18},{18,26},{... | collective-permute-start | bytes 884744 | tf_op jit(solution)/shard_map/ppermute | solution.py:461
  60.9 1.5 %collective-permute-done.8 = f32[72,256]{1,0:T(8,128)S(1)} collective-permute-done((f32[72,256]{1,0:T(8,128)S(1)}, f32[72,256]{1,0:T(8,128)S(1)}, u32[]{:S(2)}, u32[]{:S(2)}) %collective-permute-start.8) | collective-permute-done | bytes 73760 | tf_op jit(solution)/shard_map/ppermute | solution.py:357
  62.5 2.6 %collective-permute-start.9 = (f32[72,256]{1,0:T(8,128)S(1)}, f32[72,256]{1,0:T(8,128)S(1)}, u32[]{:S(2)}, u32[]{:S(2)}) collective-permute-start(f32[72,256]{1,0:T(8,128)S(1)} %fusion.1), channel_id=1, source_target_pairs={{0,2},{1,3},{2,0},{3,1},{4,6},{5,7},{6,4},{7,5},{8,10},{9,11},{10,... | collective-permute-start | bytes 221192 | tf_op jit(solution)/shard_map/ppermute | solution.py:357
  65.1 1.3 %collective-permute-start.11 = (f32[6,2,512]{2,1,0:T(2,128)S(1)}, f32[6,2,512]{2,1,0:T(2,128)S(1)}, u32[]{:S(2)}, u32[]{:S(2)}) collective-permute-start(f32[6,2,512]{2,1,0:T(2,128)S(1)} %get-tuple-element.79), channel_id=1, source_target_pairs={{0,1},{1,2},{2,3},{3,4},{4,5},{5,6},{6,7},{8,9},{9,10},{10,11},{11... | collective-permute-start | bytes 73736 | tf_op jit(solution)/shard_map/ppermute | solution.py:470
  67.5 5.3 %collective-permute-start.12 = (f32[72,256]{1,0:T(8,128)S(1)}, f32[72,256]{1,0:T(8,128)S(1)}, u32[]{:S(2)}, u32[]{:S(2)}) collective-permute-start(f32[72,256]{1,0:T(8,128)S(1)} %add.54), channel_id=1, source_target_pairs={{0,4},{1,5},{2,6},{3,7},{4,0},{5,1},{6,2},{7,3},{8,12},{9,13},{10,... | collective-permute-start | bytes 221192 | tf_op jit(solution)/shard_map/ppermute | solution.py:357
  72.8 1.3 %collective-permute-start.13 = (f32[6,2,512]{2,1,0:T(2,128)S(1)}, f32[6,2,512]{2,1,0:T(2,128)S(1)}, u32[]{:S(2)}, u32[]{:S(2)}) collective-permute-start(f32[6,2,512]{2,1,0:T(2,128)S(1)} %get-tuple-element.81), channel_id=1, source_target_pairs={{1,0},{2,1},{3,2},{4,3},{5,4},{6,5},{7,6},{9,8},{10,9},{11,10},{12... | collective-permute-start | bytes 73736 | tf_op jit(solution)/shard_map/ppermute | solution.py:476
  74.1 2.4 %collective-permute-done.12 = f32[72,256]{1,0:T(8,128)S(1)} collective-permute-done((f32[72,256]{1,0:T(8,128)S(1)}, f32[72,256]{1,0:T(8,128)S(1)}, u32[]{:S(2)}, u32[]{:S(2)}) %collective-permute-start.12) | collective-permute-done | bytes 73760 | tf_op jit(solution)/shard_map/ppermute | solution.py:357
  77.4 2.6 %collective-permute-start.16 = (f32[72,256]{1,0:T(8,128)S(1)}, f32[72,256]{1,0:T(8,128)S(1)}, u32[]{:S(2)}, u32[]{:S(2)}) collective-permute-start(f32[72,256]{1,0:T(8,128)S(1)} %add.55), channel_id=1, source_target_pairs={{0,24},{8,16},{16,8},{24,0},{1,25},{9,17},{17,9},{25,1},{2,26},{10... | collective-permute-start | bytes 221192 | tf_op jit(solution)/shard_map/ppermute | solution.py:357
  80.1 2.0 %fields.1 = (f32[3,32,512]{2,1,0:T(8,128)}, f32[3,32,512]{2,1,0:T(8,128)}) custom-call(f32[2,4]{1,0:T(2,128)} %table.1, s32[32,512]{1,0:T(8,128)} %bitcast.45, f32[3,32,512]{2,1,0:T(8,128)} %bitcast.40, f32[6,16,512]{2,1,0:T(8,128)S(1)} %get-tuple-element.72.first, f32[9,16,512]{2,1,0:T(8,128)S(1)} %get-tuple-element.78.second, ...), custom_call_target="tpu_custom_call" | custom-call | tf_op jit(solution)/shard_map/fields/pallas_call | solution.py:486
  83.4 1.3 %collective-permute-done.17.other = f32[4,72,256]{2,1,0:T(8,128)S(1)} collective-permute-done((f32[4,72,256]{2,1,0:T(8,128)S(1)}, f32[4,72,256]{2,1,0:T(8,128)S(1)}, u32[]{:S(2)}, u32[]{:S(2)}) %collective-permute-start.17) | collective-permute-done | bytes 294944 | tf_op jit(solution)/shard_map/ppermute | solution.py:357
  84.7 1.6 %finish.1 = (f32[10,256]{1,0:T(8,128)}, f32[1,256]{1,0:T(1,128)}, f32[512,256]{1,0:T(8,128)}, f32[2,256]{1,0:T(2,128)}, f32[9,256]{1,0:T(8,128)}, /*index=5*/f32[1,9]{1,0:T(1,128)}) custom-call(s32[2]{0:T(128)S(1)} %pad_add_fusion.place, f32[4,72,256]{2,1,0:T(8,128)S(1)} %pad_maximum_fusion.mine, f32[4,72,256]{2,1,0:T(8,128)S(1)} %collective-permute-done.17.other), custom_call_target="tpu_custom_call" | custom-call | tf_op jit(solution)/shard_map/finish/pallas_call | solution.py:512
  (25 shorter events, 4.0 us)
Async XLA Ops:
  1.9 11.1 %collective-permute-start.3 = (f32[6,16,512]{2,1,0:T(8,128)S(1)}, f32[6,16,512]{2,1,0:T(8,128)S(1)}, u32[]{:S(2)}, u32[]{:S(2)}) collective-permute-start(f32[6,16,512]{2,1,0:T(8,128)S(1)} %get-tuple-element.57), channel_id=1, source_target_pairs={{0,8},{8,16},{16,24},{1,9},{9,17},{17,25},{2,10},{10,18},{18,26},{... | collective-permute-start | bytes 589832 | tf_op jit(solution)/shard_map/ppermute | solution.py:401
  6.8 4.7 %collective-permute-start.1 = (f32[9,2,512]{2,1,0:T(2,128)S(1)}, f32[9,2,512]{2,1,0:T(2,128)S(1)}, u32[]{:S(2)}, u32[]{:S(2)}) collective-permute-start(f32[9,2,512]{2,1,0:T(2,128)S(1)} %get-tuple-element.55), channel_id=1, source_target_pairs={{0,1},{1,2},{2,3},{3,4},{4,5},{5,6},{6,7},{8,9},{9,10},{10,11},{11... | collective-permute-start | bytes 110600 | tf_op jit(solution)/shard_map/ppermute | solution.py:402
  8.3 4.7 %collective-permute-start.2 = (f32[9,2,512]{2,1,0:T(2,128)S(1)}, f32[9,2,512]{2,1,0:T(2,128)S(1)}, u32[]{:S(2)}, u32[]{:S(2)}) collective-permute-start(f32[9,2,512]{2,1,0:T(2,128)S(1)} %get-tuple-element.56), channel_id=1, source_target_pairs={{1,0},{2,1},{3,2},{4,3},{5,4},{6,5},{7,6},{9,8},{10,9},{11,10},{12... | collective-permute-start | bytes 110600 | tf_op jit(solution)/shard_map/ppermute | solution.py:403
  9.6 22.1 %collective-permute-start = (f32[9,16,512]{2,1,0:T(8,128)S(1)}, f32[9,16,512]{2,1,0:T(8,128)S(1)}, u32[]{:S(2)}, u32[]{:S(2)}) collective-permute-start(f32[9,16,512]{2,1,0:T(8,128)S(1)} %get-tuple-element.54), channel_id=1, source_target_pairs={{8,0},{16,8},{24,16},{9,1},{17,9},{25,17},{10,2},{18,10},{26,18},{... | collective-permute-start | bytes 884744 | tf_op jit(solution)/shard_map/ppermute | solution.py:404
  30.1 18.6 %collective-permute-start.4 = (f32[6,16,512]{2,1,0:T(8,128)S(1)}, f32[6,16,512]{2,1,0:T(8,128)S(1)}, u32[]{:S(2)}, u32[]{:S(2)}) collective-permute-start(f32[6,16,512]{2,1,0:T(8,128)S(1)} %get-tuple-element.72.first), channel_id=1, source_target_pairs={{8,0},{16,8},{24,16},{9,1},{17,9},{25,17},{10,2},{18,10},{26,18},{... | collective-permute-start | bytes 589832 | tf_op jit(solution)/shard_map/ppermute | solution.py:459
  48.7 4.2 %collective-permute-start.5 = (f32[4,72,256]{2,1,0:T(8,128)S(1)}, f32[4,72,256]{2,1,0:T(8,128)S(1)}, u32[]{:S(2)}, u32[]{:S(2)}) collective-permute-start(f32[4,72,256]{2,1,0:T(8,128)S(1)} %dynamic-slice_bitcast_fusion), channel_id=1, source_target_pairs={{0,1},{1,0},{2,3},{3,2},{4,5},{5,4},{6,7},{7,6},{8,9},{9,8},{10,11... | collective-permute-start | bytes 884744 | tf_op jit(solution)/shard_map/ppermute | solution.py:357
  53.1 7.9 %collective-permute-start.6 = (f32[72,256]{1,0:T(8,128)S(1)}, f32[72,256]{1,0:T(8,128)S(1)}, u32[]{:S(2)}, u32[]{:S(2)}) collective-permute-start(f32[72,256]{1,0:T(8,128)S(1)} %get-tuple-element.100), channel_id=1, source_target_pairs={{0,8},{8,0},{16,24},{24,16},{1,9},{9,1},{17,25},{25,17},{2,10},{10... | collective-permute-start | bytes 221192 | tf_op jit(solution)/shard_map/ppermute | solution.py:357
  55.5 5.4 %collective-permute-start.7 = (f32[72,256]{1,0:T(8,128)S(1)}, f32[72,256]{1,0:T(8,128)S(1)}, u32[]{:S(2)}, u32[]{:S(2)}) collective-permute-start(f32[72,256]{1,0:T(8,128)S(1)} %get-tuple-element.102), channel_id=1, source_target_pairs={{0,16},{8,24},{16,0},{24,8},{1,17},{9,25},{17,1},{25,9},{2,18},{10... | collective-permute-start | bytes 221192 | tf_op jit(solution)/shard_map/ppermute | solution.py:357
  57.2 5.3 %collective-permute-start.8 = (f32[72,256]{1,0:T(8,128)S(1)}, f32[72,256]{1,0:T(8,128)S(1)}, u32[]{:S(2)}, u32[]{:S(2)}) collective-permute-start(f32[72,256]{1,0:T(8,128)S(1)} %get-tuple-element.101), channel_id=1, source_target_pairs={{0,24},{8,16},{16,8},{24,0},{1,25},{9,17},{17,9},{25,1},{2,26},{10... | collective-permute-start | bytes 221192 | tf_op jit(solution)/shard_map/ppermute | solution.py:357
  57.6 9.8 %collective-permute-start.10 = (f32[9,16,512]{2,1,0:T(8,128)S(1)}, f32[9,16,512]{2,1,0:T(8,128)S(1)}, u32[]{:S(2)}, u32[]{:S(2)}) collective-permute-start(f32[9,16,512]{2,1,0:T(8,128)S(1)} %get-tuple-element.78.second), channel_id=1, source_target_pairs={{0,8},{8,16},{16,24},{1,9},{9,17},{17,25},{2,10},{10,18},{18,26},{... | collective-permute-start | bytes 884744 | tf_op jit(solution)/shard_map/ppermute | solution.py:461
  62.5 4.9 %collective-permute-start.9 = (f32[72,256]{1,0:T(8,128)S(1)}, f32[72,256]{1,0:T(8,128)S(1)}, u32[]{:S(2)}, u32[]{:S(2)}) collective-permute-start(f32[72,256]{1,0:T(8,128)S(1)} %fusion.1), channel_id=1, source_target_pairs={{0,2},{1,3},{2,0},{3,1},{4,6},{5,7},{6,4},{7,5},{8,10},{9,11},{10,... | collective-permute-start | bytes 221192 | tf_op jit(solution)/shard_map/ppermute | solution.py:357
  65.1 2.4 %collective-permute-start.11 = (f32[6,2,512]{2,1,0:T(2,128)S(1)}, f32[6,2,512]{2,1,0:T(2,128)S(1)}, u32[]{:S(2)}, u32[]{:S(2)}) collective-permute-start(f32[6,2,512]{2,1,0:T(2,128)S(1)} %get-tuple-element.79), channel_id=1, source_target_pairs={{0,1},{1,2},{2,3},{3,4},{4,5},{5,6},{6,7},{8,9},{9,10},{10,11},{11... | collective-permute-start | bytes 73736 | tf_op jit(solution)/shard_map/ppermute | solution.py:470
  67.5 9.0 %collective-permute-start.12 = (f32[72,256]{1,0:T(8,128)S(1)}, f32[72,256]{1,0:T(8,128)S(1)}, u32[]{:S(2)}, u32[]{:S(2)}) collective-permute-start(f32[72,256]{1,0:T(8,128)S(1)} %add.54), channel_id=1, source_target_pairs={{0,4},{1,5},{2,6},{3,7},{4,0},{5,1},{6,2},{7,3},{8,12},{9,13},{10,... | collective-permute-start | bytes 221192 | tf_op jit(solution)/shard_map/ppermute | solution.py:357
  72.8 3.7 %collective-permute-start.13 = (f32[6,2,512]{2,1,0:T(2,128)S(1)}, f32[6,2,512]{2,1,0:T(2,128)S(1)}, u32[]{:S(2)}, u32[]{:S(2)}) collective-permute-start(f32[6,2,512]{2,1,0:T(2,128)S(1)} %get-tuple-element.81), channel_id=1, source_target_pairs={{1,0},{2,1},{3,2},{4,3},{5,4},{6,5},{7,6},{9,8},{10,9},{11,10},{12... | collective-permute-start | bytes 73736 | tf_op jit(solution)/shard_map/ppermute | solution.py:476
  76.5 5.5 %collective-permute-start.14 = (f32[72,256]{1,0:T(8,128)S(1)}, f32[72,256]{1,0:T(8,128)S(1)}, u32[]{:S(2)}, u32[]{:S(2)}) collective-permute-start(f32[72,256]{1,0:T(8,128)S(1)} %add.55), channel_id=1, source_target_pairs={{0,8},{8,0},{16,24},{24,16},{1,9},{9,1},{17,25},{25,17},{2,10},{10... | collective-permute-start | bytes 221192 | tf_op jit(solution)/shard_map/ppermute | solution.py:357
  77.1 4.9 %collective-permute-start.15 = (f32[72,256]{1,0:T(8,128)S(1)}, f32[72,256]{1,0:T(8,128)S(1)}, u32[]{:S(2)}, u32[]{:S(2)}) collective-permute-start(f32[72,256]{1,0:T(8,128)S(1)} %add.55), channel_id=1, source_target_pairs={{0,16},{8,24},{16,0},{24,8},{1,17},{9,25},{17,1},{25,9},{2,18},{10... | collective-permute-start | bytes 221192 | tf_op jit(solution)/shard_map/ppermute | solution.py:357
  77.4 5.6 %collective-permute-start.16 = (f32[72,256]{1,0:T(8,128)S(1)}, f32[72,256]{1,0:T(8,128)S(1)}, u32[]{:S(2)}, u32[]{:S(2)}) collective-permute-start(f32[72,256]{1,0:T(8,128)S(1)} %add.55), channel_id=1, source_target_pairs={{0,24},{8,16},{16,8},{24,0},{1,25},{9,17},{17,9},{25,1},{2,26},{10... | collective-permute-start | bytes 221192 | tf_op jit(solution)/shard_map/ppermute | solution.py:357
  83.1 1.6 %collective-permute-start.17 = (f32[4,72,256]{2,1,0:T(8,128)S(1)}, f32[4,72,256]{2,1,0:T(8,128)S(1)}, u32[]{:S(2)}, u32[]{:S(2)}) collective-permute-start(f32[4,72,256]{2,1,0:T(8,128)S(1)} %pad_maximum_fusion.mine), channel_id=1, source_target_pairs={{0,1},{1,0},{2,3},{3,2},{4,5},{5,4},{6,7},{7,6},{8,9},{9,8},{10,11... | collective-permute-start | bytes 884744 | tf_op jit(solution)/shard_map/ppermute | solution.py:357

commit v4 on v3

--- a/solution.py
+++ b/solution.py
@@ -48,28 +48,16 @@
     return occupied, pick(table, 1, material)
 
 
-def x_ends(field, low, high, rows):
+def near_first():
+    near = 1 - lax.rem(lax.axis_index("gx"), 2)
+    return near, lax.rem(lax.axis_index("gy"), 2)
+
+
+def y_ends(field, low, high, rows):
+    where = lax.broadcasted_iota(jnp.int32, field.shape, 0)
     return (
-        jnp.concatenate([low, field[:-rows]], 0),
-        jnp.concatenate([field[rows:], high], 0),
-    )
-
-
-def y_ends(field, low, high, rows):
-    planes = field.shape[0] // rows
-    where = lax.broadcasted_iota(jnp.int32, field.shape, 0)
-
-    def spread(edge):
-        return jnp.concatenate(
-            [jnp.broadcast_to(edge[p : p + 1], (rows, field.shape[1])) for p in range(planes)], 0
-        )
-
-    before, after = pltpu.roll(field, 1, 0), pltpu.roll(field, field.shape[0] - 1, 0)
-    low = 0.0 if low is None else spread(low)
-    high = 0.0 if high is None else spread(high)
-    return (
-        jnp.where(where % rows == 0, low, before),
-        jnp.where(where % rows == rows - 1, high, after),
+        jnp.where(where == 0, low, pltpu.roll(field, 1, 0)),
+        jnp.where(where == rows - 1, high, pltpu.roll(field, rows - 1, 0)),
     )
 
 
@@ -87,34 +75,45 @@
 
 
 def faces_kernel(rows, *refs):
-    sources, (xf, xb, yf, yb), targets, sems = refs[:5], refs[5:9], refs[9:14], refs[14]
-    for copy in fetch(sources, targets, sems):
+    sources, outs, targets, sems = refs[:5], refs[5:9], refs[9:14], refs[14]
+    copies = fetch(sources, targets, sems)
+    near, side = near_first()
+    for copy in copies:
         copy.wait()
+    x_pair, x_next, y_pair, y_next = outs
     table, material, displacement, velocity, cotangent = targets
-    occupied, density = step_factor(table, material[...])
-    for i in range(3):
-        carried = time_step * occupied * cotangent[i] / density
-        for slot, field in ((i, displacement[i]), (3 + i, carried), (6 + i, velocity[i])):
-            if slot < 6:
-                xf[slot] = field[rows:]
-            xb[slot] = field[:rows]
-            for p in range(2):
-                yf[slot, p : p + 1] = field[(p + 1) * rows - 1 : (p + 1) * rows]
-                yb[slot, p : p + 1] = field[p * rows : p * rows + 1]
-
-
-def network_kernel(plane, rows, block, *refs):
-    sources, refs = refs[: 12 - plane * 3], refs[12 - plane * 3 :]
-    (edge, yl, yh), refs = refs[:3], refs[3:]
-    if plane:
-        (yf_first, yb_first), given, refs = refs[:2], refs[2:13], refs[13:]
-        (sx, yf, yb, rest, grads), refs = refs[:5], refs[5:]
+    for k, plane in enumerate((near, 1 - near)):
+        own = pl.ds(pl.multiple_of(plane * rows, rows), rows)
+        occupied, density = step_factor(table, material[own])
+        for i in range(3):
+            carried = time_step * occupied * cotangent[i, own] / density
+            moving = velocity[i, own]
+            for slot, field in ((i, displacement[i, own]), (3 + i, carried), (6 + i, moving)):
+                if k:
+                    x_next[slot] = field
+                elif slot < 6:
+                    x_pair[slot] = field
+                y_pair[slot, k : k + 1] = jnp.where(side == 0, field[rows - 1 :], field[:1])
+                y_next[slot, k : k + 1] = jnp.where(side == 0, field[:1], field[rows - 1 :])
+
+
+def low_high(side, pair, following):
+    return jnp.where(side == 0, following, pair), jnp.where(side == 0, pair, following)
+
+
+def network_kernel(order, rows, block, *refs):
+    sources, refs = refs[: 13 - order * 5], refs[13 - order * 5 :]
+    (edge, y_pair, y_next), refs = refs[:3], refs[3:]
+    if order:
+        faces_first, given, refs = refs[:2], refs[2:13], refs[13:]
+        (sx, s_pair, s_next, rest, grads), refs = refs[:5], refs[5:]
     else:
-        (sx, yf, yb, rest), kept, refs = refs[:4], refs[4:15], refs[15:]
+        (sx, s_pair, s_next, rest), kept, refs = refs[:4], refs[4:15], refs[15:]
     targets, sems, refs = refs[: len(sources)], refs[len(sources)], refs[len(sources) + 1 :]
     grid_in, grid_delta, feats, delta, net, back, wide, *refs = refs
     copies = fetch(sources, targets, sems)
-    if plane:
+    near, side = near_first()
+    if order:
         acc_mid, acc_in, acc_out, acc_b, acc_bo = refs
         win, winT, wmidT, wout, woutT, bias = given[5:]
         for ref, source in zip(refs, given[:5]):
@@ -130,12 +129,14 @@
     lanes = material.shape[1]
     tiles = lanes // 128
     voxels = rows * lanes
-    own = slice(plane * rows, (plane + 1) * rows)
-    occupied, density = step_factor(table, material[...])
-    strength = (occupied * pick(table, 0, material[...]))[own]
-
-    if not plane:
-        w_inT, b_in, b_mid, w_out = targets[8:]
+    plane = 1 - near if order else near
+    own = pl.ds(pl.multiple_of(plane * rows, rows), rows)
+    across = pl.ds(pl.multiple_of((1 - plane) * rows, rows), rows)
+    occupied, _ = step_factor(table, material[own])
+    strength = occupied * pick(table, 0, material[own])
+
+    if not order:
+        w_inT, b_in, b_mid, w_out = targets[8:12]
         wide[...] = jnp.zeros_like(wide)
         wide[:FEAT] = w_inT[...].astype(f32)
         winT[...] = wide[:16].astype(bf16)
@@ -153,17 +154,26 @@
         for t in range(tiles):
             ref[t, slot * rows : (slot + 1) * rows] = field[:, t * 128 : (t + 1) * 128]
 
-    def strains(field, slot):
-        mine = field[own]
-        ends = (field[:rows], edge[slot]) if plane else (edge[slot], field[rows:])
-        low, high = yl[slot, plane : plane + 1], yh[slot, plane : plane + 1]
-        return half_diff(ends), half_diff(y_ends(mine, low, high, rows)), half_diff(z_ends(mine))
-
-    factor = time_step * occupied
+    uphill = jnp.where(plane == 0, 0.5, -0.5)
+
+    def strains(mine, other, slot):
+        low, high = low_high(
+            side, y_pair[slot, order : order + 1], y_next[slot, order : order + 1]
+        )
+        return (
+            (other - edge[slot]) * uphill,
+            half_diff(y_ends(mine, low, high, rows)),
+            half_diff(z_ends(mine)),
+        )
+
+    def carried(rows_of, slot):
+        full, thick = step_factor(table, material[rows_of])
+        return time_step * full * cotangent[slot, rows_of] / thick
+
     for i in range(3):
-        for j, value in enumerate(strains(displacement[i], i)):
+        for j, value in enumerate(strains(displacement[i, own], displacement[i, across], i)):
             put(grid_in, 3 * i + j, value)
-        for j, value in enumerate(strains(factor * cotangent[i] / density, 3 + i)):
+        for j, value in enumerate(strains(carried(own, i), carried(across, i), 3 + i)):
             put(grid_delta, 3 * i + j, strength * -value)
     put(grid_in, 9, jnp.sin(two_pi * phase[own].astype(f32) / PHASES + clock[0]))
     put(grid_in, 10, jnp.ones((rows, lanes), f32))
@@ -238,18 +248,19 @@
                 along = [scale * item for item in along]
             slot = base + i
             sx[slot] = along[0]
-            yf[slot, plane : plane + 1] = along[1][rows - 1 :]
-            yb[slot, plane : plane + 1] = along[1][:1]
-            if plane:
-                yf[slot, 0:1] = yf_first[slot, 0:1]
-                yb[slot, 0:1] = yb_first[slot, 0:1]
-            rest[slot] = half_diff(y_ends(along[1], None, None, rows)) + half_diff(
+            first, last = along[1][:1], along[1][rows - 1 :]
+            s_pair[slot, order : order + 1] = jnp.where(side == 0, last, first)
+            s_next[slot, order : order + 1] = jnp.where(side == 0, first, last)
+            if order:
+                s_pair[slot, 0:1] = faces_first[0][slot, 0:1]
+                s_next[slot, 0:1] = faces_first[1][slot, 0:1]
+            rest[slot] = half_diff(y_ends(along[1], 0.0, 0.0, rows)) + half_diff(
                 z_ends(along[2])
             )
-    if not plane:
+    if not order:
+        for i in range(3):
+            sx[6 + i] = targets[12][i, own]
         return
-    for i in range(3):
-        sx[6 + i] = targets[8][i, own]
 
     chunks = grads.shape[0]
     part = 2 * HID // chunks
@@ -272,60 +283,54 @@
     table,
     material,
     velocity,
-    first,
-    second,
-    rest_first,
-    rest_second,
-    xh,
-    yl,
-    yh,
-    sxl,
-    sxh,
-    syl,
-    syh,
+    stress_near,
+    stress_far,
+    rest_near,
+    rest_far,
+    x_next,
+    y_pair,
+    y_next,
+    sx_pair,
+    sx_next,
+    sy_pair,
+    sy_next,
     velocity_new,
     displacement_grad,
 ):
-    size, lanes = material.shape
-    occupied, density = step_factor(table, material[...])
-    where = lax.broadcasted_iota(jnp.int32, (size, lanes), 0)
-
-    def spread(edge):
-        return jnp.concatenate(
-            [jnp.broadcast_to(edge[p : p + 1], (rows, lanes)) for p in range(2)], 0
-        )
-
-    def total(slot):
-        value = jnp.concatenate(
-            [
-                rest_first[slot] + half_diff((sxl[slot], second[slot])),
-                rest_second[slot] + half_diff((first[slot], sxh[slot])),
-            ],
-            0,
-        )
-        value = value - jnp.where(where % rows == 0, spread(syl[slot]) * 0.5, 0.0)
-        return value + jnp.where(where % rows == rows - 1, spread(syh[slot]) * 0.5, 0.0)
-
-    for i in range(3):
-        value = velocity[i]
-        around = -6.0 * value
-        for low, high in (
-            x_ends(value, sxl[6 + i], xh[6 + i], rows),
-            y_ends(value, yl[6 + i], yh[6 + i], rows),
-            z_ends(value),
-        ):
-            around = around + high + low
-        pull = total(i) + viscosity * around
-        velocity_new[i] = value + time_step * occupied * pull / density
-        displacement_grad[i] = -total(3 + i)
-
-
-def finish_kernel(place, mine, other, g_in, gb_in, g_mid, gb_mid, g_out, gb_out, small):
+    near, side = near_first()
+    lanes = material.shape[1]
+    where = lax.broadcasted_iota(jnp.int32, (rows, lanes), 0)
+    for k, plane in enumerate((near, 1 - near)):
+        own = pl.ds(pl.multiple_of(plane * rows, rows), rows)
+        across = pl.ds(pl.multiple_of((1 - plane) * rows, rows), rows)
+        occupied, density = step_factor(table, material[own])
+        uphill = jnp.where(plane == 0, 0.5, -0.5)
+        other, edge = (stress_near, sx_next) if k else (stress_far, sx_pair)
+        moving, rest = (x_next, rest_far) if k else (sx_pair, rest_near)
+
+        def total(slot):
+            low, high = low_high(side, sy_pair[slot, k : k + 1], sy_next[slot, k : k + 1])
+            value = rest[slot] + (other[slot] - edge[slot]) * uphill
+            value = value - jnp.where(where == 0, low * 0.5, 0.0)
+            return value + jnp.where(where == rows - 1, high * 0.5, 0.0)
+
+        for i in range(3):
+            value = velocity[i, own]
+            low, high = low_high(side, y_pair[6 + i, k : k + 1], y_next[6 + i, k : k + 1])
+            around = velocity[i, across] + moving[6 + i] - 6.0 * value
+            for ends in (y_ends(value, low, high, rows), z_ends(value)):
+                around = around + ends[0] + ends[1]
+            pull = total(i) + viscosity * around
+            velocity_new[i, own] = value + time_step * occupied * pull / density
+            displacement_grad[i, own] = -total(3 + i)
+
+
+def finish_kernel(mine, other, g_in, gb_in, g_mid, gb_mid, g_out, gb_out, small):
     count, height, _ = mine.shape
     part = height - SMALL
     total = jnp.sum(jnp.square(mine[...])) + jnp.sum(jnp.square(other[...]))
     scale = lax.rsqrt(jnp.full((1, 1), total, f32) / NPARAM + norm_eps)
-    half, index = place[0], place[1]
+    half, index = lax.rem(lax.axis_index("gy"), 2), lax.axis_index("gx")
     for m in range(count):
         for ref, side in ((mine, half), (other, 1 - half)):
             chunk = side * count + (index ^ m)
@@ -348,9 +353,11 @@
     return pltpu.with_memory_space_constraint(value, pltpu.HBM)
 
 
-def along(axis, step):
-    count = lax.axis_size(axis)
-    return [(i, i + step) for i in range(count) if 0 <= i + step < count]
+def swap_next(value, axis):
+    inner = lax.axis_size(axis) - 1
+    return lax.ppermute(
+        value, axis, [(i, i + 1 if i % 2 else i - 1) for i in range(1, inner)]
+    )
 
 
 def swap(value, axis, mask):
@@ -377,7 +384,7 @@
     nx, ny = lax.axis_size("gx"), lax.axis_size("gy")
     chunks = 2 * nx
     part = 2 * HID // chunks
-    assert planes == 2 and chunks >= GROUPS and ny % 2 == 0 and part % 8 == 0
+    assert planes == 2 and chunks >= GROUPS and nx % 2 == ny % 2 == 0 and part % 8 == 0
     material = material.reshape(size, lanes)
     phase = phase.reshape(size, lanes)
     displacement = displacement.reshape(3, size, lanes)
@@ -398,10 +405,10 @@
         compiler_params=pltpu.CompilerParams(vmem_limit_bytes=6 << 20),
         name="faces",
     )(*map(stay, (material_table, material, displacement, velocity, cotangent)))
-    xl = lax.ppermute(faces[0], "gx", along("gx", 1))
-    yl = lax.ppermute(faces[2], "gy", along("gy", 1))
-    yh = lax.ppermute(faces[3], "gy", along("gy", -1))
-    xh = lax.ppermute(faces[1], "gx", along("gx", -1))
+    x_pair = swap(faces[0], "gx", 1)
+    y_pair = swap(faces[2], "gy", 1)
+    y_next = swap_next(faces[3], "gy")
+    x_next = swap_next(faces[1], "gx")
 
     voxels = rows * lanes
     block = 4096
@@ -421,14 +428,14 @@
         ((3, HID, 128), f32),
     ]
 
-    def network(plane, sources, near):
+    def network(order, sources, near):
         outs = [jax.ShapeDtypeStruct(*item) for item in handed]
-        if plane:
+        if order:
             outs = shapes((chunks, part + SMALL, HID))
         return pl.pallas_call(
-            functools.partial(network_kernel, plane, rows, block),
+            functools.partial(network_kernel, order, rows, block),
             out_shape=shapes(
-                (6 + 3 * plane, rows, lanes), *[(6, 1 + plane, lanes)] * 2, (6, rows, lanes)
+                (9 - 3 * order, rows, lanes), *[(6, 1 + order, lanes)] * 2, (6, rows, lanes)
             )
             + outs,
             in_specs=[HBM] * len(sources) + [VMEM] * len(near),
@@ -441,7 +448,7 @@
                 *[pltpu.VMEM((16, voxels), bf16)] * 2,
                 *[pltpu.VMEM((16, voxels), f32)] * 2,
                 pltpu.VMEM((128, HID), f32),
-                *[pltpu.VMEM(*item) for item in handed[: 5 * plane]],
+                *[pltpu.VMEM(*item) for item in handed[: 5 * order]],
             ],
             compiler_params=pltpu.CompilerParams(vmem_limit_bytes=36 << 20),
             cost_estimate=pl.CostEstimate(
@@ -454,33 +461,35 @@
 
     common = [material_table, clock, b_out, material, phase, displacement, cotangent, w_mid]
     first = network(
-        0, common + [w_in.T, b_in.reshape(1, HID), b_mid, w_out], [xl, yl, yh]
-    )
-    sxh = lax.ppermute(first[0], "gx", along("gx", -1))
-    second = network(1, common + [velocity], [xh, yl, yh, *first[1:3], *first[4:]])
-    sxl = lax.ppermute(second[0], "gx", along("gx", 1))
+        0,
+        common + [w_in.T, b_in.reshape(1, HID), b_mid, w_out, velocity],
+        [x_pair, y_pair, y_next],
+    )
+    sx_pair = swap(first[0], "gx", 1)
+    second = network(1, common, [x_next, y_pair, y_next, *first[1:3], *first[4:]])
+    sx_next = swap_next(second[0], "gx")
 
     half = lax.axis_index("gy") % 2
     index = lax.axis_index("gx")
-    pile, sxh = lax.optimization_barrier((second[4], sxh))
+    pile, sx_pair = lax.optimization_barrier((second[4], sx_pair))
     pile = pile.reshape(2, nx, part + SMALL, HID)
     kept = lax.dynamic_index_in_dim(pile, half, 0, keepdims=False)
     sent = lax.dynamic_index_in_dim(pile, 1 - half, 0, keepdims=False)
-    kept, face = lax.optimization_barrier((kept + swap(sent, "gy", 1), second[1]))
-    syl = lax.ppermute(face, "gy", along("gy", 1))
+    kept, face = lax.optimization_barrier((kept + swap(sent, "gy", 1), second[2]))
+    sy_next = swap_next(face, "gy")
     share = lax.dynamic_index_in_dim(kept, index, 0, keepdims=False)
     for m in range(1, nx):
         piece = lax.dynamic_index_in_dim(kept, index ^ m, 0, keepdims=False)
         share = share + swap(piece, "gx", m)
-    share, face = lax.optimization_barrier((share, second[2]))
-    syh = lax.ppermute(face, "gy", along("gy", -1))
+    share, face = lax.optimization_barrier((share, second[1]))
+    sy_pair = swap(face, "gy", 1)
     mask = 2
     while mask < ny:
         share = share + swap(share, "gy", mask)
         if mask == 2:
-            share, sxl, syl = lax.optimization_barrier((share, sxl, syl))
+            share, sx_next, sy_next = lax.optimization_barrier((share, sx_next, sy_next))
         mask *= 2
-    share, syh = lax.optimization_barrier((share, syh))
+    share, sy_pair = lax.optimization_barrier((share, sy_pair))
     mine = jnp.stack([share] + [swap(share, "gx", m) for m in range(1, nx)])
 
     fields = pl.pallas_call(
@@ -498,26 +507,25 @@
         second[0],
         first[3],
         second[3],
-        xh,
-        yl,
-        yh,
-        sxl,
-        sxh,
-        syl,
-        syh,
+        x_next,
+        y_pair,
+        y_next,
+        sx_pair,
+        sx_next,
+        sy_pair,
+        sy_next,
     )
     mine, *fields = lax.optimization_barrier((mine, *fields))
     other = swap(mine, "gy", 1)
-    place = jnp.stack([half, index]).astype(jnp.int32)
     done = pl.pallas_call(
         finish_kernel,
         out_shape=shapes((FEAT, HID), (1, HID), (2 * HID, HID), (2, HID), (OUT, HID), (1, OUT)),
-        in_specs=[SMEM] + [VMEM] * 2,
+        in_specs=[VMEM] * 2,
         out_specs=[VMEM] * 6,
         scratch_shapes=[pltpu.VMEM((chunks * SMALL, HID), f32)],
         compiler_params=pltpu.CompilerParams(vmem_limit_bytes=6 << 20),
         name="finish",
-    )(place, mine, other)
+    )(mine, other)
     shape = (3, planes, rows, lanes)
     return (
         fields[0].reshape(shape),

time: 86.7 us -> 80.3 us (0.926)
  starting transfers between devices: 35.6 us -> 23.1 us
  waiting for transfers between devices: 9.99 us -> 16.6 us
    ppermute x8 -> x4, starting transfers between devices: 16.2 us -> 2.64 us  [swap_next(): lax.ppermute(value, axis, [(i, i + 1 if i % 2 else i - 1) for i in range(...]
    ppermute x10 -> x14, waiting for transfers between devices: 8.5 us -> 16.6 us  [swap(): lax.ppermute(value, axis, [(i, i ^ mask) for i in range(lax.axis_size(axi...]
    ppermute x8 -> x4, waiting for transfers between devices: 1.49 us -> 0.01 us  [swap_next(): lax.ppermute(value, axis, [(i, i + 1 if i % 2 else i - 1) for i in range(...]
    ppermute x10 -> x14, starting transfers between devices: 19.3 us -> 20.5 us  [swap(): lax.ppermute(value, axis, [(i, i ^ mask) for i in range(lax.axis_size(axi...]
  transfers between devices with their start and end apart: 18 -> 18, of which waited for: 7 -> 10; matrix products, arithmetic and copies ran while one was open for 0% -> 0% of each run, Pallas kernels for 42% -> 45%
where the time goes in v4:
time: 80.3 us; the launch traced here: 80 us
  Pallas kernels  38.6 us (48%)
  starting transfers between devices  23.1 us (29%)
  waiting for transfers between devices  16.6 us (21%)
  between operations  1.44 us (2%)
    pallas_call x2, Pallas kernels, network(): pl.pallas_call(functools.partial(network_kernel, order, rows, block), out...  34.3 us
    ppermute x14, starting transfers between devices, swap(): lax.ppermute(value, axis, [(i, i ^ mask) for i in range(lax.axis_size(axi...  20.5 us
    ppermute x14, waiting for transfers between devices, swap(): lax.ppermute(value, axis, [(i, i ^ mask) for i in range(lax.axis_size(axi...  16.6 us
    ppermute x4, starting transfers between devices, swap_next(): lax.ppermute(value, axis, [(i, i + 1 if i % 2 else i - 1) for i in range(...  2.64 us
    pallas_call x1, Pallas kernels, body(): pl.pallas_call(functools.partial(fields_kernel, rows), out_shape=shapes(*...  1.94 us
  transfers between devices with their start and end apart: 18, of which 10 were waited for; matrix products, arithmetic and copies ran while one was open for 0% of the time, Pallas kernels for 45%

profile of v4, /device:TPU:0, one launch (start us, length us, event | category | flops | bytes accessed | tf_op | source)
XLA Modules:
  0.0 80.0 jit_solution(1408221406033989387)
XLA Ops:
  0.6 1.3 %faces.1 = (f32[6,16,512]{2,1,0:T(8,128)S(1)}, f32[9,16,512]{2,1,0:T(8,128)S(1)}, f32[9,2,512]{2,1,0:T(2,128)S(1)}, f32[9,2,512]{2,1,0:T(2,128)S(1)}) custom-call(f32[2,4]{1,0:T(2,128)} %table.1, s32[32,512]{1,0:T(8,128)} %bitcast.40, f32[3,32,512]{2,1,0:T(8,128)} %bitcast.44, f32[3,32,512]{2,1,0:T(8,128)} %bitcast.36, f32[3,32,512]{2,1,0:T(8,128)} %bitcast.47), custom_call_target="tpu_custom_call" | custom-call | tf_op jit(solution)/shard_map/faces/pallas_call | solution.py:394
  2.0 3.0 %collective-permute-start.3 = (f32[6,16,512]{2,1,0:T(8,128)S(1)}, f32[6,16,512]{2,1,0:T(8,128)S(1)}, u32[]{:S(2)}, u32[]{:S(2)}) collective-permute-start(f32[6,16,512]{2,1,0:T(8,128)S(1)} %get-tuple-element.57), channel_id=1, source_target_pairs={{0,8},{8,0},{16,24},{24,16},{1,9},{9,1},{17,25},{25,17},{2,10},{10... | collective-permute-start | bytes 589832 | tf_op jit(solution)/shard_map/ppermute | solution.py:364
  5.6 0.7 collective-permute-start
  7.0 2.9 %collective-permute-done.3.refs_13_ = f32[6,16,512]{2,1,0:T(8,128)S(1)} collective-permute-done((f32[6,16,512]{2,1,0:T(8,128)S(1)}, f32[6,16,512]{2,1,0:T(8,128)S(1)}, u32[]{:S(2)}, u32[]{:S(2)}) %collective-permute-start.3) | collective-permute-done | bytes 196640 | tf_op jit(solution)/shard_map/ppermute | solution.py:364
  9.9 17.2 %network.2 = (f32[9,16,512]{2,1,0:T(8,128)S(1)}, f32[6,1,512]{2,1,0:T(1,128)S(1)}, f32[6,1,512]{2,1,0:T(1,128)S(1)}, f32[6,16,512]{2,1,0:T(8,128)S(1)}, f32[512,...) custom-call(f32[2,4]{1,0:T(2,128)} %table.1, ...), custom_call_target="tpu_custom_call" | custom-call | flops 6681526272 | bytes 524288 | tf_op jit(solution)/shard_map/network/pallas_call | solution.py:435
  27.1 1.8 %collective-permute-start.4 = (f32[9,16,512]{2,1,0:T(8,128)S(1)}, f32[9,16,512]{2,1,0:T(8,128)S(1)}, u32[]{:S(2)}, u32[]{:S(2)}) collective-permute-start(f32[9,16,512]{2,1,0:T(8,128)S(1)} %get-tuple-element.72.stress_near), channel_id=1, source_target_pairs={{0,8},{8,0},{16,24},{24,16},{1,9},{9,1},{17,25},{25,17},{2,10},{10... | collective-permute-start | bytes 884744 | tf_op jit(solution)/shard_map/ppermute | solution.py:364
  28.9 17.1 %network.3 = (f32[6,16,512]{2,1,0:T(8,128)S(1)}, f32[6,2,512]{2,1,0:T(2,128)S(1)}, f32[6,2,512]{2,1,0:T(2,128)S(1)}, f32[6,16,512]{2,1,0:T(8,128)S(1)}, f32[8,72,256]{2,1,0:T(8,128)S(1)}) custom-call(f32[2,4]{1,0:T(2,128)} %table.1, f32[1]{0:T(128)S(6)} %copy.21.refs_1_, f32[9]{0:T(128)} %refs_2_.3, s32[32,512]{1,0:T(8,128)} %bitcast.42, ...), custom_call_target="tpu_custom_call" | custom-call | flops 6681526272 | bytes 524288 | tf_op jit(solution)/shard_map/network/pallas_call | solution.py:435
  46.0 2.1 %collective-permute-start.5 = (f32[4,72,256]{2,1,0:T(8,128)S(1)}, f32[4,72,256]{2,1,0:T(8,128)S(1)}, u32[]{:S(2)}, u32[]{:S(2)}) collective-permute-start(f32[4,72,256]{2,1,0:T(8,128)S(1)} %dynamic-slice_bitcast_fusion), channel_id=1, source_target_pairs={{0,1},{1,0},{2,3},{3,2},{4,5},{5,4},{6,7},{7,6},{8,9},{9,8},{10,11... | collective-permute-start | bytes 884744 | tf_op jit(solution)/shard_map/ppermute | solution.py:364
  48.2 1.2 %collective-permute-done.5 = f32[4,72,256]{2,1,0:T(8,128)S(1)} collective-permute-done((f32[4,72,256]{2,1,0:T(8,128)S(1)}, f32[4,72,256]{2,1,0:T(8,128)S(1)}, u32[]{:S(2)}, u32[]{:S(2)}) %collective-permute-start.5) | collective-permute-done | bytes 294944 | tf_op jit(solution)/shard_map/ppermute | solution.py:364
  49.8 0.7 collective-permute-start.7
  50.6 2.4 %collective-permute-start.8 = (f32[72,256]{1,0:T(8,128)S(1)}, f32[72,256]{1,0:T(8,128)S(1)}, u32[]{:S(2)}, u32[]{:S(2)}) collective-permute-start(f32[72,256]{1,0:T(8,128)S(1)} %get-tuple-element.101), channel_id=1, source_target_pairs={{0,24},{8,16},{16,8},{24,0},{1,25},{9,17},{17,9},{25,1},{2,26},{10... | collective-permute-start | bytes 221192 | tf_op jit(solution)/shard_map/ppermute | solution.py:364
  53.0 0.7 collective-permute-start.10
  53.7 0.7 collective-permute-done.6
  55.0 0.8 %collective-permute-done.8 = f32[72,256]{1,0:T(8,128)S(1)} collective-permute-done((f32[72,256]{1,0:T(8,128)S(1)}, f32[72,256]{1,0:T(8,128)S(1)}, u32[]{:S(2)}, u32[]{:S(2)}) %collective-permute-start.8) | collective-permute-done | bytes 73760 | tf_op jit(solution)/shard_map/ppermute | solution.py:364
  55.9 1.6 %collective-permute-start.9 = (f32[72,256]{1,0:T(8,128)S(1)}, f32[72,256]{1,0:T(8,128)S(1)}, u32[]{:S(2)}, u32[]{:S(2)}) collective-permute-start(f32[72,256]{1,0:T(8,128)S(1)} %fusion.1), channel_id=1, source_target_pairs={{0,2},{1,3},{2,0},{3,1},{4,6},{5,7},{6,4},{7,5},{8,10},{9,11},{10,... | collective-permute-start | bytes 221192 | tf_op jit(solution)/shard_map/ppermute | solution.py:364
  58.2 2.1 %collective-permute-done.9 = f32[72,256]{1,0:T(8,128)S(1)} collective-permute-done((f32[72,256]{1,0:T(8,128)S(1)}, f32[72,256]{1,0:T(8,128)S(1)}, u32[]{:S(2)}, u32[]{:S(2)}) %collective-permute-start.9) | collective-permute-done | bytes 73760 | tf_op jit(solution)/shard_map/ppermute | solution.py:364
  60.3 4.7 %collective-permute-start.12 = (f32[72,256]{1,0:T(8,128)S(1)}, f32[72,256]{1,0:T(8,128)S(1)}, u32[]{:S(2)}, u32[]{:S(2)}) collective-permute-start(f32[72,256]{1,0:T(8,128)S(1)} %add.54), channel_id=1, source_target_pairs={{0,4},{1,5},{2,6},{3,7},{4,0},{5,1},{6,2},{7,3},{8,12},{9,13},{10,... | collective-permute-start | bytes 221192 | tf_op jit(solution)/shard_map/ppermute | solution.py:364
  65.0 3.9 %collective-permute-done.12 = f32[72,256]{1,0:T(8,128)S(1)} collective-permute-done((f32[72,256]{1,0:T(8,128)S(1)}, f32[72,256]{1,0:T(8,128)S(1)}, u32[]{:S(2)}, u32[]{:S(2)}) %collective-permute-start.12) | collective-permute-done | bytes 73760 | tf_op jit(solution)/shard_map/ppermute | solution.py:364
  68.9 1.7 %collective-permute-start.14 = (f32[72,256]{1,0:T(8,128)S(1)}, f32[72,256]{1,0:T(8,128)S(1)}, u32[]{:S(2)}, u32[]{:S(2)}) collective-permute-start(f32[72,256]{1,0:T(8,128)S(1)} %add.55), channel_id=1, source_target_pairs={{0,8},{8,0},{16,24},{24,16},{1,9},{9,1},{17,25},{25,17},{2,10},{10... | collective-permute-start | bytes 221192 | tf_op jit(solution)/shard_map/ppermute | solution.py:364
  70.7 1.4 %collective-permute-start.15 = (f32[72,256]{1,0:T(8,128)S(1)}, f32[72,256]{1,0:T(8,128)S(1)}, u32[]{:S(2)}, u32[]{:S(2)}) collective-permute-start(f32[72,256]{1,0:T(8,128)S(1)} %add.55), channel_id=1, source_target_pairs={{0,16},{8,24},{16,0},{24,8},{1,17},{9,25},{17,1},{25,9},{2,18},{10... | collective-permute-start | bytes 221192 | tf_op jit(solution)/shard_map/ppermute | solution.py:364
  72.5 1.9 %fields.1 = (f32[3,32,512]{2,1,0:T(8,128)}, f32[3,32,512]{2,1,0:T(8,128)}) custom-call(f32[2,4]{1,0:T(2,128)} %table.1, s32[32,512]{1,0:T(8,128)} %bitcast.43, f32[3,32,512]{2,1,0:T(8,128)} %bitcast.38, f32[9,16,512]{2,1,0:T(8,128)S(1)} %get-tuple-element.72.stress_near, f32[6,16,512]{2,1,0:T(8,128)S(1)} %get-tuple-element.78.stress_far, ...), custom_call_target="tpu_custom_call" | custom-call | tf_op jit(solution)/shard_map/fields/pallas_call | solution.py:495
  75.0 2.3 %collective-permute-done.16 = f32[72,256]{1,0:T(8,128)S(1)} collective-permute-done((f32[72,256]{1,0:T(8,128)S(1)}, f32[72,256]{1,0:T(8,128)S(1)}, u32[]{:S(2)}, u32[]{:S(2)}) %collective-permute-start.16) | collective-permute-done | bytes 73760 | tf_op jit(solution)/shard_map/ppermute | solution.py:364
  77.4 1.6 %collective-permute-done.17.other = f32[4,72,256]{2,1,0:T(8,128)S(1)} collective-permute-done((f32[4,72,256]{2,1,0:T(8,128)S(1)}, f32[4,72,256]{2,1,0:T(8,128)S(1)}, u32[]{:S(2)}, u32[]{:S(2)}) %collective-permute-start.17) | collective-permute-done | bytes 294944 | tf_op jit(solution)/shard_map/ppermute | solution.py:364
  78.9 1.1 %finish.1 = (f32[10,256]{1,0:T(8,128)}, f32[1,256]{1,0:T(1,128)}, f32[512,256]{1,0:T(8,128)}, f32[2,256]{1,0:T(2,128)}, f32[9,256]{1,0:T(8,128)}, /*index=5*/f32[1,9]{1,0:T(1,128)}) custom-call(f32[4,72,256]{2,1,0:T(8,128)S(1)} %pad_maximum_fusion.mine, f32[4,72,256]{2,1,0:T(8,128)S(1)} %collective-permute-done.17.other), custom_call_target="tpu_custom_call" | custom-call | tf_op jit(solution)/shard_map/finish/pallas_call | solution.py:520
  (24 shorter events, 3.6 us)
Async XLA Ops:
  2.0 7.9 %collective-permute-start.3 = (f32[6,16,512]{2,1,0:T(8,128)S(1)}, f32[6,16,512]{2,1,0:T(8,128)S(1)}, u32[]{:S(2)}, u32[]{:S(2)}) collective-permute-start(f32[6,16,512]{2,1,0:T(8,128)S(1)} %get-tuple-element.57), channel_id=1, source_target_pairs={{0,8},{8,0},{16,24},{24,16},{1,9},{9,1},{17,25},{25,17},{2,10},{10... | collective-permute-start | bytes 589832 | tf_op jit(solution)/shard_map/ppermute | solution.py:364
  5.0 2.0 %collective-permute-start.1 = (f32[9,2,512]{2,1,0:T(2,128)S(1)}, f32[9,2,512]{2,1,0:T(2,128)S(1)}, u32[]{:S(2)}, u32[]{:S(2)}) collective-permute-start(f32[9,2,512]{2,1,0:T(2,128)S(1)} %get-tuple-element.55), channel_id=1, source_target_pairs={{0,1},{1,0},{2,3},{3,2},{4,5},{5,4},{6,7},{7,6},{8,9},{9,8},{10,11... | collective-permute-start | bytes 110600 | tf_op jit(solution)/shard_map/ppermute | solution.py:364
  5.0 2.0 %collective-permute-start.2 = (f32[9,2,512]{2,1,0:T(2,128)S(1)}, f32[9,2,512]{2,1,0:T(2,128)S(1)}, u32[]{:S(2)}, u32[]{:S(2)}) collective-permute-start(f32[9,2,512]{2,1,0:T(2,128)S(1)} %get-tuple-element.56), channel_id=1, source_target_pairs={{1,2},{2,1},{3,4},{4,3},{5,6},{6,5},{9,10},{10,9},{11,12},{12,11},... | collective-permute-start | bytes 110600 | tf_op jit(solution)/shard_map/ppermute | solution.py:358
  5.6 23.3 %collective-permute-start = (f32[9,16,512]{2,1,0:T(8,128)S(1)}, f32[9,16,512]{2,1,0:T(8,128)S(1)}, u32[]{:S(2)}, u32[]{:S(2)}) collective-permute-start(f32[9,16,512]{2,1,0:T(8,128)S(1)} %get-tuple-element.54), channel_id=1, source_target_pairs={{8,16},{16,8},{9,17},{17,9},{10,18},{18,10},{11,19},{19,11},{12,20... | collective-permute-start | bytes 884744 | tf_op jit(solution)/shard_map/ppermute | solution.py:358
  27.1 18.9 %collective-permute-start.4 = (f32[9,16,512]{2,1,0:T(8,128)S(1)}, f32[9,16,512]{2,1,0:T(8,128)S(1)}, u32[]{:S(2)}, u32[]{:S(2)}) collective-permute-start(f32[9,16,512]{2,1,0:T(8,128)S(1)} %get-tuple-element.72.stress_near), channel_id=1, source_target_pairs={{0,8},{8,0},{16,24},{24,16},{1,9},{9,1},{17,25},{25,17},{2,10},{10... | collective-permute-start | bytes 884744 | tf_op jit(solution)/shard_map/ppermute | solution.py:364
  46.0 3.3 %collective-permute-start.5 = (f32[4,72,256]{2,1,0:T(8,128)S(1)}, f32[4,72,256]{2,1,0:T(8,128)S(1)}, u32[]{:S(2)}, u32[]{:S(2)}) collective-permute-start(f32[4,72,256]{2,1,0:T(8,128)S(1)} %dynamic-slice_bitcast_fusion), channel_id=1, source_target_pairs={{0,1},{1,0},{2,3},{3,2},{4,5},{5,4},{6,7},{7,6},{8,9},{9,8},{10,11... | collective-permute-start | bytes 884744 | tf_op jit(solution)/shard_map/ppermute | solution.py:364
  49.5 5.0 %collective-permute-start.6 = (f32[72,256]{1,0:T(8,128)S(1)}, f32[72,256]{1,0:T(8,128)S(1)}, u32[]{:S(2)}, u32[]{:S(2)}) collective-permute-start(f32[72,256]{1,0:T(8,128)S(1)} %get-tuple-element.100), channel_id=1, source_target_pairs={{0,8},{8,0},{16,24},{24,16},{1,9},{9,1},{17,25},{25,17},{2,10},{10... | collective-permute-start | bytes 221192 | tf_op jit(solution)/shard_map/ppermute | solution.py:364
  49.8 5.1 %collective-permute-start.7 = (f32[72,256]{1,0:T(8,128)S(1)}, f32[72,256]{1,0:T(8,128)S(1)}, u32[]{:S(2)}, u32[]{:S(2)}) collective-permute-start(f32[72,256]{1,0:T(8,128)S(1)} %get-tuple-element.102), channel_id=1, source_target_pairs={{0,16},{8,24},{16,0},{24,8},{1,17},{9,25},{17,1},{25,9},{2,18},{10... | collective-permute-start | bytes 221192 | tf_op jit(solution)/shard_map/ppermute | solution.py:364
  50.6 5.3 %collective-permute-start.8 = (f32[72,256]{1,0:T(8,128)S(1)}, f32[72,256]{1,0:T(8,128)S(1)}, u32[]{:S(2)}, u32[]{:S(2)}) collective-permute-start(f32[72,256]{1,0:T(8,128)S(1)} %get-tuple-element.101), channel_id=1, source_target_pairs={{0,24},{8,16},{16,8},{24,0},{1,25},{9,17},{17,9},{25,1},{2,26},{10... | collective-permute-start | bytes 221192 | tf_op jit(solution)/shard_map/ppermute | solution.py:364
  53.0 7.3 %collective-permute-start.10 = (f32[6,16,512]{2,1,0:T(8,128)S(1)}, f32[6,16,512]{2,1,0:T(8,128)S(1)}, u32[]{:S(2)}, u32[]{:S(2)}) collective-permute-start(f32[6,16,512]{2,1,0:T(8,128)S(1)} %get-tuple-element.78.stress_far), channel_id=1, source_target_pairs={{8,16},{16,8},{9,17},{17,9},{10,18},{18,10},{11,19},{19,11},{12,20... | collective-permute-start | bytes 589832 | tf_op jit(solution)/shard_map/ppermute | solution.py:358
  55.9 4.4 %collective-permute-start.9 = (f32[72,256]{1,0:T(8,128)S(1)}, f32[72,256]{1,0:T(8,128)S(1)}, u32[]{:S(2)}, u32[]{:S(2)}) collective-permute-start(f32[72,256]{1,0:T(8,128)S(1)} %fusion.1), channel_id=1, source_target_pairs={{0,2},{1,3},{2,0},{3,1},{4,6},{5,7},{6,4},{7,5},{8,10},{9,11},{10,... | collective-permute-start | bytes 221192 | tf_op jit(solution)/shard_map/ppermute | solution.py:364
  57.5 2.8 %collective-permute-start.11 = (f32[6,2,512]{2,1,0:T(2,128)S(1)}, f32[6,2,512]{2,1,0:T(2,128)S(1)}, u32[]{:S(2)}, u32[]{:S(2)}) collective-permute-start(f32[6,2,512]{2,1,0:T(2,128)S(1)} %get-tuple-element.79), channel_id=1, source_target_pairs={{1,2},{2,1},{3,4},{4,3},{5,6},{6,5},{9,10},{10,9},{11,12},{12,11},... | collective-permute-start | bytes 73736 | tf_op jit(solution)/shard_map/ppermute | solution.py:358
  60.3 8.6 %collective-permute-start.12 = (f32[72,256]{1,0:T(8,128)S(1)}, f32[72,256]{1,0:T(8,128)S(1)}, u32[]{:S(2)}, u32[]{:S(2)}) collective-permute-start(f32[72,256]{1,0:T(8,128)S(1)} %add.54), channel_id=1, source_target_pairs={{0,4},{1,5},{2,6},{3,7},{4,0},{5,1},{6,2},{7,3},{8,12},{9,13},{10,... | collective-permute-start | bytes 221192 | tf_op jit(solution)/shard_map/ppermute | solution.py:364
  65.0 3.9 %collective-permute-start.13 = (f32[6,2,512]{2,1,0:T(2,128)S(1)}, f32[6,2,512]{2,1,0:T(2,128)S(1)}, u32[]{:S(2)}, u32[]{:S(2)}) collective-permute-start(f32[6,2,512]{2,1,0:T(2,128)S(1)} %get-tuple-element.81), channel_id=1, source_target_pairs={{0,1},{1,0},{2,3},{3,2},{4,5},{5,4},{6,7},{7,6},{8,9},{9,8},{10,11... | collective-permute-start | bytes 73736 | tf_op jit(solution)/shard_map/ppermute | solution.py:364
  68.9 5.5 %collective-permute-start.14 = (f32[72,256]{1,0:T(8,128)S(1)}, f32[72,256]{1,0:T(8,128)S(1)}, u32[]{:S(2)}, u32[]{:S(2)}) collective-permute-start(f32[72,256]{1,0:T(8,128)S(1)} %add.55), channel_id=1, source_target_pairs={{0,8},{8,0},{16,24},{24,16},{1,9},{9,1},{17,25},{25,17},{2,10},{10... | collective-permute-start | bytes 221192 | tf_op jit(solution)/shard_map/ppermute | solution.py:364
  70.7 4.4 %collective-permute-start.15 = (f32[72,256]{1,0:T(8,128)S(1)}, f32[72,256]{1,0:T(8,128)S(1)}, u32[]{:S(2)}, u32[]{:S(2)}) collective-permute-start(f32[72,256]{1,0:T(8,128)S(1)} %add.55), channel_id=1, source_target_pairs={{0,16},{8,24},{16,0},{24,8},{1,17},{9,25},{17,1},{25,9},{2,18},{10... | collective-permute-start | bytes 221192 | tf_op jit(solution)/shard_map/ppermute | solution.py:364
  72.0 5.3 %collective-permute-start.16 = (f32[72,256]{1,0:T(8,128)S(1)}, f32[72,256]{1,0:T(8,128)S(1)}, u32[]{:S(2)}, u32[]{:S(2)}) collective-permute-start(f32[72,256]{1,0:T(8,128)S(1)} %add.55), channel_id=1, source_target_pairs={{0,24},{8,16},{16,8},{24,0},{1,25},{9,17},{17,9},{25,1},{2,26},{10... | collective-permute-start | bytes 221192 | tf_op jit(solution)/shard_map/ppermute | solution.py:364
  77.3 1.6 %collective-permute-start.17 = (f32[4,72,256]{2,1,0:T(8,128)S(1)}, f32[4,72,256]{2,1,0:T(8,128)S(1)}, u32[]{:S(2)}, u32[]{:S(2)}) collective-permute-start(f32[4,72,256]{2,1,0:T(8,128)S(1)} %pad_maximum_fusion.mine), channel_id=1, source_target_pairs={{0,1},{1,0},{2,3},{3,2},{4,5},{5,4},{6,7},{7,6},{8,9},{9,8},{10,11... | collective-permute-start | bytes 884744 | tf_op jit(solution)/shard_map/ppermute | solution.py:364

commit v5 on v4

--- a/solution.py
+++ b/solution.py
@@ -97,6 +97,19 @@
                 y_next[slot, k : k + 1] = jnp.where(side == 0, field[:1], field[rows - 1 :])
 
 
+def put_face(ref, base, slot, k, face):
+    pieces = face.shape[1] // HID
+    at = base + (2 * slot + k) * pieces
+    for j in range(pieces):
+        ref[at + j : at + j + 1] = face[:, j * HID : (j + 1) * HID]
+
+
+def get_face(ref, base, slot, k, lanes):
+    pieces = lanes // HID
+    at = base + (2 * slot + k) * pieces
+    return jnp.concatenate([ref[at + j : at + j + 1] for j in range(pieces)], 1)
+
+
 def low_high(side, pair, following):
     return jnp.where(side == 0, following, pair), jnp.where(side == 0, pair, following)
 
@@ -106,11 +119,11 @@
     (edge, y_pair, y_next), refs = refs[:3], refs[3:]
     if order:
         faces_first, given, refs = refs[:2], refs[2:13], refs[13:]
-        (sx, s_pair, s_next, rest, grads), refs = refs[:5], refs[5:]
+        (sx, s_next, rest, kept_half, sent), refs = refs[:5], refs[5:]
     else:
         (sx, s_pair, s_next, rest), kept, refs = refs[:4], refs[4:15], refs[15:]
     targets, sems, refs = refs[: len(sources)], refs[len(sources)], refs[len(sources) + 1 :]
-    grid_in, grid_delta, feats, delta, net, back, wide, *refs = refs
+    grid_in, grid_delta, feats, delta, net, back, wide, small, *refs = refs
     copies = fetch(sources, targets, sems)
     near, side = near_first()
     if order:
@@ -249,11 +262,18 @@
             slot = base + i
             sx[slot] = along[0]
             first, last = along[1][:1], along[1][rows - 1 :]
-            s_pair[slot, order : order + 1] = jnp.where(side == 0, last, first)
-            s_next[slot, order : order + 1] = jnp.where(side == 0, first, last)
+            to_pair = jnp.where(side == 0, last, first)
+            to_next = jnp.where(side == 0, first, last)
             if order:
-                s_pair[slot, 0:1] = faces_first[0][slot, 0:1]
-                s_next[slot, 0:1] = faces_first[1][slot, 0:1]
+                tail = sent.shape[0] - s_next.shape[0]
+                near_pair, near_next = (ref[slot] for ref in faces_first)
+                put_face(sent, tail, slot, 0, near_pair)
+                put_face(sent, tail, slot, 1, to_pair)
+                put_face(s_next, 0, slot, 0, near_next)
+                put_face(s_next, 0, slot, 1, to_next)
+            else:
+                s_pair[slot] = to_pair
+                s_next[slot] = to_next
             rest[slot] = half_diff(y_ends(along[1], 0.0, 0.0, rows)) + half_diff(
                 z_ends(along[2])
             )
@@ -262,20 +282,26 @@
             sx[6 + i] = targets[12][i, own]
         return
 
-    chunks = grads.shape[0]
-    part = 2 * HID // chunks
-    for c in range(chunks):
-        grads[c, :part] = acc_mid[c * part : (c + 1) * part]
-        grads[c, part:] = jnp.zeros((SMALL, HID), f32)
-    grads[0, part:] = acc_in[:8]
-    grads[1, part:] = jnp.where(rowid[:8] < 3, acc_in[8:], 0.0)
-    grads[2, part:] = acc_out[:8]
-    grads[3, part:] = acc_out[8:]
+    count = kept_half.shape[0]
+    part = HID // count
+    small[...] = jnp.zeros_like(small)
+    small[:8] = acc_in[:8]
+    small[8:16] = jnp.where(rowid[:8] < 3, acc_in[8:], 0.0)
+    small[16:32] = acc_out[...]
     for k in range(2):
-        grads[4, part + k : part + k + 1] = jnp.sum(acc_b[k].T, axis=0, keepdims=True)
+        small[32 + k : 33 + k] = jnp.sum(acc_b[k].T, axis=0, keepdims=True)
     wide[...] = jnp.zeros_like(wide)
     wide[:16, :128] = acc_bo[...]
-    grads[4, part + 2 : part + 3, :128] = jnp.sum(wide[:, :128].T, axis=0, keepdims=True)
+    small[34:35, :128] = jnp.sum(wide[:, :128].T, axis=0, keepdims=True)
+    half = lax.rem(lax.axis_index("gy"), 2)
+    for c in range(count):
+        mine, theirs = half * count + c, (1 - half) * count + c
+        kept_half[c, :part] = acc_mid[pl.ds(pl.multiple_of(mine * part, part), part)]
+        kept_half[c, part:] = small[pl.ds(pl.multiple_of(mine * SMALL, SMALL), SMALL)]
+        at = c * (part + SMALL)
+        sent[at : at + part] = acc_mid[pl.ds(pl.multiple_of(theirs * part, part), part)]
+        at += part
+        sent[at : at + SMALL] = small[pl.ds(pl.multiple_of(theirs * SMALL, SMALL), SMALL)]
 
 
 def fields_kernel(
@@ -309,7 +335,11 @@
         moving, rest = (x_next, rest_far) if k else (sx_pair, rest_near)
 
         def total(slot):
-            low, high = low_high(side, sy_pair[slot, k : k + 1], sy_next[slot, k : k + 1])
+            low, high = low_high(
+                side,
+                get_face(sy_pair, sy_pair.shape[0] - sy_next.shape[0], slot, k, lanes),
+                get_face(sy_next, 0, slot, k, lanes),
+            )
             value = rest[slot] + (other[slot] - edge[slot]) * uphill
             value = value - jnp.where(where == 0, low * 0.5, 0.0)
             return value + jnp.where(where == rows - 1, high * 0.5, 0.0)
@@ -384,6 +414,8 @@
     nx, ny = lax.axis_size("gx"), lax.axis_size("gy")
     chunks = 2 * nx
     part = 2 * HID // chunks
+    face_rows = 12 * (lanes // HID)
+    assert lanes % HID == 0 and ny & (ny - 1) == 0
     assert planes == 2 and chunks >= GROUPS and nx % 2 == ny % 2 == 0 and part % 8 == 0
     material = material.reshape(size, lanes)
     phase = phase.reshape(size, lanes)
@@ -430,16 +462,18 @@
 
     def network(order, sources, near):
         outs = [jax.ShapeDtypeStruct(*item) for item in handed]
+        faces_out = [(6, 1, lanes)] * 2
         if order:
-            outs = shapes((chunks, part + SMALL, HID))
+            outs = shapes((nx, part + SMALL, HID), (nx * (part + SMALL) + face_rows, HID))
+            faces_out = [(face_rows, HID)]
         return pl.pallas_call(
             functools.partial(network_kernel, order, rows, block),
             out_shape=shapes(
-                (9 - 3 * order, rows, lanes), *[(6, 1 + order, lanes)] * 2, (6, rows, lanes)
+                (9 - 3 * order, rows, lanes), *faces_out, (6, rows, lanes)
             )
             + outs,
             in_specs=[HBM] * len(sources) + [VMEM] * len(near),
-            out_specs=[VMEM] * (4 + len(outs)),
+            out_specs=[VMEM] * (2 + len(faces_out) + len(outs)),
             scratch_shapes=[
                 *[pltpu.SMEM(item.shape, f32) for item in sources[:3]],
                 *[pltpu.VMEM(item.shape, item.dtype) for item in sources[3:]],
@@ -448,6 +482,7 @@
                 *[pltpu.VMEM((16, voxels), bf16)] * 2,
                 *[pltpu.VMEM((16, voxels), f32)] * 2,
                 pltpu.VMEM((128, HID), f32),
+                pltpu.VMEM((chunks * SMALL, HID), f32),
                 *[pltpu.VMEM(*item) for item in handed[: 5 * order]],
             ],
             compiler_params=pltpu.CompilerParams(vmem_limit_bytes=36 << 20),
@@ -469,27 +504,24 @@
     second = network(1, common, [x_next, y_pair, y_next, *first[1:3], *first[4:]])
     sx_next = swap_next(second[0], "gx")
 
-    half = lax.axis_index("gy") % 2
     index = lax.axis_index("gx")
-    pile, sx_pair = lax.optimization_barrier((second[4], sx_pair))
-    pile = pile.reshape(2, nx, part + SMALL, HID)
-    kept = lax.dynamic_index_in_dim(pile, half, 0, keepdims=False)
-    sent = lax.dynamic_index_in_dim(pile, 1 - half, 0, keepdims=False)
-    kept, face = lax.optimization_barrier((kept + swap(sent, "gy", 1), second[2]))
-    sy_next = swap_next(face, "gy")
+    sent, sx_pair = lax.optimization_barrier((second[4], sx_pair))
+    sy_pair = swap(sent, "gy", 1)
+    height = part + SMALL
+    kept = second[3] + sy_pair[: nx * height].reshape(nx, height, HID)
     share = lax.dynamic_index_in_dim(kept, index, 0, keepdims=False)
     for m in range(1, nx):
         piece = lax.dynamic_index_in_dim(kept, index ^ m, 0, keepdims=False)
         share = share + swap(piece, "gx", m)
     share, face = lax.optimization_barrier((share, second[1]))
-    sy_pair = swap(face, "gy", 1)
+    sy_next = swap_next(face, "gy")
     mask = 2
     while mask < ny:
         share = share + swap(share, "gy", mask)
         if mask == 2:
-            share, sx_next, sy_next = lax.optimization_barrier((share, sx_next, sy_next))
+            share, sx_next = lax.optimization_barrier((share, sx_next))
         mask *= 2
-    share, sy_pair = lax.optimization_barrier((share, sy_pair))
+    share, sy_next = lax.optimization_barrier((share, sy_next))
     mine = jnp.stack([share] + [swap(share, "gx", m) for m in range(1, nx)])
 
     fields = pl.pallas_call(
@@ -506,7 +538,7 @@
         first[0],
         second[0],
         first[3],
-        second[3],
+        second[2],
         x_next,
         y_pair,
         y_next,

time: 80.3 us -> 78 us (0.971)
  starting transfers between devices: 23.1 us -> 21.6 us
  waiting for transfers between devices: 16.6 us -> 15.2 us
    ppermute x14 -> x13, starting transfers between devices: 20.5 us -> 18.9 us  [swap(): lax.ppermute(value, axis, [(i, i ^ mask) for i in range(lax.axis_size(axi...]
    ppermute x14 -> x13, waiting for transfers between devices: 16.6 us -> 15.2 us  [swap(): lax.ppermute(value, axis, [(i, i ^ mask) for i in range(lax.axis_size(axi...]
  transfers between devices with their start and end apart: 18 -> 17, of which waited for: 10 -> 10; matrix products, arithmetic and copies ran while one was open for 0% -> 0% of each run, Pallas kernels for 45% -> 47%
where the time goes in v5:
time: 78 us; the launch traced here: 77 us
  Pallas kernels  38.7 us (50%)
  starting transfers between devices  21.6 us (28%)
  waiting for transfers between devices  15.2 us (19%)
  between operations  1.41 us (2%)
    pallas_call x2, Pallas kernels, network(): pl.pallas_call(functools.partial(network_kernel, order, rows, block), out...  34.3 us
    ppermute x13, starting transfers between devices, swap(): lax.ppermute(value, axis, [(i, i ^ mask) for i in range(lax.axis_size(axi...  18.9 us
    ppermute x13, waiting for transfers between devices, swap(): lax.ppermute(value, axis, [(i, i ^ mask) for i in range(lax.axis_size(axi...  15.2 us
    ppermute x4, starting transfers between devices, swap_next(): lax.ppermute(value, axis, [(i, i + 1 if i % 2 else i - 1) for i in range(...  2.64 us
    pallas_call x1, Pallas kernels, body(): pl.pallas_call(functools.partial(fields_kernel, rows), out_shape=shapes(*...  1.96 us
  transfers between devices with their start and end apart: 17, of which 10 were waited for; matrix products, arithmetic and copies ran while one was open for 0% of the time, Pallas kernels for 47%

profile of v5, /device:TPU:0, one launch (start us, length us, event | category | flops | bytes accessed | tf_op | source)
XLA Modules:
  0.0 77.0 jit_solution(4568269022229788629)
XLA Ops:
  0.6 1.3 %faces.1 = (f32[6,16,512]{2,1,0:T(8,128)S(1)}, f32[9,16,512]{2,1,0:T(8,128)S(1)}, f32[9,2,512]{2,1,0:T(2,128)S(1)}, f32[9,2,512]{2,1,0:T(2,128)S(1)}) custom-call(f32[2,4]{1,0:T(2,128)} %table.1, s32[32,512]{1,0:T(8,128)} %bitcast.35, f32[3,32,512]{2,1,0:T(8,128)} %bitcast.39, f32[3,32,512]{2,1,0:T(8,128)} %bitcast.31, f32[3,32,512]{2,1,0:T(8,128)} %bitcast.42), custom_call_target="tpu_custom_call" | custom-call | tf_op jit(solution)/shard_map/faces/pallas_call | solution.py:426
  2.0 3.0 %collective-permute-start.3 = (f32[6,16,512]{2,1,0:T(8,128)S(1)}, f32[6,16,512]{2,1,0:T(8,128)S(1)}, u32[]{:S(2)}, u32[]{:S(2)}) collective-permute-start(f32[6,16,512]{2,1,0:T(8,128)S(1)} %get-tuple-element.54), channel_id=1, source_target_pairs={{0,8},{8,0},{16,24},{24,16},{1,9},{9,1},{17,25},{25,17},{2,10},{10... | collective-permute-start | bytes 589832 | tf_op jit(solution)/shard_map/ppermute | solution.py:394
  5.6 0.7 collective-permute-start
  7.0 2.9 %collective-permute-done.3.refs_13_ = f32[6,16,512]{2,1,0:T(8,128)S(1)} collective-permute-done((f32[6,16,512]{2,1,0:T(8,128)S(1)}, f32[6,16,512]{2,1,0:T(8,128)S(1)}, u32[]{:S(2)}, u32[]{:S(2)}) %collective-permute-start.3) | collective-permute-done | bytes 196640 | tf_op jit(solution)/shard_map/ppermute | solution.py:394
  9.9 17.2 %network.2 = (f32[9,16,512]{2,1,0:T(8,128)S(1)}, f32[6,1,512]{2,1,0:T(1,128)S(1)}, f32[6,1,512]{2,1,0:T(1,128)S(1)}, f32[6,16,512]{2,1,0:T(8,128)S(1)}, f32[512,...) custom-call(f32[2,4]{1,0:T(2,128)} %table.1, ...), custom_call_target="tpu_custom_call" | custom-call | flops 6681526272 | bytes 524288 | tf_op jit(solution)/shard_map/network/pallas_call | solution.py:469
  27.1 1.8 %collective-permute-start.4 = (f32[9,16,512]{2,1,0:T(8,128)S(1)}, f32[9,16,512]{2,1,0:T(8,128)S(1)}, u32[]{:S(2)}, u32[]{:S(2)}) collective-permute-start(f32[9,16,512]{2,1,0:T(8,128)S(1)} %get-tuple-element.70.stress_near), channel_id=1, source_target_pairs={{0,8},{8,0},{16,24},{24,16},{1,9},{9,1},{17,25},{25,17},{2,10},{10... | collective-permute-start | bytes 884744 | tf_op jit(solution)/shard_map/ppermute | solution.py:394
  28.9 17.1 %network.3 = (f32[6,16,512]{2,1,0:T(8,128)S(1)}, f32[24,256]{1,0:T(8,128)S(1)}, f32[6,16,512]{2,1,0:T(8,128)S(1)}, f32[4,72,256]{2,1,0:T(8,128)S(1)}, f32[312,256]{1,0:T(8,128)S(1)}) custom-call(f32[2,4]{1,0:T(2,128)} %table.1, f32[1]{0:T(128)S(6)} %copy.21.refs_1_, f32[9]{0:T(128)} %refs_2_.3, s32[32,512]{1,0:T(8,128)} %bitcast.37, s32[32,512]{1,0:T(8,128)} %bitcast.52, ...), custom_call_target="tpu_custom_call" | custom-call | flops 6681526272 | bytes 524288 | tf_op jit(solution)/shard_map/network/pallas_call | solution.py:469
  46.0 2.1 %collective-permute-start.5 = (f32[312,256]{1,0:T(8,128)S(1)}, f32[312,256]{1,0:T(8,128)S(1)}, u32[]{:S(2)}, u32[]{:S(2)}) collective-permute-start(f32[312,256]{1,0:T(8,128)S(1)} %get-tuple-element.71), channel_id=1, source_target_pairs={{0,1},{1,0},{2,3},{3,2},{4,5},{5,4},{6,7},{7,6},{8,9},{9,8},{10,11... | collective-permute-start | bytes 958472 | tf_op jit(solution)/shard_map/ppermute | solution.py:394
  48.1 1.2 %collective-permute-done.5.sy_pair = f32[312,256]{1,0:T(8,128)S(1)} collective-permute-done((f32[312,256]{1,0:T(8,128)S(1)}, f32[312,256]{1,0:T(8,128)S(1)}, u32[]{:S(2)}, u32[]{:S(2)}) %collective-permute-start.5) | collective-permute-done | bytes 319520 | tf_op jit(solution)/shard_map/ppermute | solution.py:394
  49.9 0.7 collective-permute-start.7
  50.6 2.4 %collective-permute-start.8 = (f32[72,256]{1,0:T(8,128)S(1)}, f32[72,256]{1,0:T(8,128)S(1)}, u32[]{:S(2)}, u32[]{:S(2)}) collective-permute-start(f32[72,256]{1,0:T(8,128)S(1)} %get-tuple-element.95), channel_id=1, source_target_pairs={{0,24},{8,16},{16,8},{24,0},{1,25},{9,17},{17,9},{25,1},{2,26},{10... | collective-permute-start | bytes 221192 | tf_op jit(solution)/shard_map/ppermute | solution.py:394
  53.7 0.7 collective-permute-done.6
  55.0 0.8 %collective-permute-done.8 = f32[72,256]{1,0:T(8,128)S(1)} collective-permute-done((f32[72,256]{1,0:T(8,128)S(1)}, f32[72,256]{1,0:T(8,128)S(1)}, u32[]{:S(2)}, u32[]{:S(2)}) %collective-permute-start.8) | collective-permute-done | bytes 73760 | tf_op jit(solution)/shard_map/ppermute | solution.py:394
  55.9 1.6 %collective-permute-start.9 = (f32[72,256]{1,0:T(8,128)S(1)}, f32[72,256]{1,0:T(8,128)S(1)}, u32[]{:S(2)}, u32[]{:S(2)}) collective-permute-start(f32[72,256]{1,0:T(8,128)S(1)} %fusion.1), channel_id=1, source_target_pairs={{0,2},{1,3},{2,0},{3,1},{4,6},{5,7},{6,4},{7,5},{8,10},{9,11},{10,... | collective-permute-start | bytes 221192 | tf_op jit(solution)/shard_map/ppermute | solution.py:394
  57.5 2.8 %collective-permute-done.9 = f32[72,256]{1,0:T(8,128)S(1)} collective-permute-done((f32[72,256]{1,0:T(8,128)S(1)}, f32[72,256]{1,0:T(8,128)S(1)}, u32[]{:S(2)}, u32[]{:S(2)}) %collective-permute-start.9) | collective-permute-done | bytes 73760 | tf_op jit(solution)/shard_map/ppermute | solution.py:394
  60.3 2.6 %collective-permute-start.11 = (f32[72,256]{1,0:T(8,128)S(1)}, f32[72,256]{1,0:T(8,128)S(1)}, u32[]{:S(2)}, u32[]{:S(2)}) collective-permute-start(f32[72,256]{1,0:T(8,128)S(1)} %add.39), channel_id=1, source_target_pairs={{0,4},{1,5},{2,6},{3,7},{4,0},{5,1},{6,2},{7,3},{8,12},{9,13},{10,... | collective-permute-start | bytes 221192 | tf_op jit(solution)/shard_map/ppermute | solution.py:394
  63.6 2.0 %collective-permute-done.11 = f32[72,256]{1,0:T(8,128)S(1)} collective-permute-done((f32[72,256]{1,0:T(8,128)S(1)}, f32[72,256]{1,0:T(8,128)S(1)}, u32[]{:S(2)}, u32[]{:S(2)}) %collective-permute-start.11) | collective-permute-done | bytes 73760 | tf_op jit(solution)/shard_map/ppermute | solution.py:394
  65.7 2.2 %collective-permute-start.13 = (f32[72,256]{1,0:T(8,128)S(1)}, f32[72,256]{1,0:T(8,128)S(1)}, u32[]{:S(2)}, u32[]{:S(2)}) collective-permute-start(f32[72,256]{1,0:T(8,128)S(1)} %add.40), channel_id=1, source_target_pairs={{0,8},{8,0},{16,24},{24,16},{1,9},{9,1},{17,25},{25,17},{2,10},{10... | collective-permute-start | bytes 221192 | tf_op jit(solution)/shard_map/ppermute | solution.py:394
  67.8 0.9 %collective-permute-start.14 = (f32[72,256]{1,0:T(8,128)S(1)}, f32[72,256]{1,0:T(8,128)S(1)}, u32[]{:S(2)}, u32[]{:S(2)}) collective-permute-start(f32[72,256]{1,0:T(8,128)S(1)} %add.40), channel_id=1, source_target_pairs={{0,16},{8,24},{16,0},{24,8},{1,17},{9,25},{17,1},{25,9},{2,18},{10... | collective-permute-start | bytes 221192 | tf_op jit(solution)/shard_map/ppermute | solution.py:394
  69.4 2.0 %fields.1 = (f32[3,32,512]{2,1,0:T(8,128)}, f32[3,32,512]{2,1,0:T(8,128)}) custom-call(f32[2,4]{1,0:T(2,128)} %table.1, s32[32,512]{1,0:T(8,128)} %bitcast.38, f32[3,32,512]{2,1,0:T(8,128)} %bitcast.33, f32[9,16,512]{2,1,0:T(8,128)S(1)} %get-tuple-element.70.stress_near, f32[6,16,512]{2,1,0:T(8,128)S(1)} %get-tuple-element.74.stress_far, ...), custom_call_target="tpu_custom_call" | custom-call | tf_op jit(solution)/shard_map/fields/pallas_call | solution.py:527
  71.4 1.0 %collective-permute-done.14 = f32[72,256]{1,0:T(8,128)S(1)} collective-permute-done((f32[72,256]{1,0:T(8,128)S(1)}, f32[72,256]{1,0:T(8,128)S(1)}, u32[]{:S(2)}, u32[]{:S(2)}) %collective-permute-start.14) | collective-permute-done | bytes 73760 | tf_op jit(solution)/shard_map/ppermute | solution.py:394
  72.4 1.8 %collective-permute-done.15 = f32[72,256]{1,0:T(8,128)S(1)} collective-permute-done((f32[72,256]{1,0:T(8,128)S(1)}, f32[72,256]{1,0:T(8,128)S(1)}, u32[]{:S(2)}, u32[]{:S(2)}) %collective-permute-start.15) | collective-permute-done | bytes 73760 | tf_op jit(solution)/shard_map/ppermute | solution.py:394
  74.7 1.2 %collective-permute-done.16.other = f32[4,72,256]{2,1,0:T(8,128)S(1)} collective-permute-done((f32[4,72,256]{2,1,0:T(8,128)S(1)}, f32[4,72,256]{2,1,0:T(8,128)S(1)}, u32[]{:S(2)}, u32[]{:S(2)}) %collective-permute-start.16) | collective-permute-done | bytes 294944 | tf_op jit(solution)/shard_map/ppermute | solution.py:394
  75.9 1.1 %finish.1 = (f32[10,256]{1,0:T(8,128)}, f32[1,256]{1,0:T(1,128)}, f32[512,256]{1,0:T(8,128)}, f32[2,256]{1,0:T(2,128)}, f32[9,256]{1,0:T(8,128)}, /*index=5*/f32[1,9]{1,0:T(1,128)}) custom-call(f32[4,72,256]{2,1,0:T(8,128)S(1)} %pad_maximum_fusion.mine, f32[4,72,256]{2,1,0:T(8,128)S(1)} %collective-permute-done.16.other), custom_call_target="tpu_custom_call" | custom-call | tf_op jit(solution)/shard_map/finish/pallas_call | solution.py:552
  (22 shorter events, 4.2 us)
Async XLA Ops:
  2.0 7.9 %collective-permute-start.3 = (f32[6,16,512]{2,1,0:T(8,128)S(1)}, f32[6,16,512]{2,1,0:T(8,128)S(1)}, u32[]{:S(2)}, u32[]{:S(2)}) collective-permute-start(f32[6,16,512]{2,1,0:T(8,128)S(1)} %get-tuple-element.54), channel_id=1, source_target_pairs={{0,8},{8,0},{16,24},{24,16},{1,9},{9,1},{17,25},{25,17},{2,10},{10... | collective-permute-start | bytes 589832 | tf_op jit(solution)/shard_map/ppermute | solution.py:394
  5.0 2.0 %collective-permute-start.1 = (f32[9,2,512]{2,1,0:T(2,128)S(1)}, f32[9,2,512]{2,1,0:T(2,128)S(1)}, u32[]{:S(2)}, u32[]{:S(2)}) collective-permute-start(f32[9,2,512]{2,1,0:T(2,128)S(1)} %get-tuple-element.52), channel_id=1, source_target_pairs={{0,1},{1,0},{2,3},{3,2},{4,5},{5,4},{6,7},{7,6},{8,9},{9,8},{10,11... | collective-permute-start | bytes 110600 | tf_op jit(solution)/shard_map/ppermute | solution.py:394
  5.0 2.0 %collective-permute-start.2 = (f32[9,2,512]{2,1,0:T(2,128)S(1)}, f32[9,2,512]{2,1,0:T(2,128)S(1)}, u32[]{:S(2)}, u32[]{:S(2)}) collective-permute-start(f32[9,2,512]{2,1,0:T(2,128)S(1)} %get-tuple-element.53), channel_id=1, source_target_pairs={{1,2},{2,1},{3,4},{4,3},{5,6},{6,5},{9,10},{10,9},{11,12},{12,11},... | collective-permute-start | bytes 110600 | tf_op jit(solution)/shard_map/ppermute | solution.py:388
  5.6 23.3 %collective-permute-start = (f32[9,16,512]{2,1,0:T(8,128)S(1)}, f32[9,16,512]{2,1,0:T(8,128)S(1)}, u32[]{:S(2)}, u32[]{:S(2)}) collective-permute-start(f32[9,16,512]{2,1,0:T(8,128)S(1)} %get-tuple-element.51), channel_id=1, source_target_pairs={{8,16},{16,8},{9,17},{17,9},{10,18},{18,10},{11,19},{19,11},{12,20... | collective-permute-start | bytes 884744 | tf_op jit(solution)/shard_map/ppermute | solution.py:388
  27.1 18.9 %collective-permute-start.4 = (f32[9,16,512]{2,1,0:T(8,128)S(1)}, f32[9,16,512]{2,1,0:T(8,128)S(1)}, u32[]{:S(2)}, u32[]{:S(2)}) collective-permute-start(f32[9,16,512]{2,1,0:T(8,128)S(1)} %get-tuple-element.70.stress_near), channel_id=1, source_target_pairs={{0,8},{8,0},{16,24},{24,16},{1,9},{9,1},{17,25},{25,17},{2,10},{10... | collective-permute-start | bytes 884744 | tf_op jit(solution)/shard_map/ppermute | solution.py:394
  46.0 3.3 %collective-permute-start.5 = (f32[312,256]{1,0:T(8,128)S(1)}, f32[312,256]{1,0:T(8,128)S(1)}, u32[]{:S(2)}, u32[]{:S(2)}) collective-permute-start(f32[312,256]{1,0:T(8,128)S(1)} %get-tuple-element.71), channel_id=1, source_target_pairs={{0,1},{1,0},{2,3},{3,2},{4,5},{5,4},{6,7},{7,6},{8,9},{9,8},{10,11... | collective-permute-start | bytes 958472 | tf_op jit(solution)/shard_map/ppermute | solution.py:394
  49.5 5.0 %collective-permute-start.6 = (f32[72,256]{1,0:T(8,128)S(1)}, f32[72,256]{1,0:T(8,128)S(1)}, u32[]{:S(2)}, u32[]{:S(2)}) collective-permute-start(f32[72,256]{1,0:T(8,128)S(1)} %get-tuple-element.94), channel_id=1, source_target_pairs={{0,8},{8,0},{16,24},{24,16},{1,9},{9,1},{17,25},{25,17},{2,10},{10... | collective-permute-start | bytes 221192 | tf_op jit(solution)/shard_map/ppermute | solution.py:394
  49.9 5.1 %collective-permute-start.7 = (f32[72,256]{1,0:T(8,128)S(1)}, f32[72,256]{1,0:T(8,128)S(1)}, u32[]{:S(2)}, u32[]{:S(2)}) collective-permute-start(f32[72,256]{1,0:T(8,128)S(1)} %get-tuple-element.96), channel_id=1, source_target_pairs={{0,16},{8,24},{16,0},{24,8},{1,17},{9,25},{17,1},{25,9},{2,18},{10... | collective-permute-start | bytes 221192 | tf_op jit(solution)/shard_map/ppermute | solution.py:394
  50.6 5.3 %collective-permute-start.8 = (f32[72,256]{1,0:T(8,128)S(1)}, f32[72,256]{1,0:T(8,128)S(1)}, u32[]{:S(2)}, u32[]{:S(2)}) collective-permute-start(f32[72,256]{1,0:T(8,128)S(1)} %get-tuple-element.95), channel_id=1, source_target_pairs={{0,24},{8,16},{16,8},{24,0},{1,25},{9,17},{17,9},{25,1},{2,26},{10... | collective-permute-start | bytes 221192 | tf_op jit(solution)/shard_map/ppermute | solution.py:394
  53.0 7.3 %collective-permute-start.10 = (f32[6,16,512]{2,1,0:T(8,128)S(1)}, f32[6,16,512]{2,1,0:T(8,128)S(1)}, u32[]{:S(2)}, u32[]{:S(2)}) collective-permute-start(f32[6,16,512]{2,1,0:T(8,128)S(1)} %get-tuple-element.74.stress_far), channel_id=1, source_target_pairs={{8,16},{16,8},{9,17},{17,9},{10,18},{18,10},{11,19},{19,11},{12,20... | collective-permute-start | bytes 589832 | tf_op jit(solution)/shard_map/ppermute | solution.py:388
  55.9 4.4 %collective-permute-start.9 = (f32[72,256]{1,0:T(8,128)S(1)}, f32[72,256]{1,0:T(8,128)S(1)}, u32[]{:S(2)}, u32[]{:S(2)}) collective-permute-start(f32[72,256]{1,0:T(8,128)S(1)} %fusion.1), channel_id=1, source_target_pairs={{0,2},{1,3},{2,0},{3,1},{4,6},{5,7},{6,4},{7,5},{8,10},{9,11},{10,... | collective-permute-start | bytes 221192 | tf_op jit(solution)/shard_map/ppermute | solution.py:394
  60.3 5.3 %collective-permute-start.11 = (f32[72,256]{1,0:T(8,128)S(1)}, f32[72,256]{1,0:T(8,128)S(1)}, u32[]{:S(2)}, u32[]{:S(2)}) collective-permute-start(f32[72,256]{1,0:T(8,128)S(1)} %add.39), channel_id=1, source_target_pairs={{0,4},{1,5},{2,6},{3,7},{4,0},{5,1},{6,2},{7,3},{8,12},{9,13},{10,... | collective-permute-start | bytes 221192 | tf_op jit(solution)/shard_map/ppermute | solution.py:394
  63.0 2.7 %collective-permute-start.12 = (f32[24,256]{1,0:T(8,128)S(1)}, f32[24,256]{1,0:T(8,128)S(1)}, u32[]{:S(2)}, u32[]{:S(2)}) collective-permute-start(f32[24,256]{1,0:T(8,128)S(1)} %get-tuple-element.76), channel_id=1, source_target_pairs={{1,2},{2,1},{3,4},{4,3},{5,6},{6,5},{9,10},{10,9},{11,12},{12,11},... | collective-permute-start | bytes 73736 | tf_op jit(solution)/shard_map/ppermute | solution.py:388
  65.7 5.7 %collective-permute-start.13 = (f32[72,256]{1,0:T(8,128)S(1)}, f32[72,256]{1,0:T(8,128)S(1)}, u32[]{:S(2)}, u32[]{:S(2)}) collective-permute-start(f32[72,256]{1,0:T(8,128)S(1)} %add.40), channel_id=1, source_target_pairs={{0,8},{8,0},{16,24},{24,16},{1,9},{9,1},{17,25},{25,17},{2,10},{10... | collective-permute-start | bytes 221192 | tf_op jit(solution)/shard_map/ppermute | solution.py:394
  67.8 4.5 %collective-permute-start.14 = (f32[72,256]{1,0:T(8,128)S(1)}, f32[72,256]{1,0:T(8,128)S(1)}, u32[]{:S(2)}, u32[]{:S(2)}) collective-permute-start(f32[72,256]{1,0:T(8,128)S(1)} %add.40), channel_id=1, source_target_pairs={{0,16},{8,24},{16,0},{24,8},{1,17},{9,25},{17,1},{25,9},{2,18},{10... | collective-permute-start | bytes 221192 | tf_op jit(solution)/shard_map/ppermute | solution.py:394
  68.7 5.5 %collective-permute-start.15 = (f32[72,256]{1,0:T(8,128)S(1)}, f32[72,256]{1,0:T(8,128)S(1)}, u32[]{:S(2)}, u32[]{:S(2)}) collective-permute-start(f32[72,256]{1,0:T(8,128)S(1)} %add.40), channel_id=1, source_target_pairs={{0,24},{8,16},{16,8},{24,0},{1,25},{9,17},{17,9},{25,1},{2,26},{10... | collective-permute-start | bytes 221192 | tf_op jit(solution)/shard_map/ppermute | solution.py:394
  74.3 1.6 %collective-permute-start.16 = (f32[4,72,256]{2,1,0:T(8,128)S(1)}, f32[4,72,256]{2,1,0:T(8,128)S(1)}, u32[]{:S(2)}, u32[]{:S(2)}) collective-permute-start(f32[4,72,256]{2,1,0:T(8,128)S(1)} %pad_maximum_fusion.mine), channel_id=1, source_target_pairs={{0,1},{1,0},{2,3},{3,2},{4,5},{5,4},{6,7},{7,6},{8,9},{9,8},{10,11... | collective-permute-start | bytes 884744 | tf_op jit(solution)/shard_map/ppermute | solution.py:394

commit v6 on v5

--- a/solution.py
+++ b/solution.py
@@ -75,20 +75,26 @@
 
 
 def faces_kernel(rows, *refs):
-    sources, outs, targets, sems = refs[:5], refs[5:9], refs[9:14], refs[14]
+    sources, outs, targets, sems = refs[:6], refs[6:12], refs[12:18], refs[18]
     copies = fetch(sources, targets, sems)
     near, side = near_first()
     for copy in copies:
         copy.wait()
-    x_pair, x_next, y_pair, y_next = outs
-    table, material, displacement, velocity, cotangent = targets
+    x_pair, x_next, y_pair, y_next, local, speed = outs
+    table, material, phase, displacement, velocity, cotangent = targets
     for k, plane in enumerate((near, 1 - near)):
         own = pl.ds(pl.multiple_of(plane * rows, rows), rows)
         occupied, density = step_factor(table, material[own])
+        local[k, 6] = occupied * pick(table, 0, material[own])
+        local[k, 7] = two_pi * phase[own].astype(f32) / PHASES
         for i in range(3):
             carried = time_step * occupied * cotangent[i, own] / density
             moving = velocity[i, own]
+            if not k:
+                speed[i] = moving
             for slot, field in ((i, displacement[i, own]), (3 + i, carried), (6 + i, moving)):
+                if slot < 6:
+                    local[k, slot] = field
                 if k:
                     x_next[slot] = field
                 elif slot < 6:
@@ -114,54 +120,55 @@
     return jnp.where(side == 0, following, pair), jnp.where(side == 0, pair, following)
 
 
+def weights_kernel(*refs):
+    sources, outs, refs = refs[:6], refs[7:15], refs[15:]
+    b_out, w_inT, b_in, b_mid, w_out, sems, wide = refs
+    win, winT, wmidT, wout, woutT, bias, w_mid, bias_out = outs
+    for copy in fetch(sources, (b_out, w_inT, b_in, b_mid, w_out, w_mid), sems):
+        copy.wait()
+    rowid = lax.broadcasted_iota(jnp.int32, (16, 128), 0)
+    wide[...] = jnp.zeros_like(wide)
+    wide[:FEAT] = w_inT[...].astype(f32)
+    winT[...] = wide[:16].astype(bf16)
+    win[...] = wide[...].T[:, :16].astype(bf16)
+    wide[...] = jnp.zeros_like(wide)
+    wide[:OUT] = w_out[...].astype(f32)
+    wout[...] = wide[:16].astype(bf16)
+    woutT[...] = wide[...].T[:, :16].astype(bf16)
+    for k in range(2):
+        wmidT[k] = w_mid[k].astype(f32).T.astype(bf16)
+    for k, row in enumerate((b_in[...], b_mid[0:1], b_mid[1:2])):
+        bias[k] = jnp.broadcast_to(row, (128, HID)).T
+    column = jnp.zeros((16, 128), f32)
+    for k in range(OUT):
+        column = jnp.where(rowid == k, b_out[k], column)
+    bias_out[...] = column
+
+
 def network_kernel(order, rows, block, *refs):
-    sources, refs = refs[: 13 - order * 5], refs[13 - order * 5 :]
-    (edge, y_pair, y_next), refs = refs[:3], refs[3:]
+    clock, edge, y_pair, y_next, local, *refs = refs
+    (win, winT, wmidT, wout, woutT, bias, w_mid, bias_out), refs = refs[:8], refs[8:]
     if order:
-        faces_first, given, refs = refs[:2], refs[2:13], refs[13:]
+        faces_first, given, refs = refs[:2], refs[2:7], refs[7:]
         (sx, s_next, rest, kept_half, sent), refs = refs[:5], refs[5:]
     else:
-        (sx, s_pair, s_next, rest), kept, refs = refs[:4], refs[4:15], refs[15:]
-    targets, sems, refs = refs[: len(sources)], refs[len(sources)], refs[len(sources) + 1 :]
+        speed, sx, s_pair, s_next, rest, *refs = refs
+        given, refs = refs[:5], refs[5:]
     grid_in, grid_delta, feats, delta, net, back, wide, small, *refs = refs
-    copies = fetch(sources, targets, sems)
     near, side = near_first()
     if order:
         acc_mid, acc_in, acc_out, acc_b, acc_bo = refs
-        win, winT, wmidT, wout, woutT, bias = given[5:]
-        for ref, source in zip(refs, given[:5]):
+        for ref, source in zip(refs, given):
             ref[...] = source[...]
     else:
-        acc_mid, acc_in, acc_out, acc_b, acc_bo = kept[:5]
-        win, winT, wmidT, wout, woutT, bias = kept[5:]
-        for ref in kept[:5]:
+        acc_mid, acc_in, acc_out, acc_b, acc_bo = given
+        for ref in given:
             ref[...] = jnp.zeros_like(ref)
-    for copy in copies:
-        copy.wait()
-    table, clock, b_out, material, phase, displacement, cotangent, w_mid = targets[:8]
-    lanes = material.shape[1]
+    lanes = local.shape[3]
     tiles = lanes // 128
     voxels = rows * lanes
     plane = 1 - near if order else near
-    own = pl.ds(pl.multiple_of(plane * rows, rows), rows)
-    across = pl.ds(pl.multiple_of((1 - plane) * rows, rows), rows)
-    occupied, _ = step_factor(table, material[own])
-    strength = occupied * pick(table, 0, material[own])
-
-    if not order:
-        w_inT, b_in, b_mid, w_out = targets[8:12]
-        wide[...] = jnp.zeros_like(wide)
-        wide[:FEAT] = w_inT[...].astype(f32)
-        winT[...] = wide[:16].astype(bf16)
-        win[...] = wide[...].T[:, :16].astype(bf16)
-        wide[...] = jnp.zeros_like(wide)
-        wide[:OUT] = w_out[...].astype(f32)
-        wout[...] = wide[:16].astype(bf16)
-        woutT[...] = wide[...].T[:, :16].astype(bf16)
-        for k in range(2):
-            wmidT[k] = w_mid[k].astype(f32).T.astype(bf16)
-        for k, row in enumerate((b_in[...], b_mid[0:1], b_mid[1:2])):
-            bias[k] = jnp.broadcast_to(row, (128, HID)).T
+    strength = local[order, 6]
 
     def put(ref, slot, field):
         for t in range(tiles):
@@ -179,16 +186,12 @@
             half_diff(z_ends(mine)),
         )
 
-    def carried(rows_of, slot):
-        full, thick = step_factor(table, material[rows_of])
-        return time_step * full * cotangent[slot, rows_of] / thick
-
     for i in range(3):
-        for j, value in enumerate(strains(displacement[i, own], displacement[i, across], i)):
+        for j, value in enumerate(strains(local[order, i], local[1 - order, i], i)):
             put(grid_in, 3 * i + j, value)
-        for j, value in enumerate(strains(carried(own, i), carried(across, i), 3 + i)):
+        for j, value in enumerate(strains(local[order, 3 + i], local[1 - order, 3 + i], 3 + i)):
             put(grid_delta, 3 * i + j, strength * -value)
-    put(grid_in, 9, jnp.sin(two_pi * phase[own].astype(f32) / PHASES + clock[0]))
+    put(grid_in, 9, jnp.sin(local[order, 7] + clock[0]))
     put(grid_in, 10, jnp.ones((rows, lanes), f32))
     for slot in range(11, 16):
         put(grid_in, slot, jnp.zeros((rows, lanes), f32))
@@ -200,10 +203,7 @@
             feats[:, at] = grid_in[t, pl.ds(r, 16, stride=rows), :].astype(bf16)
             delta[:, at] = grid_delta[t, pl.ds(r, 16, stride=rows), :].astype(bf16)
 
-    rowid = lax.broadcasted_iota(jnp.int32, (16, 1), 0)
-    bias_out = jnp.zeros((16, 1), f32)
-    for k in range(OUT):
-        bias_out = jnp.where(rowid == k, b_out[k], bias_out)
+    rowid = lax.broadcasted_iota(jnp.int32, (16, 128), 0)
 
     def mul(a, b):
         return jnp.dot(a, b, preferred_element_type=f32)
@@ -227,7 +227,7 @@
         h1 = jnp.tanh(mul(win[...], f) + bias[0][:, :1]).astype(bf16)
         h2 = jnp.tanh(mul(w_mid[0], h1) + bias[1][:, :1]).astype(bf16)
         h3 = jnp.tanh(mul(w_mid[1], h2) + bias[2][:, :1]).astype(bf16)
-        net[:, at] = mul(wout[...], h3) + bias_out
+        net[:, at] = mul(wout[...], h3) + bias_out[:, :1]
         acc_out[...] += mul_t(d, h3)
         acc_bo[...] += lane_sum(d)
         d3 = (mul(woutT[...], d) * slope(h3)).astype(bf16)
@@ -279,14 +279,14 @@
             )
     if not order:
         for i in range(3):
-            sx[6 + i] = targets[12][i, own]
+            sx[6 + i] = speed[i]
         return
 
     count = kept_half.shape[0]
     part = HID // count
     small[...] = jnp.zeros_like(small)
     small[:8] = acc_in[:8]
-    small[8:16] = jnp.where(rowid[:8] < 3, acc_in[8:], 0.0)
+    small[8:16] = jnp.where(rowid[:8, :1] < 3, acc_in[8:], 0.0)
     small[16:32] = acc_out[...]
     for k in range(2):
         small[32 + k : 33 + k] = jnp.sum(acc_b[k].T, axis=0, keepdims=True)
@@ -425,18 +425,24 @@
 
     faces = pl.pallas_call(
         functools.partial(faces_kernel, rows),
-        out_shape=shapes((6, rows, lanes), (9, rows, lanes), *[(9, 2, lanes)] * 2),
-        in_specs=[HBM] * 5,
-        out_specs=[VMEM] * 4,
+        out_shape=shapes(
+            (6, rows, lanes),
+            (9, rows, lanes),
+            *[(9, 2, lanes)] * 2,
+            (2, 8, rows, lanes),
+            (3, rows, lanes),
+        ),
+        in_specs=[HBM] * 6,
+        out_specs=[VMEM] * 6,
         scratch_shapes=[
             pltpu.SMEM(material_table.shape, f32),
-            pltpu.VMEM((size, lanes), jnp.int32),
+            *[pltpu.VMEM((size, lanes), jnp.int32)] * 2,
             *[pltpu.VMEM((3, size, lanes), f32)] * 3,
-            pltpu.SemaphoreType.DMA((5,)),
+            pltpu.SemaphoreType.DMA((6,)),
         ],
         compiler_params=pltpu.CompilerParams(vmem_limit_bytes=6 << 20),
         name="faces",
-    )(*map(stay, (material_table, material, displacement, velocity, cotangent)))
+    )(*map(stay, (material_table, material, phase, displacement, velocity, cotangent)))
     x_pair = swap(faces[0], "gx", 1)
     y_pair = swap(faces[2], "gy", 1)
     y_next = swap_next(faces[3], "gy")
@@ -452,15 +458,36 @@
         ((16, HID), f32),
         ((2, HID, 128), f32),
         ((16, 128), f32),
+    ]
+    ready = [
         ((HID, 16), bf16),
         ((16, HID), bf16),
         ((2, HID, HID), bf16),
         ((16, HID), bf16),
         ((HID, 16), bf16),
         ((3, HID, 128), f32),
+        ((2, HID, HID), bf16),
+        ((16, 128), f32),
     ]
-
-    def network(order, sources, near):
+    weights = pl.pallas_call(
+        weights_kernel,
+        out_shape=[jax.ShapeDtypeStruct(*item) for item in ready],
+        in_specs=[HBM] * 6 + [VMEM],
+        out_specs=[VMEM] * 8,
+        scratch_shapes=[
+            pltpu.SMEM(b_out.shape, f32),
+            pltpu.VMEM((FEAT, HID), bf16),
+            pltpu.VMEM((1, HID), f32),
+            pltpu.VMEM((2, HID), f32),
+            pltpu.VMEM((OUT, HID), bf16),
+            pltpu.SemaphoreType.DMA((6,)),
+            pltpu.VMEM((128, HID), f32),
+        ],
+        compiler_params=pltpu.CompilerParams(vmem_limit_bytes=6 << 20),
+        name="weights",
+    )(*map(stay, (b_out, w_in.T, b_in.reshape(1, HID), b_mid, w_out, w_mid)), faces[5])
+
+    def network(order, near):
         outs = [jax.ShapeDtypeStruct(*item) for item in handed]
         faces_out = [(6, 1, lanes)] * 2
         if order:
@@ -472,12 +499,9 @@
                 (9 - 3 * order, rows, lanes), *faces_out, (6, rows, lanes)
             )
             + outs,
-            in_specs=[HBM] * len(sources) + [VMEM] * len(near),
+            in_specs=[SMEM] + [VMEM] * len(near),
             out_specs=[VMEM] * (2 + len(faces_out) + len(outs)),
             scratch_shapes=[
-                *[pltpu.SMEM(item.shape, f32) for item in sources[:3]],
-                *[pltpu.VMEM(item.shape, item.dtype) for item in sources[3:]],
-                pltpu.SemaphoreType.DMA((len(sources),)),
                 *[pltpu.VMEM((lanes // 128, 16 * rows, 128), f32)] * 2,
                 *[pltpu.VMEM((16, voxels), bf16)] * 2,
                 *[pltpu.VMEM((16, voxels), f32)] * 2,
@@ -492,16 +516,11 @@
                 transcendentals=3 * HID * voxels,
             ),
             name="network",
-        )(*map(stay, sources), *near)
-
-    common = [material_table, clock, b_out, material, phase, displacement, cotangent, w_mid]
-    first = network(
-        0,
-        common + [w_in.T, b_in.reshape(1, HID), b_mid, w_out, velocity],
-        [x_pair, y_pair, y_next],
-    )
+        )(clock, *near)
+
+    first = network(0, [x_pair, y_pair, y_next, faces[4], *weights, faces[5]])
     sx_pair = swap(first[0], "gx", 1)
-    second = network(1, common, [x_next, y_pair, y_next, *first[1:3], *first[4:]])
+    second = network(1, [x_next, y_pair, y_next, faces[4], *weights, *first[1:3], *first[4:]])
     sx_next = swap_next(second[0], "gx")
 
     index = lax.axis_index("gx")

time: 78 us -> 76.2 us (0.977)
  Pallas kernels: 38.7 us -> 36.9 us
  waiting for transfers between devices: 15.2 us -> 13.8 us
  starting transfers between devices: 21.6 us -> 22.9 us
    pallas_call x2, Pallas kernels: 34.3 us -> 31.1 us  [network(): pl.pallas_call(functools.partial(network_kernel, order, rows, block), out...]
    ppermute x13, waiting for transfers between devices: 15.2 us -> 13.8 us  [swap(): lax.ppermute(value, axis, [(i, i ^ mask) for i in range(lax.axis_size(axi...]
    pallas_call x0 -> x1, Pallas kernels: none -> 1.36 us  [body(): pl.pallas_call(weights_kernel, out_shape=[jax.ShapeDtypeStruct(*item) for...]
    ppermute x13, starting transfers between devices: 18.9 us -> 20.3 us  [swap(): lax.ppermute(value, axis, [(i, i ^ mask) for i in range(lax.axis_size(axi...]
  transfers between devices with their start and end apart: 17 -> 17, of which waited for: 10 -> 10; matrix products, arithmetic and copies ran while one was open for 0% -> 0% of each run, Pallas kernels for 47% -> 46%
where the time goes in v6:
time: 76.2 us; the launch traced here: 75.2 us
  Pallas kernels  36.9 us (48%)
  starting transfers between devices  22.9 us (30%)
  waiting for transfers between devices  13.8 us (18%)
  between operations  1.41 us (2%)
    pallas_call x2, Pallas kernels, network(): pl.pallas_call(functools.partial(network_kernel, order, rows, block), out...  31.1 us
    ppermute x13, starting transfers between devices, swap(): lax.ppermute(value, axis, [(i, i ^ mask) for i in range(lax.axis_size(axi...  20.3 us
    ppermute x13, waiting for transfers between devices, swap(): lax.ppermute(value, axis, [(i, i ^ mask) for i in range(lax.axis_size(axi...  13.8 us
    ppermute x4, starting transfers between devices, swap_next(): lax.ppermute(value, axis, [(i, i + 1 if i % 2 else i - 1) for i in range(...  2.64 us
    pallas_call x1, Pallas kernels, body(): pl.pallas_call(functools.partial(fields_kernel, rows), out_shape=shapes(*...  1.96 us
  transfers between devices with their start and end apart: 17, of which 10 were waited for; matrix products, arithmetic and copies ran while one was open for 0% of the time, Pallas kernels for 46%

profile of v6, /device:TPU:0, one launch (start us, length us, event | category | flops | bytes accessed | tf_op | source)
XLA Modules:
  0.0 75.2 jit_solution(4061460597479360709)
XLA Ops:
  0.6 1.4 %faces.1 = (f32[6,16,512]{2,1,0:T(8,128)S(1)}, f32[9,16,512]{2,1,0:T(8,128)S(1)}, f32[9,2,512]{2,1,0:T(2,128)S(1)}, f32[9,2,512]{2,1,0:T(2,128)S(1)}, f32[2,8,16...) custom-call(f32[2,4]{1,0:T(2,128)} %table.1, s32[32,512]{1,0:T(8,128)} %bitcast.34, s32[32,512]{1,0:T(8,128)} %bitcast.41, ...), custom_call_target="tpu_custom_call" | custom-call | tf_op jit(solution)/shard_map/faces/pallas_call | solution.py:426
  2.0 3.0 %collective-permute-start.3 = (f32[6,16,512]{2,1,0:T(8,128)S(1)}, f32[6,16,512]{2,1,0:T(8,128)S(1)}, u32[]{:S(2)}, u32[]{:S(2)}) collective-permute-start(f32[6,16,512]{2,1,0:T(8,128)S(1)} %get-tuple-element.68), channel_id=1, source_target_pairs={{0,8},{8,0},{16,24},{24,16},{1,9},{9,1},{17,25},{25,17},{2,10},{10... | collective-permute-start | bytes 589832 | tf_op jit(solution)/shard_map/ppermute | solution.py:394
  7.0 1.4 %weights.1 = (bf16[256,16]{1,0:T(8,128)(2,1)S(1)}, bf16[16,256]{1,0:T(8,128)(2,1)S(1)}, bf16[2,256,256]{2,1,0:T(8,128)(2,1)S(1)}, bf16[16,256]{1,0:T(8,128)(2,1)...) custom-call(f32[9]{0:T(128)} %refs_0_.5, ...), custom_call_target="tpu_custom_call" | custom-call | tf_op jit(solution)/shard_map/weights/pallas_call | solution.py:472
  8.4 1.5 %collective-permute-done.3.refs_1_ = f32[6,16,512]{2,1,0:T(8,128)S(1)} collective-permute-done((f32[6,16,512]{2,1,0:T(8,128)S(1)}, f32[6,16,512]{2,1,0:T(8,128)S(1)}, u32[]{:S(2)}, u32[]{:S(2)}) %collective-permute-start.3) | collective-permute-done | bytes 196640 | tf_op jit(solution)/shard_map/ppermute | solution.py:394
  9.9 15.4 %network.2 = (f32[9,16,512]{2,1,0:T(8,128)S(1)}, f32[6,1,512]{2,1,0:T(1,128)S(1)}, f32[6,1,512]{2,1,0:T(1,128)S(1)}, f32[6,16,512]{2,1,0:T(8,128)S(1)}, f32[512,...) custom-call(f32[1]{0:T(128)S(6)} %copy.21.refs_0_, ...), custom_call_target="tpu_custom_call" | custom-call | flops 6681526272 | bytes 524288 | tf_op jit(solution)/shard_map/network/pallas_call | solution.py:496
  25.4 2.8 %collective-permute-start.4 = (f32[9,16,512]{2,1,0:T(8,128)S(1)}, f32[9,16,512]{2,1,0:T(8,128)S(1)}, u32[]{:S(2)}, u32[]{:S(2)}) collective-permute-start(f32[9,16,512]{2,1,0:T(8,128)S(1)} %get-tuple-element.78.stress_near), channel_id=1, source_target_pairs={{0,8},{8,0},{16,24},{24,16},{1,9},{9,1},{17,25},{25,17},{2,10},{10... | collective-permute-start | bytes 884744 | tf_op jit(solution)/shard_map/ppermute | solution.py:394
  28.2 15.7 %network.3 = (f32[6,16,512]{2,1,0:T(8,128)S(1)}, f32[24,256]{1,0:T(8,128)S(1)}, f32[6,16,512]{2,1,0:T(8,128)S(1)}, f32[4,72,256]{2,1,0:T(8,128)S(1)}, f32[312,256]{1,0:T(8,128)S(1)}) custom-call(f32[1]{0:T(128)S(6)} %copy.21.refs_0_, f32[9,16,512]{2,1,0:T(8,128)S(1)} %collective-permute-done.refs_1_.x_next, ...), custom_call_target="tpu_custom_call" | custom-call | flops 6681526272 | bytes 524288 | tf_op jit(solution)/shard_map/network/pallas_call | solution.py:496
  43.9 2.4 %collective-permute-start.5 = (f32[312,256]{1,0:T(8,128)S(1)}, f32[312,256]{1,0:T(8,128)S(1)}, u32[]{:S(2)}, u32[]{:S(2)}) collective-permute-start(f32[312,256]{1,0:T(8,128)S(1)} %get-tuple-element.79), channel_id=1, source_target_pairs={{0,1},{1,0},{2,3},{3,2},{4,5},{5,4},{6,7},{7,6},{8,9},{9,8},{10,11... | collective-permute-start | bytes 958472 | tf_op jit(solution)/shard_map/ppermute | solution.py:394
  46.3 1.2 %collective-permute-done.5.sy_pair = f32[312,256]{1,0:T(8,128)S(1)} collective-permute-done((f32[312,256]{1,0:T(8,128)S(1)}, f32[312,256]{1,0:T(8,128)S(1)}, u32[]{:S(2)}, u32[]{:S(2)}) %collective-permute-start.5) | collective-permute-done | bytes 319520 | tf_op jit(solution)/shard_map/ppermute | solution.py:394
  48.1 0.7 collective-permute-start.7
  48.8 2.5 %collective-permute-start.8 = (f32[72,256]{1,0:T(8,128)S(1)}, f32[72,256]{1,0:T(8,128)S(1)}, u32[]{:S(2)}, u32[]{:S(2)}) collective-permute-start(f32[72,256]{1,0:T(8,128)S(1)} %get-tuple-element.103), channel_id=1, source_target_pairs={{0,24},{8,16},{16,8},{24,0},{1,25},{9,17},{17,9},{25,1},{2,26},{10... | collective-permute-start | bytes 221192 | tf_op jit(solution)/shard_map/ppermute | solution.py:394
  51.9 0.7 collective-permute-done.6
  53.2 0.8 %collective-permute-done.8 = f32[72,256]{1,0:T(8,128)S(1)} collective-permute-done((f32[72,256]{1,0:T(8,128)S(1)}, f32[72,256]{1,0:T(8,128)S(1)}, u32[]{:S(2)}, u32[]{:S(2)}) %collective-permute-start.8) | collective-permute-done | bytes 73760 | tf_op jit(solution)/shard_map/ppermute | solution.py:394
  54.1 1.6 %collective-permute-start.9 = (f32[72,256]{1,0:T(8,128)S(1)}, f32[72,256]{1,0:T(8,128)S(1)}, u32[]{:S(2)}, u32[]{:S(2)}) collective-permute-start(f32[72,256]{1,0:T(8,128)S(1)} %fusion.1), channel_id=1, source_target_pairs={{0,2},{1,3},{2,0},{3,1},{4,6},{5,7},{6,4},{7,5},{8,10},{9,11},{10,... | collective-permute-start | bytes 221192 | tf_op jit(solution)/shard_map/ppermute | solution.py:394
  55.7 2.8 %collective-permute-done.9 = f32[72,256]{1,0:T(8,128)S(1)} collective-permute-done((f32[72,256]{1,0:T(8,128)S(1)}, f32[72,256]{1,0:T(8,128)S(1)}, u32[]{:S(2)}, u32[]{:S(2)}) %collective-permute-start.9) | collective-permute-done | bytes 73760 | tf_op jit(solution)/shard_map/ppermute | solution.py:394
  58.5 2.7 %collective-permute-start.11 = (f32[72,256]{1,0:T(8,128)S(1)}, f32[72,256]{1,0:T(8,128)S(1)}, u32[]{:S(2)}, u32[]{:S(2)}) collective-permute-start(f32[72,256]{1,0:T(8,128)S(1)} %add.39), channel_id=1, source_target_pairs={{0,4},{1,5},{2,6},{3,7},{4,0},{5,1},{6,2},{7,3},{8,12},{9,13},{10,... | collective-permute-start | bytes 221192 | tf_op jit(solution)/shard_map/ppermute | solution.py:394
  61.8 2.0 %collective-permute-done.11 = f32[72,256]{1,0:T(8,128)S(1)} collective-permute-done((f32[72,256]{1,0:T(8,128)S(1)}, f32[72,256]{1,0:T(8,128)S(1)}, u32[]{:S(2)}, u32[]{:S(2)}) %collective-permute-start.11) | collective-permute-done | bytes 73760 | tf_op jit(solution)/shard_map/ppermute | solution.py:394
  63.8 2.2 %collective-permute-start.13 = (f32[72,256]{1,0:T(8,128)S(1)}, f32[72,256]{1,0:T(8,128)S(1)}, u32[]{:S(2)}, u32[]{:S(2)}) collective-permute-start(f32[72,256]{1,0:T(8,128)S(1)} %add.40), channel_id=1, source_target_pairs={{0,8},{8,0},{16,24},{24,16},{1,9},{9,1},{17,25},{25,17},{2,10},{10... | collective-permute-start | bytes 221192 | tf_op jit(solution)/shard_map/ppermute | solution.py:394
  66.0 0.9 %collective-permute-start.14 = (f32[72,256]{1,0:T(8,128)S(1)}, f32[72,256]{1,0:T(8,128)S(1)}, u32[]{:S(2)}, u32[]{:S(2)}) collective-permute-start(f32[72,256]{1,0:T(8,128)S(1)} %add.40), channel_id=1, source_target_pairs={{0,16},{8,24},{16,0},{24,8},{1,17},{9,25},{17,1},{25,9},{2,18},{10... | collective-permute-start | bytes 221192 | tf_op jit(solution)/shard_map/ppermute | solution.py:394
  67.6 2.0 %fields.1 = (f32[3,32,512]{2,1,0:T(8,128)}, f32[3,32,512]{2,1,0:T(8,128)}) custom-call(f32[2,4]{1,0:T(2,128)} %table.1, s32[32,512]{1,0:T(8,128)} %bitcast.35, f32[3,32,512]{2,1,0:T(8,128)} %bitcast.32, f32[9,16,512]{2,1,0:T(8,128)S(1)} %get-tuple-element.78.stress_near, f32[6,16,512]{2,1,0:T(8,128)S(1)} %get-tuple-element.82.stress_far, ...), custom_call_target="tpu_custom_call" | custom-call | tf_op jit(solution)/shard_map/fields/pallas_call | solution.py:546
  69.5 1.0 %collective-permute-done.14 = f32[72,256]{1,0:T(8,128)S(1)} collective-permute-done((f32[72,256]{1,0:T(8,128)S(1)}, f32[72,256]{1,0:T(8,128)S(1)}, u32[]{:S(2)}, u32[]{:S(2)}) %collective-permute-start.14) | collective-permute-done | bytes 73760 | tf_op jit(solution)/shard_map/ppermute | solution.py:394
  70.6 1.8 %collective-permute-done.15 = f32[72,256]{1,0:T(8,128)S(1)} collective-permute-done((f32[72,256]{1,0:T(8,128)S(1)}, f32[72,256]{1,0:T(8,128)S(1)}, u32[]{:S(2)}, u32[]{:S(2)}) %collective-permute-start.15) | collective-permute-done | bytes 73760 | tf_op jit(solution)/shard_map/ppermute | solution.py:394
  72.9 1.2 %collective-permute-done.16.other = f32[4,72,256]{2,1,0:T(8,128)S(1)} collective-permute-done((f32[4,72,256]{2,1,0:T(8,128)S(1)}, f32[4,72,256]{2,1,0:T(8,128)S(1)}, u32[]{:S(2)}, u32[]{:S(2)}) %collective-permute-start.16) | collective-permute-done | bytes 294944 | tf_op jit(solution)/shard_map/ppermute | solution.py:394
  74.1 1.1 %finish.1 = (f32[10,256]{1,0:T(8,128)}, f32[1,256]{1,0:T(1,128)}, f32[512,256]{1,0:T(8,128)}, f32[2,256]{1,0:T(2,128)}, f32[9,256]{1,0:T(8,128)}, /*index=5*/f32[1,9]{1,0:T(1,128)}) custom-call(f32[4,72,256]{2,1,0:T(8,128)S(1)} %pad_maximum_fusion.mine, f32[4,72,256]{2,1,0:T(8,128)S(1)} %collective-permute-done.16.other), custom_call_target="tpu_custom_call" | custom-call | tf_op jit(solution)/shard_map/finish/pallas_call | solution.py:571
  (23 shorter events, 4.9 us)
Async XLA Ops:
  2.0 7.9 %collective-permute-start.3 = (f32[6,16,512]{2,1,0:T(8,128)S(1)}, f32[6,16,512]{2,1,0:T(8,128)S(1)}, u32[]{:S(2)}, u32[]{:S(2)}) collective-permute-start(f32[6,16,512]{2,1,0:T(8,128)S(1)} %get-tuple-element.68), channel_id=1, source_target_pairs={{0,8},{8,0},{16,24},{24,16},{1,9},{9,1},{17,25},{25,17},{2,10},{10... | collective-permute-start | bytes 589832 | tf_op jit(solution)/shard_map/ppermute | solution.py:394
  5.0 3.4 %collective-permute-start.1 = (f32[9,2,512]{2,1,0:T(2,128)S(1)}, f32[9,2,512]{2,1,0:T(2,128)S(1)}, u32[]{:S(2)}, u32[]{:S(2)}) collective-permute-start(f32[9,2,512]{2,1,0:T(2,128)S(1)} %get-tuple-element.56), channel_id=1, source_target_pairs={{0,1},{1,0},{2,3},{3,2},{4,5},{5,4},{6,7},{7,6},{8,9},{9,8},{10,11... | collective-permute-start | bytes 110600 | tf_op jit(solution)/shard_map/ppermute | solution.py:394
  5.0 3.4 %collective-permute-start.2 = (f32[9,2,512]{2,1,0:T(2,128)S(1)}, f32[9,2,512]{2,1,0:T(2,128)S(1)}, u32[]{:S(2)}, u32[]{:S(2)}) collective-permute-start(f32[9,2,512]{2,1,0:T(2,128)S(1)} %get-tuple-element.57), channel_id=1, source_target_pairs={{1,2},{2,1},{3,4},{4,3},{5,6},{6,5},{9,10},{10,9},{11,12},{12,11},... | collective-permute-start | bytes 110600 | tf_op jit(solution)/shard_map/ppermute | solution.py:388
  5.7 22.5 %collective-permute-start = (f32[9,16,512]{2,1,0:T(8,128)S(1)}, f32[9,16,512]{2,1,0:T(8,128)S(1)}, u32[]{:S(2)}, u32[]{:S(2)}) collective-permute-start(f32[9,16,512]{2,1,0:T(8,128)S(1)} %get-tuple-element.55), channel_id=1, source_target_pairs={{8,16},{16,8},{9,17},{17,9},{10,18},{18,10},{11,19},{19,11},{12,20... | collective-permute-start | bytes 884744 | tf_op jit(solution)/shard_map/ppermute | solution.py:388
  25.4 18.5 %collective-permute-start.4 = (f32[9,16,512]{2,1,0:T(8,128)S(1)}, f32[9,16,512]{2,1,0:T(8,128)S(1)}, u32[]{:S(2)}, u32[]{:S(2)}) collective-permute-start(f32[9,16,512]{2,1,0:T(8,128)S(1)} %get-tuple-element.78.stress_near), channel_id=1, source_target_pairs={{0,8},{8,0},{16,24},{24,16},{1,9},{9,1},{17,25},{25,17},{2,10},{10... | collective-permute-start | bytes 884744 | tf_op jit(solution)/shard_map/ppermute | solution.py:394
  43.9 3.7 %collective-permute-start.5 = (f32[312,256]{1,0:T(8,128)S(1)}, f32[312,256]{1,0:T(8,128)S(1)}, u32[]{:S(2)}, u32[]{:S(2)}) collective-permute-start(f32[312,256]{1,0:T(8,128)S(1)} %get-tuple-element.79), channel_id=1, source_target_pairs={{0,1},{1,0},{2,3},{3,2},{4,5},{5,4},{6,7},{7,6},{8,9},{9,8},{10,11... | collective-permute-start | bytes 958472 | tf_op jit(solution)/shard_map/ppermute | solution.py:394
  47.7 5.0 %collective-permute-start.6 = (f32[72,256]{1,0:T(8,128)S(1)}, f32[72,256]{1,0:T(8,128)S(1)}, u32[]{:S(2)}, u32[]{:S(2)}) collective-permute-start(f32[72,256]{1,0:T(8,128)S(1)} %get-tuple-element.102), channel_id=1, source_target_pairs={{0,8},{8,0},{16,24},{24,16},{1,9},{9,1},{17,25},{25,17},{2,10},{10... | collective-permute-start | bytes 221192 | tf_op jit(solution)/shard_map/ppermute | solution.py:394
  48.1 5.1 %collective-permute-start.7 = (f32[72,256]{1,0:T(8,128)S(1)}, f32[72,256]{1,0:T(8,128)S(1)}, u32[]{:S(2)}, u32[]{:S(2)}) collective-permute-start(f32[72,256]{1,0:T(8,128)S(1)} %get-tuple-element.104), channel_id=1, source_target_pairs={{0,16},{8,24},{16,0},{24,8},{1,17},{9,25},{17,1},{25,9},{2,18},{10... | collective-permute-start | bytes 221192 | tf_op jit(solution)/shard_map/ppermute | solution.py:394
  48.8 5.3 %collective-permute-start.8 = (f32[72,256]{1,0:T(8,128)S(1)}, f32[72,256]{1,0:T(8,128)S(1)}, u32[]{:S(2)}, u32[]{:S(2)}) collective-permute-start(f32[72,256]{1,0:T(8,128)S(1)} %get-tuple-element.103), channel_id=1, source_target_pairs={{0,24},{8,16},{16,8},{24,0},{1,25},{9,17},{17,9},{25,1},{2,26},{10... | collective-permute-start | bytes 221192 | tf_op jit(solution)/shard_map/ppermute | solution.py:394
  51.2 7.3 %collective-permute-start.10 = (f32[6,16,512]{2,1,0:T(8,128)S(1)}, f32[6,16,512]{2,1,0:T(8,128)S(1)}, u32[]{:S(2)}, u32[]{:S(2)}) collective-permute-start(f32[6,16,512]{2,1,0:T(8,128)S(1)} %get-tuple-element.82.stress_far), channel_id=1, source_target_pairs={{8,16},{16,8},{9,17},{17,9},{10,18},{18,10},{11,19},{19,11},{12,20... | collective-permute-start | bytes 589832 | tf_op jit(solution)/shard_map/ppermute | solution.py:388
  54.1 4.4 %collective-permute-start.9 = (f32[72,256]{1,0:T(8,128)S(1)}, f32[72,256]{1,0:T(8,128)S(1)}, u32[]{:S(2)}, u32[]{:S(2)}) collective-permute-start(f32[72,256]{1,0:T(8,128)S(1)} %fusion.1), channel_id=1, source_target_pairs={{0,2},{1,3},{2,0},{3,1},{4,6},{5,7},{6,4},{7,5},{8,10},{9,11},{10,... | collective-permute-start | bytes 221192 | tf_op jit(solution)/shard_map/ppermute | solution.py:394
  58.5 5.3 %collective-permute-start.11 = (f32[72,256]{1,0:T(8,128)S(1)}, f32[72,256]{1,0:T(8,128)S(1)}, u32[]{:S(2)}, u32[]{:S(2)}) collective-permute-start(f32[72,256]{1,0:T(8,128)S(1)} %add.39), channel_id=1, source_target_pairs={{0,4},{1,5},{2,6},{3,7},{4,0},{5,1},{6,2},{7,3},{8,12},{9,13},{10,... | collective-permute-start | bytes 221192 | tf_op jit(solution)/shard_map/ppermute | solution.py:394
  61.2 2.7 %collective-permute-start.12 = (f32[24,256]{1,0:T(8,128)S(1)}, f32[24,256]{1,0:T(8,128)S(1)}, u32[]{:S(2)}, u32[]{:S(2)}) collective-permute-start(f32[24,256]{1,0:T(8,128)S(1)} %get-tuple-element.84), channel_id=1, source_target_pairs={{1,2},{2,1},{3,4},{4,3},{5,6},{6,5},{9,10},{10,9},{11,12},{12,11},... | collective-permute-start | bytes 73736 | tf_op jit(solution)/shard_map/ppermute | solution.py:388
  63.8 5.7 %collective-permute-start.13 = (f32[72,256]{1,0:T(8,128)S(1)}, f32[72,256]{1,0:T(8,128)S(1)}, u32[]{:S(2)}, u32[]{:S(2)}) collective-permute-start(f32[72,256]{1,0:T(8,128)S(1)} %add.40), channel_id=1, source_target_pairs={{0,8},{8,0},{16,24},{24,16},{1,9},{9,1},{17,25},{25,17},{2,10},{10... | collective-permute-start | bytes 221192 | tf_op jit(solution)/shard_map/ppermute | solution.py:394
  66.0 4.5 %collective-permute-start.14 = (f32[72,256]{1,0:T(8,128)S(1)}, f32[72,256]{1,0:T(8,128)S(1)}, u32[]{:S(2)}, u32[]{:S(2)}) collective-permute-start(f32[72,256]{1,0:T(8,128)S(1)} %add.40), channel_id=1, source_target_pairs={{0,16},{8,24},{16,0},{24,8},{1,17},{9,25},{17,1},{25,9},{2,18},{10... | collective-permute-start | bytes 221192 | tf_op jit(solution)/shard_map/ppermute | solution.py:394
  66.9 5.5 %collective-permute-start.15 = (f32[72,256]{1,0:T(8,128)S(1)}, f32[72,256]{1,0:T(8,128)S(1)}, u32[]{:S(2)}, u32[]{:S(2)}) collective-permute-start(f32[72,256]{1,0:T(8,128)S(1)} %add.40), channel_id=1, source_target_pairs={{0,24},{8,16},{16,8},{24,0},{1,25},{9,17},{17,9},{25,1},{2,26},{10... | collective-permute-start | bytes 221192 | tf_op jit(solution)/shard_map/ppermute | solution.py:394
  72.5 1.6 %collective-permute-start.16 = (f32[4,72,256]{2,1,0:T(8,128)S(1)}, f32[4,72,256]{2,1,0:T(8,128)S(1)}, u32[]{:S(2)}, u32[]{:S(2)}) collective-permute-start(f32[4,72,256]{2,1,0:T(8,128)S(1)} %pad_maximum_fusion.mine), channel_id=1, source_target_pairs={{0,1},{1,0},{2,3},{3,2},{4,5},{5,4},{6,7},{7,6},{8,9},{9,8},{10,11... | collective-permute-start | bytes 884744 | tf_op jit(solution)/shard_map/ppermute | solution.py:394

commit v7 on v6

--- a/solution.py
+++ b/solution.py
@@ -241,7 +241,7 @@
         back[:, at] = mul(winT[...], d1)
         return carry
 
-    lax.fori_loop(0, voxels // block, step, 0)
+    lax.fori_loop(0, voxels // block, step, 0, unroll=2)
 
     for r in range(rows):
         for t in range(tiles):
@@ -449,7 +449,7 @@
     x_next = swap_next(faces[1], "gx")
 
     voxels = rows * lanes
-    block = 4096
+    block = 2048
     while voxels % block:
         block //= 2
     handed = [

time: 76.2 us -> 73.5 us (0.965)
  Pallas kernels: 36.9 us -> 34.2 us
    pallas_call x2, Pallas kernels: 31.1 us -> 28.4 us  [network(): pl.pallas_call(functools.partial(network_kernel, order, rows, block), out...]
  transfers between devices with their start and end apart: 17 -> 17, of which waited for: 10 -> 10; matrix products, arithmetic and copies ran while one was open for 0% -> 0% of each run, Pallas kernels for 46% -> 44%
where the time goes in v7:
time: 73.5 us; the launch traced here: 72.4 us
  Pallas kernels  34.2 us (47%)
  starting transfers between devices  22.9 us (31%)
  waiting for transfers between devices  13.8 us (19%)
  between operations  1.41 us (2%)
    pallas_call x2, Pallas kernels, network(): pl.pallas_call(functools.partial(network_kernel, order, rows, block), out...  28.4 us
    ppermute x13, starting transfers between devices, swap(): lax.ppermute(value, axis, [(i, i ^ mask) for i in range(lax.axis_size(axi...  20.3 us
    ppermute x13, waiting for transfers between devices, swap(): lax.ppermute(value, axis, [(i, i ^ mask) for i in range(lax.axis_size(axi...  13.8 us
    ppermute x4, starting transfers between devices, swap_next(): lax.ppermute(value, axis, [(i, i + 1 if i % 2 else i - 1) for i in range(...  2.64 us
    pallas_call x1, Pallas kernels, body(): pl.pallas_call(functools.partial(fields_kernel, rows), out_shape=shapes(*...  1.96 us
  transfers between devices with their start and end apart: 17, of which 10 were waited for; matrix products, arithmetic and copies ran while one was open for 0% of the time, Pallas kernels for 44%

profile of v7, /device:TPU:0, one launch (start us, length us, event | category | flops | bytes accessed | tf_op | source)
XLA Modules:
  0.0 72.4 jit_solution(12013812926747881969)
XLA Ops:
  0.6 1.4 %faces.1 = (f32[6,16,512]{2,1,0:T(8,128)S(1)}, f32[9,16,512]{2,1,0:T(8,128)S(1)}, f32[9,2,512]{2,1,0:T(2,128)S(1)}, f32[9,2,512]{2,1,0:T(2,128)S(1)}, f32[2,8,16...) custom-call(f32[2,4]{1,0:T(2,128)} %table.1, s32[32,512]{1,0:T(8,128)} %bitcast.34, s32[32,512]{1,0:T(8,128)} %bitcast.41, ...), custom_call_target="tpu_custom_call" | custom-call | tf_op jit(solution)/shard_map/faces/pallas_call | solution.py:426
  2.0 3.0 %collective-permute-start.3 = (f32[6,16,512]{2,1,0:T(8,128)S(1)}, f32[6,16,512]{2,1,0:T(8,128)S(1)}, u32[]{:S(2)}, u32[]{:S(2)}) collective-permute-start(f32[6,16,512]{2,1,0:T(8,128)S(1)} %get-tuple-element.68), channel_id=1, source_target_pairs={{0,8},{8,0},{16,24},{24,16},{1,9},{9,1},{17,25},{25,17},{2,10},{10... | collective-permute-start | bytes 589832 | tf_op jit(solution)/shard_map/ppermute | solution.py:394
  7.0 1.4 %weights.1 = (bf16[256,16]{1,0:T(8,128)(2,1)S(1)}, bf16[16,256]{1,0:T(8,128)(2,1)S(1)}, bf16[2,256,256]{2,1,0:T(8,128)(2,1)S(1)}, bf16[16,256]{1,0:T(8,128)(2,1)...) custom-call(f32[9]{0:T(128)} %refs_0_.5, ...), custom_call_target="tpu_custom_call" | custom-call | tf_op jit(solution)/shard_map/weights/pallas_call | solution.py:472
  8.4 1.5 %collective-permute-done.3.refs_1_ = f32[6,16,512]{2,1,0:T(8,128)S(1)} collective-permute-done((f32[6,16,512]{2,1,0:T(8,128)S(1)}, f32[6,16,512]{2,1,0:T(8,128)S(1)}, u32[]{:S(2)}, u32[]{:S(2)}) %collective-permute-start.3) | collective-permute-done | bytes 196640 | tf_op jit(solution)/shard_map/ppermute | solution.py:394
  9.9 14.1 %network.2 = (f32[9,16,512]{2,1,0:T(8,128)S(1)}, f32[6,1,512]{2,1,0:T(1,128)S(1)}, f32[6,1,512]{2,1,0:T(1,128)S(1)}, f32[6,16,512]{2,1,0:T(8,128)S(1)}, f32[512,...) custom-call(f32[1]{0:T(128)S(6)} %copy.21.refs_0_, ...), custom_call_target="tpu_custom_call" | custom-call | flops 6681526272 | bytes 524288 | tf_op jit(solution)/shard_map/network/pallas_call | solution.py:496
  24.0 2.8 %collective-permute-start.4 = (f32[9,16,512]{2,1,0:T(8,128)S(1)}, f32[9,16,512]{2,1,0:T(8,128)S(1)}, u32[]{:S(2)}, u32[]{:S(2)}) collective-permute-start(f32[9,16,512]{2,1,0:T(8,128)S(1)} %get-tuple-element.78.stress_near), channel_id=1, source_target_pairs={{0,8},{8,0},{16,24},{24,16},{1,9},{9,1},{17,25},{25,17},{2,10},{10... | collective-permute-start | bytes 884744 | tf_op jit(solution)/shard_map/ppermute | solution.py:394
  26.8 14.3 %network.3 = (f32[6,16,512]{2,1,0:T(8,128)S(1)}, f32[24,256]{1,0:T(8,128)S(1)}, f32[6,16,512]{2,1,0:T(8,128)S(1)}, f32[4,72,256]{2,1,0:T(8,128)S(1)}, f32[312,256]{1,0:T(8,128)S(1)}) custom-call(f32[1]{0:T(128)S(6)} %copy.21.refs_0_, f32[9,16,512]{2,1,0:T(8,128)S(1)} %collective-permute-done.refs_1_.x_next, ...), custom_call_target="tpu_custom_call" | custom-call | flops 6681526272 | bytes 524288 | tf_op jit(solution)/shard_map/network/pallas_call | solution.py:496
  41.2 2.4 %collective-permute-start.5 = (f32[312,256]{1,0:T(8,128)S(1)}, f32[312,256]{1,0:T(8,128)S(1)}, u32[]{:S(2)}, u32[]{:S(2)}) collective-permute-start(f32[312,256]{1,0:T(8,128)S(1)} %get-tuple-element.79), channel_id=1, source_target_pairs={{0,1},{1,0},{2,3},{3,2},{4,5},{5,4},{6,7},{7,6},{8,9},{9,8},{10,11... | collective-permute-start | bytes 958472 | tf_op jit(solution)/shard_map/ppermute | solution.py:394
  43.6 1.2 %collective-permute-done.5.sy_pair = f32[312,256]{1,0:T(8,128)S(1)} collective-permute-done((f32[312,256]{1,0:T(8,128)S(1)}, f32[312,256]{1,0:T(8,128)S(1)}, u32[]{:S(2)}, u32[]{:S(2)}) %collective-permute-start.5) | collective-permute-done | bytes 319520 | tf_op jit(solution)/shard_map/ppermute | solution.py:394
  45.3 0.7 %collective-permute-start.7 = (f32[72,256]{1,0:T(8,128)S(1)}, f32[72,256]{1,0:T(8,128)S(1)}, u32[]{:S(2)}, u32[]{:S(2)}) collective-permute-start(f32[72,256]{1,0:T(8,128)S(1)} %get-tuple-element.104), channel_id=1, source_target_pairs={{0,16},{8,24},{16,0},{24,8},{1,17},{9,25},{17,1},{25,9},{2,18},{10... | collective-permute-start | bytes 221192 | tf_op jit(solution)/shard_map/ppermute | solution.py:394
  46.1 2.4 %collective-permute-start.8 = (f32[72,256]{1,0:T(8,128)S(1)}, f32[72,256]{1,0:T(8,128)S(1)}, u32[]{:S(2)}, u32[]{:S(2)}) collective-permute-start(f32[72,256]{1,0:T(8,128)S(1)} %get-tuple-element.103), channel_id=1, source_target_pairs={{0,24},{8,16},{16,8},{24,0},{1,25},{9,17},{17,9},{25,1},{2,26},{10... | collective-permute-start | bytes 221192 | tf_op jit(solution)/shard_map/ppermute | solution.py:394
  49.2 0.7 %collective-permute-done.6 = f32[72,256]{1,0:T(8,128)S(1)} collective-permute-done((f32[72,256]{1,0:T(8,128)S(1)}, f32[72,256]{1,0:T(8,128)S(1)}, u32[]{:S(2)}, u32[]{:S(2)}) %collective-permute-start.6) | collective-permute-done | bytes 73760 | tf_op jit(solution)/shard_map/ppermute | solution.py:394
  50.5 0.8 %collective-permute-done.8 = f32[72,256]{1,0:T(8,128)S(1)} collective-permute-done((f32[72,256]{1,0:T(8,128)S(1)}, f32[72,256]{1,0:T(8,128)S(1)}, u32[]{:S(2)}, u32[]{:S(2)}) %collective-permute-start.8) | collective-permute-done | bytes 73760 | tf_op jit(solution)/shard_map/ppermute | solution.py:394
  51.3 1.6 %collective-permute-start.9 = (f32[72,256]{1,0:T(8,128)S(1)}, f32[72,256]{1,0:T(8,128)S(1)}, u32[]{:S(2)}, u32[]{:S(2)}) collective-permute-start(f32[72,256]{1,0:T(8,128)S(1)} %fusion.1), channel_id=1, source_target_pairs={{0,2},{1,3},{2,0},{3,1},{4,6},{5,7},{6,4},{7,5},{8,10},{9,11},{10,... | collective-permute-start | bytes 221192 | tf_op jit(solution)/shard_map/ppermute | solution.py:394
  53.0 2.8 %collective-permute-done.9 = f32[72,256]{1,0:T(8,128)S(1)} collective-permute-done((f32[72,256]{1,0:T(8,128)S(1)}, f32[72,256]{1,0:T(8,128)S(1)}, u32[]{:S(2)}, u32[]{:S(2)}) %collective-permute-start.9) | collective-permute-done | bytes 73760 | tf_op jit(solution)/shard_map/ppermute | solution.py:394
  55.8 2.7 %collective-permute-start.11 = (f32[72,256]{1,0:T(8,128)S(1)}, f32[72,256]{1,0:T(8,128)S(1)}, u32[]{:S(2)}, u32[]{:S(2)}) collective-permute-start(f32[72,256]{1,0:T(8,128)S(1)} %add.39), channel_id=1, source_target_pairs={{0,4},{1,5},{2,6},{3,7},{4,0},{5,1},{6,2},{7,3},{8,12},{9,13},{10,... | collective-permute-start | bytes 221192 | tf_op jit(solution)/shard_map/ppermute | solution.py:394
  59.1 2.0 %collective-permute-done.11 = f32[72,256]{1,0:T(8,128)S(1)} collective-permute-done((f32[72,256]{1,0:T(8,128)S(1)}, f32[72,256]{1,0:T(8,128)S(1)}, u32[]{:S(2)}, u32[]{:S(2)}) %collective-permute-start.11) | collective-permute-done | bytes 73760 | tf_op jit(solution)/shard_map/ppermute | solution.py:394
  61.1 2.2 %collective-permute-start.13 = (f32[72,256]{1,0:T(8,128)S(1)}, f32[72,256]{1,0:T(8,128)S(1)}, u32[]{:S(2)}, u32[]{:S(2)}) collective-permute-start(f32[72,256]{1,0:T(8,128)S(1)} %add.40), channel_id=1, source_target_pairs={{0,8},{8,0},{16,24},{24,16},{1,9},{9,1},{17,25},{25,17},{2,10},{10... | collective-permute-start | bytes 221192 | tf_op jit(solution)/shard_map/ppermute | solution.py:394
  63.3 0.9 %collective-permute-start.14 = (f32[72,256]{1,0:T(8,128)S(1)}, f32[72,256]{1,0:T(8,128)S(1)}, u32[]{:S(2)}, u32[]{:S(2)}) collective-permute-start(f32[72,256]{1,0:T(8,128)S(1)} %add.40), channel_id=1, source_target_pairs={{0,16},{8,24},{16,0},{24,8},{1,17},{9,25},{17,1},{25,9},{2,18},{10... | collective-permute-start | bytes 221192 | tf_op jit(solution)/shard_map/ppermute | solution.py:394
  64.9 2.0 %fields.1 = (f32[3,32,512]{2,1,0:T(8,128)}, f32[3,32,512]{2,1,0:T(8,128)}) custom-call(f32[2,4]{1,0:T(2,128)} %table.1, s32[32,512]{1,0:T(8,128)} %bitcast.35, f32[3,32,512]{2,1,0:T(8,128)} %bitcast.32, f32[9,16,512]{2,1,0:T(8,128)S(1)} %get-tuple-element.78.stress_near, f32[6,16,512]{2,1,0:T(8,128)S(1)} %get-tuple-element.82.stress_far, ...), custom_call_target="tpu_custom_call" | custom-call | tf_op jit(solution)/shard_map/fields/pallas_call | solution.py:546
  66.8 1.0 %collective-permute-done.14 = f32[72,256]{1,0:T(8,128)S(1)} collective-permute-done((f32[72,256]{1,0:T(8,128)S(1)}, f32[72,256]{1,0:T(8,128)S(1)}, u32[]{:S(2)}, u32[]{:S(2)}) %collective-permute-start.14) | collective-permute-done | bytes 73760 | tf_op jit(solution)/shard_map/ppermute | solution.py:394
  67.9 1.9 %collective-permute-done.15 = f32[72,256]{1,0:T(8,128)S(1)} collective-permute-done((f32[72,256]{1,0:T(8,128)S(1)}, f32[72,256]{1,0:T(8,128)S(1)}, u32[]{:S(2)}, u32[]{:S(2)}) %collective-permute-start.15) | collective-permute-done | bytes 73760 | tf_op jit(solution)/shard_map/ppermute | solution.py:394
  70.2 1.2 %collective-permute-done.16.other = f32[4,72,256]{2,1,0:T(8,128)S(1)} collective-permute-done((f32[4,72,256]{2,1,0:T(8,128)S(1)}, f32[4,72,256]{2,1,0:T(8,128)S(1)}, u32[]{:S(2)}, u32[]{:S(2)}) %collective-permute-start.16) | collective-permute-done | bytes 294944 | tf_op jit(solution)/shard_map/ppermute | solution.py:394
  71.4 1.1 %finish.1 = (f32[10,256]{1,0:T(8,128)}, f32[1,256]{1,0:T(1,128)}, f32[512,256]{1,0:T(8,128)}, f32[2,256]{1,0:T(2,128)}, f32[9,256]{1,0:T(8,128)}, /*index=5*/f32[1,9]{1,0:T(1,128)}) custom-call(f32[4,72,256]{2,1,0:T(8,128)S(1)} %pad_maximum_fusion.mine, f32[4,72,256]{2,1,0:T(8,128)S(1)} %collective-permute-done.16.other), custom_call_target="tpu_custom_call" | custom-call | tf_op jit(solution)/shard_map/finish/pallas_call | solution.py:571
  (23 shorter events, 4.9 us)
Async XLA Ops:
  2.0 7.9 %collective-permute-start.3 = (f32[6,16,512]{2,1,0:T(8,128)S(1)}, f32[6,16,512]{2,1,0:T(8,128)S(1)}, u32[]{:S(2)}, u32[]{:S(2)}) collective-permute-start(f32[6,16,512]{2,1,0:T(8,128)S(1)} %get-tuple-element.68), channel_id=1, source_target_pairs={{0,8},{8,0},{16,24},{24,16},{1,9},{9,1},{17,25},{25,17},{2,10},{10... | collective-permute-start | bytes 589832 | tf_op jit(solution)/shard_map/ppermute | solution.py:394
  5.0 3.4 %collective-permute-start.1 = (f32[9,2,512]{2,1,0:T(2,128)S(1)}, f32[9,2,512]{2,1,0:T(2,128)S(1)}, u32[]{:S(2)}, u32[]{:S(2)}) collective-permute-start(f32[9,2,512]{2,1,0:T(2,128)S(1)} %get-tuple-element.56), channel_id=1, source_target_pairs={{0,1},{1,0},{2,3},{3,2},{4,5},{5,4},{6,7},{7,6},{8,9},{9,8},{10,11... | collective-permute-start | bytes 110600 | tf_op jit(solution)/shard_map/ppermute | solution.py:394
  5.0 3.4 %collective-permute-start.2 = (f32[9,2,512]{2,1,0:T(2,128)S(1)}, f32[9,2,512]{2,1,0:T(2,128)S(1)}, u32[]{:S(2)}, u32[]{:S(2)}) collective-permute-start(f32[9,2,512]{2,1,0:T(2,128)S(1)} %get-tuple-element.57), channel_id=1, source_target_pairs={{1,2},{2,1},{3,4},{4,3},{5,6},{6,5},{9,10},{10,9},{11,12},{12,11},... | collective-permute-start | bytes 110600 | tf_op jit(solution)/shard_map/ppermute | solution.py:388
  5.7 21.1 %collective-permute-start = (f32[9,16,512]{2,1,0:T(8,128)S(1)}, f32[9,16,512]{2,1,0:T(8,128)S(1)}, u32[]{:S(2)}, u32[]{:S(2)}) collective-permute-start(f32[9,16,512]{2,1,0:T(8,128)S(1)} %get-tuple-element.55), channel_id=1, source_target_pairs={{8,16},{16,8},{9,17},{17,9},{10,18},{18,10},{11,19},{19,11},{12,20... | collective-permute-start | bytes 884744 | tf_op jit(solution)/shard_map/ppermute | solution.py:388
  24.0 17.1 %collective-permute-start.4 = (f32[9,16,512]{2,1,0:T(8,128)S(1)}, f32[9,16,512]{2,1,0:T(8,128)S(1)}, u32[]{:S(2)}, u32[]{:S(2)}) collective-permute-start(f32[9,16,512]{2,1,0:T(8,128)S(1)} %get-tuple-element.78.stress_near), channel_id=1, source_target_pairs={{0,8},{8,0},{16,24},{24,16},{1,9},{9,1},{17,25},{25,17},{2,10},{10... | collective-permute-start | bytes 884744 | tf_op jit(solution)/shard_map/ppermute | solution.py:394
  41.2 3.7 %collective-permute-start.5 = (f32[312,256]{1,0:T(8,128)S(1)}, f32[312,256]{1,0:T(8,128)S(1)}, u32[]{:S(2)}, u32[]{:S(2)}) collective-permute-start(f32[312,256]{1,0:T(8,128)S(1)} %get-tuple-element.79), channel_id=1, source_target_pairs={{0,1},{1,0},{2,3},{3,2},{4,5},{5,4},{6,7},{7,6},{8,9},{9,8},{10,11... | collective-permute-start | bytes 958472 | tf_op jit(solution)/shard_map/ppermute | solution.py:394
  45.0 5.0 %collective-permute-start.6 = (f32[72,256]{1,0:T(8,128)S(1)}, f32[72,256]{1,0:T(8,128)S(1)}, u32[]{:S(2)}, u32[]{:S(2)}) collective-permute-start(f32[72,256]{1,0:T(8,128)S(1)} %get-tuple-element.102), channel_id=1, source_target_pairs={{0,8},{8,0},{16,24},{24,16},{1,9},{9,1},{17,25},{25,17},{2,10},{10... | collective-permute-start | bytes 221192 | tf_op jit(solution)/shard_map/ppermute | solution.py:394
  45.3 5.1 %collective-permute-start.7 = (f32[72,256]{1,0:T(8,128)S(1)}, f32[72,256]{1,0:T(8,128)S(1)}, u32[]{:S(2)}, u32[]{:S(2)}) collective-permute-start(f32[72,256]{1,0:T(8,128)S(1)} %get-tuple-element.104), channel_id=1, source_target_pairs={{0,16},{8,24},{16,0},{24,8},{1,17},{9,25},{17,1},{25,9},{2,18},{10... | collective-permute-start | bytes 221192 | tf_op jit(solution)/shard_map/ppermute | solution.py:394
  46.1 5.3 %collective-permute-start.8 = (f32[72,256]{1,0:T(8,128)S(1)}, f32[72,256]{1,0:T(8,128)S(1)}, u32[]{:S(2)}, u32[]{:S(2)}) collective-permute-start(f32[72,256]{1,0:T(8,128)S(1)} %get-tuple-element.103), channel_id=1, source_target_pairs={{0,24},{8,16},{16,8},{24,0},{1,25},{9,17},{17,9},{25,1},{2,26},{10... | collective-permute-start | bytes 221192 | tf_op jit(solution)/shard_map/ppermute | solution.py:394
  48.5 7.3 %collective-permute-start.10 = (f32[6,16,512]{2,1,0:T(8,128)S(1)}, f32[6,16,512]{2,1,0:T(8,128)S(1)}, u32[]{:S(2)}, u32[]{:S(2)}) collective-permute-start(f32[6,16,512]{2,1,0:T(8,128)S(1)} %get-tuple-element.82.stress_far), channel_id=1, source_target_pairs={{8,16},{16,8},{9,17},{17,9},{10,18},{18,10},{11,19},{19,11},{12,20... | collective-permute-start | bytes 589832 | tf_op jit(solution)/shard_map/ppermute | solution.py:388
  51.3 4.4 %collective-permute-start.9 = (f32[72,256]{1,0:T(8,128)S(1)}, f32[72,256]{1,0:T(8,128)S(1)}, u32[]{:S(2)}, u32[]{:S(2)}) collective-permute-start(f32[72,256]{1,0:T(8,128)S(1)} %fusion.1), channel_id=1, source_target_pairs={{0,2},{1,3},{2,0},{3,1},{4,6},{5,7},{6,4},{7,5},{8,10},{9,11},{10,... | collective-permute-start | bytes 221192 | tf_op jit(solution)/shard_map/ppermute | solution.py:394
  55.8 5.3 %collective-permute-start.11 = (f32[72,256]{1,0:T(8,128)S(1)}, f32[72,256]{1,0:T(8,128)S(1)}, u32[]{:S(2)}, u32[]{:S(2)}) collective-permute-start(f32[72,256]{1,0:T(8,128)S(1)} %add.39), channel_id=1, source_target_pairs={{0,4},{1,5},{2,6},{3,7},{4,0},{5,1},{6,2},{7,3},{8,12},{9,13},{10,... | collective-permute-start | bytes 221192 | tf_op jit(solution)/shard_map/ppermute | solution.py:394
  58.4 2.7 %collective-permute-start.12 = (f32[24,256]{1,0:T(8,128)S(1)}, f32[24,256]{1,0:T(8,128)S(1)}, u32[]{:S(2)}, u32[]{:S(2)}) collective-permute-start(f32[24,256]{1,0:T(8,128)S(1)} %get-tuple-element.84), channel_id=1, source_target_pairs={{1,2},{2,1},{3,4},{4,3},{5,6},{6,5},{9,10},{10,9},{11,12},{12,11},... | collective-permute-start | bytes 73736 | tf_op jit(solution)/shard_map/ppermute | solution.py:388
  61.1 5.7 %collective-permute-start.13 = (f32[72,256]{1,0:T(8,128)S(1)}, f32[72,256]{1,0:T(8,128)S(1)}, u32[]{:S(2)}, u32[]{:S(2)}) collective-permute-start(f32[72,256]{1,0:T(8,128)S(1)} %add.40), channel_id=1, source_target_pairs={{0,8},{8,0},{16,24},{24,16},{1,9},{9,1},{17,25},{25,17},{2,10},{10... | collective-permute-start | bytes 221192 | tf_op jit(solution)/shard_map/ppermute | solution.py:394
  63.3 4.5 %collective-permute-start.14 = (f32[72,256]{1,0:T(8,128)S(1)}, f32[72,256]{1,0:T(8,128)S(1)}, u32[]{:S(2)}, u32[]{:S(2)}) collective-permute-start(f32[72,256]{1,0:T(8,128)S(1)} %add.40), channel_id=1, source_target_pairs={{0,16},{8,24},{16,0},{24,8},{1,17},{9,25},{17,1},{25,9},{2,18},{10... | collective-permute-start | bytes 221192 | tf_op jit(solution)/shard_map/ppermute | solution.py:394
  64.2 5.5 %collective-permute-start.15 = (f32[72,256]{1,0:T(8,128)S(1)}, f32[72,256]{1,0:T(8,128)S(1)}, u32[]{:S(2)}, u32[]{:S(2)}) collective-permute-start(f32[72,256]{1,0:T(8,128)S(1)} %add.40), channel_id=1, source_target_pairs={{0,24},{8,16},{16,8},{24,0},{1,25},{9,17},{17,9},{25,1},{2,26},{10... | collective-permute-start | bytes 221192 | tf_op jit(solution)/shard_map/ppermute | solution.py:394
  69.7 1.6 %collective-permute-start.16 = (f32[4,72,256]{2,1,0:T(8,128)S(1)}, f32[4,72,256]{2,1,0:T(8,128)S(1)}, u32[]{:S(2)}, u32[]{:S(2)}) collective-permute-start(f32[4,72,256]{2,1,0:T(8,128)S(1)} %pad_maximum_fusion.mine), channel_id=1, source_target_pairs={{0,1},{1,0},{2,3},{3,2},{4,5},{5,4},{6,7},{7,6},{8,9},{9,8},{10,11... | collective-permute-start | bytes 884744 | tf_op jit(solution)/shard_map/ppermute | solution.py:394

commit v8 on v7

--- a/solution.py
+++ b/solution.py
@@ -241,7 +241,7 @@
         back[:, at] = mul(winT[...], d1)
         return carry
 
-    lax.fori_loop(0, voxels // block, step, 0, unroll=2)
+    lax.fori_loop(0, voxels // block, step, 0, unroll=4)
 
     for r in range(rows):
         for t in range(tiles):

time: 73.5 us -> 71.7 us (0.976)
  Pallas kernels: 34.2 us -> 32.4 us
    pallas_call x2, Pallas kernels: 28.4 us -> 26.7 us  [network(): pl.pallas_call(functools.partial(network_kernel, order, rows, block), out...]
  transfers between devices with their start and end apart: 17 -> 17, of which waited for: 10 -> 10; matrix products, arithmetic and copies ran while one was open for 0% -> 0% of each run, Pallas kernels for 44% -> 42%
where the time goes in v8:
time: 71.7 us; the launch traced here: 70.6 us
  Pallas kernels  32.4 us (45%)
  starting transfers between devices  22.9 us (32%)
  waiting for transfers between devices  13.8 us (19%)
  between operations  1.4 us (2%)
    pallas_call x2, Pallas kernels, network(): pl.pallas_call(functools.partial(network_kernel, order, rows, block), out...  26.7 us
    ppermute x13, starting transfers between devices, swap(): lax.ppermute(value, axis, [(i, i ^ mask) for i in range(lax.axis_size(axi...  20.2 us
    ppermute x13, waiting for transfers between devices, swap(): lax.ppermute(value, axis, [(i, i ^ mask) for i in range(lax.axis_size(axi...  13.8 us
    ppermute x4, starting transfers between devices, swap_next(): lax.ppermute(value, axis, [(i, i + 1 if i % 2 else i - 1) for i in range(...  2.64 us
    pallas_call x1, Pallas kernels, body(): pl.pallas_call(functools.partial(fields_kernel, rows), out_shape=shapes(*...  1.96 us
  transfers between devices with their start and end apart: 17, of which 10 were waited for; matrix products, arithmetic and copies ran while one was open for 0% of the time, Pallas kernels for 42%

profile of v8, /device:TPU:0, one launch (start us, length us, event | category | flops | bytes accessed | tf_op | source)
XLA Modules:
  0.0 70.6 jit_solution(6599193219752688943)
XLA Ops:
  0.6 1.4 %faces.1 = (f32[6,16,512]{2,1,0:T(8,128)S(1)}, f32[9,16,512]{2,1,0:T(8,128)S(1)}, f32[9,2,512]{2,1,0:T(2,128)S(1)}, f32[9,2,512]{2,1,0:T(2,128)S(1)}, f32[2,8,16...) custom-call(f32[2,4]{1,0:T(2,128)} %table.1, s32[32,512]{1,0:T(8,128)} %bitcast.34, s32[32,512]{1,0:T(8,128)} %bitcast.41, ...), custom_call_target="tpu_custom_call" | custom-call | tf_op jit(solution)/shard_map/faces/pallas_call | solution.py:426
  2.0 3.0 %collective-permute-start.3 = (f32[6,16,512]{2,1,0:T(8,128)S(1)}, f32[6,16,512]{2,1,0:T(8,128)S(1)}, u32[]{:S(2)}, u32[]{:S(2)}) collective-permute-start(f32[6,16,512]{2,1,0:T(8,128)S(1)} %get-tuple-element.68), channel_id=1, source_target_pairs={{0,8},{8,0},{16,24},{24,16},{1,9},{9,1},{17,25},{25,17},{2,10},{10... | collective-permute-start | bytes 589832 | tf_op jit(solution)/shard_map/ppermute | solution.py:394
  7.0 1.4 %weights.1 = (bf16[256,16]{1,0:T(8,128)(2,1)S(1)}, bf16[16,256]{1,0:T(8,128)(2,1)S(1)}, bf16[2,256,256]{2,1,0:T(8,128)(2,1)S(1)}, bf16[16,256]{1,0:T(8,128)(2,1)...) custom-call(f32[9]{0:T(128)} %refs_0_.5, ...), custom_call_target="tpu_custom_call" | custom-call | tf_op jit(solution)/shard_map/weights/pallas_call | solution.py:472
  8.4 1.5 %collective-permute-done.3.refs_1_ = f32[6,16,512]{2,1,0:T(8,128)S(1)} collective-permute-done((f32[6,16,512]{2,1,0:T(8,128)S(1)}, f32[6,16,512]{2,1,0:T(8,128)S(1)}, u32[]{:S(2)}, u32[]{:S(2)}) %collective-permute-start.3) | collective-permute-done | bytes 196640 | tf_op jit(solution)/shard_map/ppermute | solution.py:394
  9.9 13.2 %network.2 = (f32[9,16,512]{2,1,0:T(8,128)S(1)}, f32[6,1,512]{2,1,0:T(1,128)S(1)}, f32[6,1,512]{2,1,0:T(1,128)S(1)}, f32[6,16,512]{2,1,0:T(8,128)S(1)}, f32[512,...) custom-call(f32[1]{0:T(128)S(6)} %copy.21.refs_0_, ...), custom_call_target="tpu_custom_call" | custom-call | flops 6681526272 | bytes 524288 | tf_op jit(solution)/shard_map/network/pallas_call | solution.py:496
  23.2 2.7 %collective-permute-start.4 = (f32[9,16,512]{2,1,0:T(8,128)S(1)}, f32[9,16,512]{2,1,0:T(8,128)S(1)}, u32[]{:S(2)}, u32[]{:S(2)}) collective-permute-start(f32[9,16,512]{2,1,0:T(8,128)S(1)} %get-tuple-element.78.stress_near), channel_id=1, source_target_pairs={{0,8},{8,0},{16,24},{24,16},{1,9},{9,1},{17,25},{25,17},{2,10},{10... | collective-permute-start | bytes 884744 | tf_op jit(solution)/shard_map/ppermute | solution.py:394
  25.9 13.4 %network.3 = (f32[6,16,512]{2,1,0:T(8,128)S(1)}, f32[24,256]{1,0:T(8,128)S(1)}, f32[6,16,512]{2,1,0:T(8,128)S(1)}, f32[4,72,256]{2,1,0:T(8,128)S(1)}, f32[312,256]{1,0:T(8,128)S(1)}) custom-call(f32[1]{0:T(128)S(6)} %copy.21.refs_0_, f32[9,16,512]{2,1,0:T(8,128)S(1)} %collective-permute-done.refs_1_.x_next, ...), custom_call_target="tpu_custom_call" | custom-call | flops 6681526272 | bytes 524288 | tf_op jit(solution)/shard_map/network/pallas_call | solution.py:496
  39.4 2.4 %collective-permute-start.5 = (f32[312,256]{1,0:T(8,128)S(1)}, f32[312,256]{1,0:T(8,128)S(1)}, u32[]{:S(2)}, u32[]{:S(2)}) collective-permute-start(f32[312,256]{1,0:T(8,128)S(1)} %get-tuple-element.79), channel_id=1, source_target_pairs={{0,1},{1,0},{2,3},{3,2},{4,5},{5,4},{6,7},{7,6},{8,9},{9,8},{10,11... | collective-permute-start | bytes 958472 | tf_op jit(solution)/shard_map/ppermute | solution.py:394
  41.8 1.2 %collective-permute-done.5.sy_pair = f32[312,256]{1,0:T(8,128)S(1)} collective-permute-done((f32[312,256]{1,0:T(8,128)S(1)}, f32[312,256]{1,0:T(8,128)S(1)}, u32[]{:S(2)}, u32[]{:S(2)}) %collective-permute-start.5) | collective-permute-done | bytes 319520 | tf_op jit(solution)/shard_map/ppermute | solution.py:394
  43.5 0.8 %collective-permute-start.7 = (f32[72,256]{1,0:T(8,128)S(1)}, f32[72,256]{1,0:T(8,128)S(1)}, u32[]{:S(2)}, u32[]{:S(2)}) collective-permute-start(f32[72,256]{1,0:T(8,128)S(1)} %get-tuple-element.104), channel_id=1, source_target_pairs={{0,16},{8,24},{16,0},{24,8},{1,17},{9,25},{17,1},{25,9},{2,18},{10... | collective-permute-start | bytes 221192 | tf_op jit(solution)/shard_map/ppermute | solution.py:394
  44.3 2.4 %collective-permute-start.8 = (f32[72,256]{1,0:T(8,128)S(1)}, f32[72,256]{1,0:T(8,128)S(1)}, u32[]{:S(2)}, u32[]{:S(2)}) collective-permute-start(f32[72,256]{1,0:T(8,128)S(1)} %get-tuple-element.103), channel_id=1, source_target_pairs={{0,24},{8,16},{16,8},{24,0},{1,25},{9,17},{17,9},{25,1},{2,26},{10... | collective-permute-start | bytes 221192 | tf_op jit(solution)/shard_map/ppermute | solution.py:394
  47.4 0.7 %collective-permute-done.6 = f32[72,256]{1,0:T(8,128)S(1)} collective-permute-done((f32[72,256]{1,0:T(8,128)S(1)}, f32[72,256]{1,0:T(8,128)S(1)}, u32[]{:S(2)}, u32[]{:S(2)}) %collective-permute-start.6) | collective-permute-done | bytes 73760 | tf_op jit(solution)/shard_map/ppermute | solution.py:394
  48.7 0.9 %collective-permute-done.8 = f32[72,256]{1,0:T(8,128)S(1)} collective-permute-done((f32[72,256]{1,0:T(8,128)S(1)}, f32[72,256]{1,0:T(8,128)S(1)}, u32[]{:S(2)}, u32[]{:S(2)}) %collective-permute-start.8) | collective-permute-done | bytes 73760 | tf_op jit(solution)/shard_map/ppermute | solution.py:394
  49.6 1.6 %collective-permute-start.9 = (f32[72,256]{1,0:T(8,128)S(1)}, f32[72,256]{1,0:T(8,128)S(1)}, u32[]{:S(2)}, u32[]{:S(2)}) collective-permute-start(f32[72,256]{1,0:T(8,128)S(1)} %fusion.1), channel_id=1, source_target_pairs={{0,2},{1,3},{2,0},{3,1},{4,6},{5,7},{6,4},{7,5},{8,10},{9,11},{10,... | collective-permute-start | bytes 221192 | tf_op jit(solution)/shard_map/ppermute | solution.py:394
  51.2 2.8 %collective-permute-done.9 = f32[72,256]{1,0:T(8,128)S(1)} collective-permute-done((f32[72,256]{1,0:T(8,128)S(1)}, f32[72,256]{1,0:T(8,128)S(1)}, u32[]{:S(2)}, u32[]{:S(2)}) %collective-permute-start.9) | collective-permute-done | bytes 73760 | tf_op jit(solution)/shard_map/ppermute | solution.py:394
  54.0 2.6 %collective-permute-start.11 = (f32[72,256]{1,0:T(8,128)S(1)}, f32[72,256]{1,0:T(8,128)S(1)}, u32[]{:S(2)}, u32[]{:S(2)}) collective-permute-start(f32[72,256]{1,0:T(8,128)S(1)} %add.39), channel_id=1, source_target_pairs={{0,4},{1,5},{2,6},{3,7},{4,0},{5,1},{6,2},{7,3},{8,12},{9,13},{10,... | collective-permute-start | bytes 221192 | tf_op jit(solution)/shard_map/ppermute | solution.py:394
  57.3 2.0 %collective-permute-done.11 = f32[72,256]{1,0:T(8,128)S(1)} collective-permute-done((f32[72,256]{1,0:T(8,128)S(1)}, f32[72,256]{1,0:T(8,128)S(1)}, u32[]{:S(2)}, u32[]{:S(2)}) %collective-permute-start.11) | collective-permute-done | bytes 73760 | tf_op jit(solution)/shard_map/ppermute | solution.py:394
  59.3 2.2 %collective-permute-start.13 = (f32[72,256]{1,0:T(8,128)S(1)}, f32[72,256]{1,0:T(8,128)S(1)}, u32[]{:S(2)}, u32[]{:S(2)}) collective-permute-start(f32[72,256]{1,0:T(8,128)S(1)} %add.40), channel_id=1, source_target_pairs={{0,8},{8,0},{16,24},{24,16},{1,9},{9,1},{17,25},{25,17},{2,10},{10... | collective-permute-start | bytes 221192 | tf_op jit(solution)/shard_map/ppermute | solution.py:394
  61.5 0.9 %collective-permute-start.14 = (f32[72,256]{1,0:T(8,128)S(1)}, f32[72,256]{1,0:T(8,128)S(1)}, u32[]{:S(2)}, u32[]{:S(2)}) collective-permute-start(f32[72,256]{1,0:T(8,128)S(1)} %add.40), channel_id=1, source_target_pairs={{0,16},{8,24},{16,0},{24,8},{1,17},{9,25},{17,1},{25,9},{2,18},{10... | collective-permute-start | bytes 221192 | tf_op jit(solution)/shard_map/ppermute | solution.py:394
  63.1 2.0 %fields.1 = (f32[3,32,512]{2,1,0:T(8,128)}, f32[3,32,512]{2,1,0:T(8,128)}) custom-call(f32[2,4]{1,0:T(2,128)} %table.1, s32[32,512]{1,0:T(8,128)} %bitcast.35, f32[3,32,512]{2,1,0:T(8,128)} %bitcast.32, f32[9,16,512]{2,1,0:T(8,128)S(1)} %get-tuple-element.78.stress_near, f32[6,16,512]{2,1,0:T(8,128)S(1)} %get-tuple-element.82.stress_far, ...), custom_call_target="tpu_custom_call" | custom-call | tf_op jit(solution)/shard_map/fields/pallas_call | solution.py:546
  65.0 1.0 %collective-permute-done.14 = f32[72,256]{1,0:T(8,128)S(1)} collective-permute-done((f32[72,256]{1,0:T(8,128)S(1)}, f32[72,256]{1,0:T(8,128)S(1)}, u32[]{:S(2)}, u32[]{:S(2)}) %collective-permute-start.14) | collective-permute-done | bytes 73760 | tf_op jit(solution)/shard_map/ppermute | solution.py:394
  66.1 1.9 %collective-permute-done.15 = f32[72,256]{1,0:T(8,128)S(1)} collective-permute-done((f32[72,256]{1,0:T(8,128)S(1)}, f32[72,256]{1,0:T(8,128)S(1)}, u32[]{:S(2)}, u32[]{:S(2)}) %collective-permute-start.15) | collective-permute-done | bytes 73760 | tf_op jit(solution)/shard_map/ppermute | solution.py:394
  68.4 1.2 %collective-permute-done.16.other = f32[4,72,256]{2,1,0:T(8,128)S(1)} collective-permute-done((f32[4,72,256]{2,1,0:T(8,128)S(1)}, f32[4,72,256]{2,1,0:T(8,128)S(1)}, u32[]{:S(2)}, u32[]{:S(2)}) %collective-permute-start.16) | collective-permute-done | bytes 294944 | tf_op jit(solution)/shard_map/ppermute | solution.py:394
  69.6 1.1 %finish.1 = (f32[10,256]{1,0:T(8,128)}, f32[1,256]{1,0:T(1,128)}, f32[512,256]{1,0:T(8,128)}, f32[2,256]{1,0:T(2,128)}, f32[9,256]{1,0:T(8,128)}, /*index=5*/f32[1,9]{1,0:T(1,128)}) custom-call(f32[4,72,256]{2,1,0:T(8,128)S(1)} %pad_maximum_fusion.mine, f32[4,72,256]{2,1,0:T(8,128)S(1)} %collective-permute-done.16.other), custom_call_target="tpu_custom_call" | custom-call | tf_op jit(solution)/shard_map/finish/pallas_call | solution.py:571
  (23 shorter events, 4.8 us)
Async XLA Ops:
  2.0 7.9 %collective-permute-start.3 = (f32[6,16,512]{2,1,0:T(8,128)S(1)}, f32[6,16,512]{2,1,0:T(8,128)S(1)}, u32[]{:S(2)}, u32[]{:S(2)}) collective-permute-start(f32[6,16,512]{2,1,0:T(8,128)S(1)} %get-tuple-element.68), channel_id=1, source_target_pairs={{0,8},{8,0},{16,24},{24,16},{1,9},{9,1},{17,25},{25,17},{2,10},{10... | collective-permute-start | bytes 589832 | tf_op jit(solution)/shard_map/ppermute | solution.py:394
  5.0 3.4 %collective-permute-start.1 = (f32[9,2,512]{2,1,0:T(2,128)S(1)}, f32[9,2,512]{2,1,0:T(2,128)S(1)}, u32[]{:S(2)}, u32[]{:S(2)}) collective-permute-start(f32[9,2,512]{2,1,0:T(2,128)S(1)} %get-tuple-element.56), channel_id=1, source_target_pairs={{0,1},{1,0},{2,3},{3,2},{4,5},{5,4},{6,7},{7,6},{8,9},{9,8},{10,11... | collective-permute-start | bytes 110600 | tf_op jit(solution)/shard_map/ppermute | solution.py:394
  5.0 3.4 %collective-permute-start.2 = (f32[9,2,512]{2,1,0:T(2,128)S(1)}, f32[9,2,512]{2,1,0:T(2,128)S(1)}, u32[]{:S(2)}, u32[]{:S(2)}) collective-permute-start(f32[9,2,512]{2,1,0:T(2,128)S(1)} %get-tuple-element.57), channel_id=1, source_target_pairs={{1,2},{2,1},{3,4},{4,3},{5,6},{6,5},{9,10},{10,9},{11,12},{12,11},... | collective-permute-start | bytes 110600 | tf_op jit(solution)/shard_map/ppermute | solution.py:388
  5.7 20.2 %collective-permute-start = (f32[9,16,512]{2,1,0:T(8,128)S(1)}, f32[9,16,512]{2,1,0:T(8,128)S(1)}, u32[]{:S(2)}, u32[]{:S(2)}) collective-permute-start(f32[9,16,512]{2,1,0:T(8,128)S(1)} %get-tuple-element.55), channel_id=1, source_target_pairs={{8,16},{16,8},{9,17},{17,9},{10,18},{18,10},{11,19},{19,11},{12,20... | collective-permute-start | bytes 884744 | tf_op jit(solution)/shard_map/ppermute | solution.py:388
  23.2 16.2 %collective-permute-start.4 = (f32[9,16,512]{2,1,0:T(8,128)S(1)}, f32[9,16,512]{2,1,0:T(8,128)S(1)}, u32[]{:S(2)}, u32[]{:S(2)}) collective-permute-start(f32[9,16,512]{2,1,0:T(8,128)S(1)} %get-tuple-element.78.stress_near), channel_id=1, source_target_pairs={{0,8},{8,0},{16,24},{24,16},{1,9},{9,1},{17,25},{25,17},{2,10},{10... | collective-permute-start | bytes 884744 | tf_op jit(solution)/shard_map/ppermute | solution.py:394
  39.4 3.7 %collective-permute-start.5 = (f32[312,256]{1,0:T(8,128)S(1)}, f32[312,256]{1,0:T(8,128)S(1)}, u32[]{:S(2)}, u32[]{:S(2)}) collective-permute-start(f32[312,256]{1,0:T(8,128)S(1)} %get-tuple-element.79), channel_id=1, source_target_pairs={{0,1},{1,0},{2,3},{3,2},{4,5},{5,4},{6,7},{7,6},{8,9},{9,8},{10,11... | collective-permute-start | bytes 958472 | tf_op jit(solution)/shard_map/ppermute | solution.py:394
  43.2 5.0 %collective-permute-start.6 = (f32[72,256]{1,0:T(8,128)S(1)}, f32[72,256]{1,0:T(8,128)S(1)}, u32[]{:S(2)}, u32[]{:S(2)}) collective-permute-start(f32[72,256]{1,0:T(8,128)S(1)} %get-tuple-element.102), channel_id=1, source_target_pairs={{0,8},{8,0},{16,24},{24,16},{1,9},{9,1},{17,25},{25,17},{2,10},{10... | collective-permute-start | bytes 221192 | tf_op jit(solution)/shard_map/ppermute | solution.py:394
  43.5 5.1 %collective-permute-start.7 = (f32[72,256]{1,0:T(8,128)S(1)}, f32[72,256]{1,0:T(8,128)S(1)}, u32[]{:S(2)}, u32[]{:S(2)}) collective-permute-start(f32[72,256]{1,0:T(8,128)S(1)} %get-tuple-element.104), channel_id=1, source_target_pairs={{0,16},{8,24},{16,0},{24,8},{1,17},{9,25},{17,1},{25,9},{2,18},{10... | collective-permute-start | bytes 221192 | tf_op jit(solution)/shard_map/ppermute | solution.py:394
  44.3 5.3 %collective-permute-start.8 = (f32[72,256]{1,0:T(8,128)S(1)}, f32[72,256]{1,0:T(8,128)S(1)}, u32[]{:S(2)}, u32[]{:S(2)}) collective-permute-start(f32[72,256]{1,0:T(8,128)S(1)} %get-tuple-element.103), channel_id=1, source_target_pairs={{0,24},{8,16},{16,8},{24,0},{1,25},{9,17},{17,9},{25,1},{2,26},{10... | collective-permute-start | bytes 221192 | tf_op jit(solution)/shard_map/ppermute | solution.py:394
  46.7 7.3 %collective-permute-start.10 = (f32[6,16,512]{2,1,0:T(8,128)S(1)}, f32[6,16,512]{2,1,0:T(8,128)S(1)}, u32[]{:S(2)}, u32[]{:S(2)}) collective-permute-start(f32[6,16,512]{2,1,0:T(8,128)S(1)} %get-tuple-element.82.stress_far), channel_id=1, source_target_pairs={{8,16},{16,8},{9,17},{17,9},{10,18},{18,10},{11,19},{19,11},{12,20... | collective-permute-start | bytes 589832 | tf_op jit(solution)/shard_map/ppermute | solution.py:388
  49.6 4.4 %collective-permute-start.9 = (f32[72,256]{1,0:T(8,128)S(1)}, f32[72,256]{1,0:T(8,128)S(1)}, u32[]{:S(2)}, u32[]{:S(2)}) collective-permute-start(f32[72,256]{1,0:T(8,128)S(1)} %fusion.1), channel_id=1, source_target_pairs={{0,2},{1,3},{2,0},{3,1},{4,6},{5,7},{6,4},{7,5},{8,10},{9,11},{10,... | collective-permute-start | bytes 221192 | tf_op jit(solution)/shard_map/ppermute | solution.py:394
  54.0 5.3 %collective-permute-start.11 = (f32[72,256]{1,0:T(8,128)S(1)}, f32[72,256]{1,0:T(8,128)S(1)}, u32[]{:S(2)}, u32[]{:S(2)}) collective-permute-start(f32[72,256]{1,0:T(8,128)S(1)} %add.39), channel_id=1, source_target_pairs={{0,4},{1,5},{2,6},{3,7},{4,0},{5,1},{6,2},{7,3},{8,12},{9,13},{10,... | collective-permute-start | bytes 221192 | tf_op jit(solution)/shard_map/ppermute | solution.py:394
  56.6 2.7 %collective-permute-start.12 = (f32[24,256]{1,0:T(8,128)S(1)}, f32[24,256]{1,0:T(8,128)S(1)}, u32[]{:S(2)}, u32[]{:S(2)}) collective-permute-start(f32[24,256]{1,0:T(8,128)S(1)} %get-tuple-element.84), channel_id=1, source_target_pairs={{1,2},{2,1},{3,4},{4,3},{5,6},{6,5},{9,10},{10,9},{11,12},{12,11},... | collective-permute-start | bytes 73736 | tf_op jit(solution)/shard_map/ppermute | solution.py:388
  59.3 5.7 %collective-permute-start.13 = (f32[72,256]{1,0:T(8,128)S(1)}, f32[72,256]{1,0:T(8,128)S(1)}, u32[]{:S(2)}, u32[]{:S(2)}) collective-permute-start(f32[72,256]{1,0:T(8,128)S(1)} %add.40), channel_id=1, source_target_pairs={{0,8},{8,0},{16,24},{24,16},{1,9},{9,1},{17,25},{25,17},{2,10},{10... | collective-permute-start | bytes 221192 | tf_op jit(solution)/shard_map/ppermute | solution.py:394
  61.5 4.5 %collective-permute-start.14 = (f32[72,256]{1,0:T(8,128)S(1)}, f32[72,256]{1,0:T(8,128)S(1)}, u32[]{:S(2)}, u32[]{:S(2)}) collective-permute-start(f32[72,256]{1,0:T(8,128)S(1)} %add.40), channel_id=1, source_target_pairs={{0,16},{8,24},{16,0},{24,8},{1,17},{9,25},{17,1},{25,9},{2,18},{10... | collective-permute-start | bytes 221192 | tf_op jit(solution)/shard_map/ppermute | solution.py:394
  62.4 5.5 %collective-permute-start.15 = (f32[72,256]{1,0:T(8,128)S(1)}, f32[72,256]{1,0:T(8,128)S(1)}, u32[]{:S(2)}, u32[]{:S(2)}) collective-permute-start(f32[72,256]{1,0:T(8,128)S(1)} %add.40), channel_id=1, source_target_pairs={{0,24},{8,16},{16,8},{24,0},{1,25},{9,17},{17,9},{25,1},{2,26},{10... | collective-permute-start | bytes 221192 | tf_op jit(solution)/shard_map/ppermute | solution.py:394
  67.9 1.6 %collective-permute-start.16 = (f32[4,72,256]{2,1,0:T(8,128)S(1)}, f32[4,72,256]{2,1,0:T(8,128)S(1)}, u32[]{:S(2)}, u32[]{:S(2)}) collective-permute-start(f32[4,72,256]{2,1,0:T(8,128)S(1)} %pad_maximum_fusion.mine), channel_id=1, source_target_pairs={{0,1},{1,0},{2,3},{3,2},{4,5},{5,4},{6,7},{7,6},{8,9},{9,8},{10,11... | collective-permute-start | bytes 884744 | tf_op jit(solution)/shard_map/ppermute | solution.py:394
